TPU v7x, 32 devices: a whole 2x2x4 slice. The times are simulated.
32 devices in a mesh: dp: 8 (over z, x), fsdp: 4 (over y, core).
Axes of the slice: x: 2, y: 2, z: 4, core: 2. Of those that a mesh axis runs over, the one named last changes fastest.
Arguments:
- frames: bfloat16 [32768, 512], P(('dp', 'fsdp')), may hold values from -6 to 6
- cotangent: bfloat16 [32768, 512], P(('dp', 'fsdp')), may hold values from -6 to 6
- lengths: int32 [32, 5], P(('dp', 'fsdp')), may hold values from 1 to 512, 1024 in all within a row
- expand: float32 [2, 512, 2048], P(None, 'fsdp'), may hold values from -0.25 to 0.25
- expand_first: float32 [2, 512, 2048], P(None, 'fsdp'), may hold values from -12 to 12
- expand_second: float32 [2, 512, 2048], P(None, 'fsdp'), may hold values from 6.5536 to 26.2144
- shrink: float32 [2, 2048, 512], P(None, 'fsdp'), may hold values from -0.125 to 0.125
- shrink_first: float32 [2, 2048, 512], P(None, 'fsdp'), may hold values from -32 to 32
- shrink_second: float32 [2, 2048, 512], P(None, 'fsdp'), may hold values from 40.96 to 163.84
- attend: float32 [512, 1536], P('fsdp'), may hold values from -0.25 to 0.25
- attend_first: float32 [512, 1536], P('fsdp'), may hold values from -12 to 12
- attend_second: float32 [512, 1536], P('fsdp'), may hold values from 6.5536 to 26.2144
- heads_out: float32 [512, 512], P('fsdp'), may hold values from -0.75 to 0.75
- heads_out_first: float32 [512, 512], P('fsdp'), may hold values from -24 to 24
- heads_out_second: float32 [512, 512], P('fsdp'), may hold values from 26.2144 to 104.8576
- pointwise: float32 [512, 1024], P('fsdp'), may hold values from -0.25 to 0.25
- pointwise_first: float32 [512, 1024], P('fsdp'), may hold values from -12 to 12
- pointwise_second: float32 [512, 1024], P('fsdp'), may hold values from 6.5536 to 26.2144
- pointwise_out: float32 [512, 512], P('fsdp'), may hold values from -0.375 to 0.375
- pointwise_out_first: float32 [512, 512], P('fsdp'), may hold values from -32 to 32
- pointwise_out_second: float32 [512, 512], P('fsdp'), may hold values from 58.9824 to 235.9296
- depthwise: float32 [32, 512], P(None, 'fsdp'), may hold values from -1 to 1
- depthwise_first: float32 [32, 512], P(None, 'fsdp'), may hold values from -32 to 32
- depthwise_second: float32 [32, 512], P(None, 'fsdp'), may hold values from 58.9824 to 235.9296
- norm_table: float32 [12, 512], P(None, 'fsdp'), may hold values from -0.8 to 1.6
- norm_table_first: float32 [12, 512], P(None, 'fsdp'), may hold values from -64 to 64
- norm_table_second: float32 [12, 512], P(None, 'fsdp'), may hold values from 163.84 to 655.36
Outputs:
- layer_output: bfloat16 [32768, 512], P(('dp', 'fsdp'))
- frames_grad: float32 [32768, 512], P(('dp', 'fsdp'))
- expand_updated: float32 [2, 512, 2048], P(None, 'fsdp')
- expand_first_updated: float32 [2, 512, 2048], P(None, 'fsdp')
- expand_second_updated: float32 [2, 512, 2048], P(None, 'fsdp')
- shrink_updated: float32 [2, 2048, 512], P(None, 'fsdp')
- shrink_first_updated: float32 [2, 2048, 512], P(None, 'fsdp')
- shrink_second_updated: float32 [2, 2048, 512], P(None, 'fsdp')
- attend_updated: float32 [512, 1536], P('fsdp')
- attend_first_updated: float32 [512, 1536], P('fsdp')
- attend_second_updated: float32 [512, 1536], P('fsdp')
- heads_out_updated: float32 [512, 512], P('fsdp')
- heads_out_first_updated: float32 [512, 512], P('fsdp')
- heads_out_second_updated: float32 [512, 512], P('fsdp')
- pointwise_updated: float32 [512, 1024], P('fsdp')
- pointwise_first_updated: float32 [512, 1024], P('fsdp')
- pointwise_second_updated: float32 [512, 1024], P('fsdp')
- pointwise_out_updated: float32 [512, 512], P('fsdp')
- pointwise_out_first_updated: float32 [512, 512], P('fsdp')
- pointwise_out_second_updated: float32 [512, 512], P('fsdp')
- depthwise_updated: float32 [32, 512], P(None, 'fsdp')
- depthwise_first_updated: float32 [32, 512], P(None, 'fsdp')
- depthwise_second_updated: float32 [32, 512], P(None, 'fsdp')
- norm_table_grad: float32 [12, 512], P(None, 'fsdp')
- norm_table_first_updated: float32 [12, 512], P(None, 'fsdp')
- norm_table_second_updated: float32 [12, 512], P(None, 'fsdp')
Inputs may be any that keep to these rules, and one draw needn't show every extreme that they name: Each row: four utterance lengths of one pack, then its padding frames; the row sums to 1024, its largest entry is exactly 512.
All inputs are finite; a program needn't handle non-finite values.
Results may differ from a plain program's by a relative error of at most 0.018.
Values may be sent and summed in bfloat16 or wider, within the bound.
No kernel may reach another device: no remote copies, remote signals or barrier semaphores. Data moves between devices by JAX's collectives and lax.ppermute only.
A program may use at most 320 MiB of HBM per device.

v0:
```python
import math

import jax
import jax.numpy as jnp
from jax import lax
from jax.sharding import PartitionSpec as P

HEADS = 8
STEP = 10


norm_epsilon = 1e-05
batch_epsilon = 1e-05
masked_score = -1000000000.0
learn_rate = 0.1
beta_first = 0.9
beta_second = 0.98
adam_epsilon = 1e-08
decay_rate = 0.01


def product(left, right):
    return jnp.dot(left, right, preferred_element_type=jnp.float32)


def times_transposed(left, right):
    return lax.dot_general(
        left, right, (((1,), (1,)), ((), ())), preferred_element_type=jnp.float32
    )


def transposed_times(left, right):
    return lax.dot_general(
        left, right, (((0,), (0,)), ((), ())), preferred_element_type=jnp.float32
    )


def layer_normalize(value, gain, bias):
    center = value - jnp.mean(value, axis=-1, keepdims=True)
    scale = lax.rsqrt(jnp.mean(center * center, axis=-1, keepdims=True) + norm_epsilon)
    normed = center * scale
    return (normed * gain + bias, normed, scale)


def norm_back(grad_out, gain, normed, scale):
    grad_norm = grad_out * gain
    grad_in = scale * (
        grad_norm
        - jnp.mean(grad_norm, axis=-1, keepdims=True)
        - normed * jnp.mean(grad_norm * normed, axis=-1, keepdims=True)
    )
    return (grad_in, jnp.sum(grad_out * normed, axis=0), jnp.sum(grad_out, axis=0))


def swish(value):
    return value * jax.nn.sigmoid(value)


def swish_slope(value):
    sigma = jax.nn.sigmoid(value)
    return sigma * (1.0 + value * (1.0 - sigma))


def layout(row, frames):
    bounds = jnp.cumsum(row[:4])
    places = jnp.arange(frames, dtype=jnp.int32)
    segment = jnp.sum((places[:, None] >= bounds[None, :]).astype(jnp.int32), axis=1)
    starts = jnp.concatenate([jnp.zeros((1,), jnp.int32), bounds])
    pick = (segment[:, None] == jnp.arange(5, dtype=jnp.int32)[None, :]).astype(jnp.int32)
    position = places - jnp.sum(pick * starts[None, :], axis=1)
    return (segment, position, segment < 4)


def rotary_tables(position, half):
    freq = jnp.exp(jnp.arange(half, dtype=jnp.float32) * (-math.log(10000.0) / half))
    angle = position.astype(jnp.float32)[:, None] * freq[None, :]
    return (jnp.cos(angle)[:, None, :], jnp.sin(angle)[:, None, :])


def rotate(value, cosine, sine):
    half = value.shape[-1] // 2
    first, second_block = (value[..., :half], value[..., half:])
    return jnp.concatenate(
        [first * cosine - second_block * sine, first * sine + second_block * cosine], axis=-1
    )


def unrotate(grad, cosine, sine):
    half = grad.shape[-1] // 2
    first, second_block = (grad[..., :half], grad[..., half:])
    return jnp.concatenate(
        [first * cosine + second_block * sine, second_block * cosine - first * sine], axis=-1
    )


def neighbour_masks(segment, size):
    left = size // 2
    frames = segment.shape[0]
    padded = jnp.pad(segment, (left, size - 1 - left), constant_values=-1)
    return [
        (padded[offset : offset + frames] == segment).astype(jnp.float32)[:, None]
        for offset in range(size)
    ]


def depth_forward(glu, kernel, masks):
    size = kernel.shape[0]
    left = size // 2
    frames = glu.shape[0]
    padded = jnp.pad(glu, ((left, size - 1 - left), (0, 0)))
    total = jnp.zeros_like(glu)
    for offset in range(size):
        total = total + kernel[offset] * padded[offset : offset + frames] * masks[offset]
    return (total, padded)


def depth_backward(grad, kernel, masks, padded):
    size = kernel.shape[0]
    left = size // 2
    frames = grad.shape[0]
    grad_wide = jnp.pad(grad, ((size - 1 - left, left), (0, 0)))
    grad_glu = jnp.zeros_like(grad)
    taps = []
    for offset in range(size):
        taps.append(jnp.sum(grad * masks[offset] * padded[offset : offset + frames], axis=0))
        mask_wide = jnp.pad(masks[offset], ((size - 1 - left, left), (0, 0)))
        begin = size - 1 - offset
        grad_glu = (
            grad_glu
            + kernel[offset] * grad_wide[begin : begin + frames] * mask_wide[begin : begin + frames]
        )
    return (grad_glu, jnp.stack(taps))


def feed_forward(value, w_in, w_out, gain, bias):
    normed_out, normed, scale = layer_normalize(value, gain, bias)
    hidden = normed_out.astype(jnp.bfloat16)
    before = product(hidden, w_in)
    active = swish(before).astype(jnp.bfloat16)
    return (value + 0.5 * product(active, w_out), (normed, scale, hidden, before, active))


def feed_back(grad, w_in, w_out, gain, saved):
    normed, scale, hidden, before, active = saved
    grad_out = (0.5 * grad).astype(jnp.bfloat16)
    grad_w_out = transposed_times(active, grad_out)
    grad_before = (times_transposed(grad_out, w_out) * swish_slope(before)).astype(jnp.bfloat16)
    grad_w_in = transposed_times(hidden, grad_before)
    grad_hidden = times_transposed(grad_before, w_in)
    grad_in, grad_gain, grad_bias = norm_back(grad_hidden, gain, normed, scale)
    return (grad + grad_in, grad_w_in, grad_w_out, grad_gain, grad_bias)


def masked_scores(query, keyset, same, score_scale):
    scores = (
        jnp.einsum("qhd,khd->hqk", query, keyset, preferred_element_type=jnp.float32) * score_scale
    )
    return jnp.where(same[None], scores, masked_score)


def adam_update(master, first, second_block, grad, decay):
    first_new = beta_first * first + (1.0 - beta_first) * grad
    second_new = beta_second * second_block + (1.0 - beta_second) * grad * grad
    first_hat = first_new / (1.0 - beta_first**STEP)
    second_hat = second_new / (1.0 - beta_second**STEP)
    master_new = master - learn_rate * (
        first_hat / (jnp.sqrt(second_hat) + adam_epsilon) + decay * master
    )
    return (master_new, first_new, second_new)


def moments_only(first, second_block, grad):
    first_new = beta_first * first + (1.0 - beta_first) * grad
    second_new = beta_second * second_block + (1.0 - beta_second) * grad * grad
    return (first_new, second_new)


def per_device(
    frames,
    cotangent,
    lengths,
    expand,
    expand_first,
    expand_second,
    shrink,
    shrink_first,
    shrink_second,
    attend,
    attend_first,
    attend_second,
    heads_out,
    heads_out_first,
    heads_out_second,
    pointwise,
    pointwise_first,
    pointwise_second,
    pointwise_out,
    pointwise_out_first,
    pointwise_out_second,
    depthwise,
    depthwise_first,
    depthwise_second,
    norm_table,
    norm_table_first,
    norm_table_second,
):
    masters = (expand, shrink, attend, heads_out, pointwise, pointwise_out, depthwise, norm_table)
    rounded_value = [master.astype(jnp.bfloat16) for master in masters]
    fetched = (
        lax.all_gather(rounded_value[0], "fsdp", axis=1, tiled=True),
        lax.all_gather(rounded_value[1], "fsdp", axis=1, tiled=True),
        lax.all_gather(rounded_value[2], "fsdp", axis=0, tiled=True),
        lax.all_gather(rounded_value[3], "fsdp", axis=0, tiled=True),
        lax.all_gather(rounded_value[4], "fsdp", axis=0, tiled=True),
        lax.all_gather(rounded_value[5], "fsdp", axis=0, tiled=True),
        lax.all_gather(rounded_value[6], "fsdp", axis=1, tiled=True),
        lax.all_gather(rounded_value[7], "fsdp", axis=1, tiled=True),
    )
    (
        full_expand,
        full_shrink,
        full_attend,
        full_heads,
        full_point,
        full_point_out,
        full_depth,
        full_norms,
    ) = fetched
    norm_entries = full_norms.astype(jnp.float32)
    kernel = full_depth.astype(jnp.float32)
    value = frames.astype(jnp.float32)
    frame_count, width = value.shape
    heads = HEADS
    head_dim = width // heads
    score_scale = head_dim ** (-0.5)
    segment, position, valid_frames = layout(lengths[0], frame_count)
    valid_col = valid_frames.astype(jnp.float32)[:, None]
    cosine, sine = rotary_tables(position, head_dim // 2)
    same = segment[:, None] == segment[None, :]
    masks = neighbour_masks(segment, kernel.shape[0])
    first, saved_one = feed_forward(
        value, full_expand[0], full_shrink[0], norm_entries[0], norm_entries[1]
    )
    attn_out, attn_normed, attn_scale = layer_normalize(first, norm_entries[2], norm_entries[3])
    attn_hidden = attn_out.astype(jnp.bfloat16)
    packed = product(attn_hidden, full_attend).reshape(frame_count, 3, heads, head_dim)
    query = rotate(packed[:, 0], cosine, sine).astype(jnp.bfloat16)
    keyset = rotate(packed[:, 1], cosine, sine).astype(jnp.bfloat16)
    values = packed[:, 2].astype(jnp.bfloat16)
    scores = masked_scores(query, keyset, same, score_scale)
    top = jnp.max(scores, axis=-1, keepdims=True)
    expo = jnp.exp(scores - top)
    total = jnp.sum(expo, axis=-1, keepdims=True)
    prob = expo / total
    log_total = top + jnp.log(total)
    mixed = jnp.einsum(
        "hqk,khd->qhd", prob.astype(jnp.bfloat16), values, preferred_element_type=jnp.float32
    )
    mixed = mixed.astype(jnp.bfloat16).reshape(frame_count, width)
    second_block = first + product(mixed, full_heads)
    conv_out, conv_normed, conv_scale = layer_normalize(
        second_block, norm_entries[4], norm_entries[5]
    )
    conv_hidden = conv_out.astype(jnp.bfloat16)
    gates = product(conv_hidden, full_point)
    half_value = gates[:, :width]
    sigma = jax.nn.sigmoid(gates[:, width:])
    glu = half_value * sigma
    convolution_module, padded_glu = depth_forward(glu, kernel, masks)
    stats = lax.psum(
        (
            jnp.sum(valid_col * convolution_module, axis=0),
            jnp.sum(valid_col * convolution_module * convolution_module, axis=0),
            jnp.sum(valid_col),
        ),
        ("dp", "fsdp"),
    )
    valid_count = stats[2]
    masked_mean = stats[0] / valid_count
    batch_norm_scale = lax.rsqrt(stats[1] / valid_count - masked_mean * masked_mean + batch_epsilon)
    zhat = (convolution_module - masked_mean) * batch_norm_scale
    zed = zhat * norm_entries[6] + norm_entries[7]
    conv_active = swish(zed).astype(jnp.bfloat16)
    third = second_block + product(conv_active, full_point_out)
    fourth_block, saved_two = feed_forward(
        third, full_expand[1], full_shrink[1], norm_entries[8], norm_entries[9]
    )
    last_out, last_normed, last_scale = layer_normalize(
        fourth_block, norm_entries[10], norm_entries[11]
    )
    layer_output = (last_out * valid_col).astype(jnp.bfloat16)
    refetched = (
        lax.all_gather(rounded_value[0], "fsdp", axis=1, tiled=True),
        lax.all_gather(rounded_value[1], "fsdp", axis=1, tiled=True),
        lax.all_gather(rounded_value[2], "fsdp", axis=0, tiled=True),
        lax.all_gather(rounded_value[3], "fsdp", axis=0, tiled=True),
        lax.all_gather(rounded_value[4], "fsdp", axis=0, tiled=True),
        lax.all_gather(rounded_value[5], "fsdp", axis=0, tiled=True),
        lax.all_gather(rounded_value[6], "fsdp", axis=1, tiled=True),
        lax.all_gather(rounded_value[7], "fsdp", axis=1, tiled=True),
    )
    (
        back_expand,
        back_shrink,
        back_attend,
        back_heads,
        back_point,
        back_point_out,
        back_depth,
        back_norms,
    ) = refetched
    norms_back = back_norms.astype(jnp.float32)
    kernel_back = back_depth.astype(jnp.float32)
    grad_y = cotangent.astype(jnp.float32) * valid_col
    grad_fourth, gain_last, bias_last = norm_back(grad_y, norms_back[10], last_normed, last_scale)
    grad_third, grad_in_two, grad_out_two, gain_four, bias_four = feed_back(
        grad_fourth, back_expand[1], back_shrink[1], norms_back[8], saved_two
    )
    grad_branch = grad_third.astype(jnp.bfloat16)
    grad_point_out = transposed_times(conv_active, grad_branch)
    grad_zed = times_transposed(grad_branch, back_point_out) * swish_slope(zed)
    local_bias = jnp.sum(grad_zed, axis=0)
    local_gain = jnp.sum(grad_zed * zhat, axis=0)
    totals = lax.psum((local_bias, local_gain), ("dp", "fsdp"))
    grad_conv = (
        batch_norm_scale
        * norms_back[6]
        * (grad_zed - valid_col * (totals[0] + zhat * totals[1]) / valid_count)
    )
    grad_glu, grad_kernel = depth_backward(grad_conv, kernel_back, masks, padded_glu)
    grad_gates = jnp.concatenate(
        [grad_glu * sigma, grad_glu * half_value * sigma * (1.0 - sigma)], axis=1
    ).astype(jnp.bfloat16)
    grad_point = transposed_times(conv_hidden, grad_gates)
    grad_conv_in, gain_conv, bias_conv = norm_back(
        times_transposed(grad_gates, back_point), norms_back[4], conv_normed, conv_scale
    )
    grad_second = grad_third + grad_conv_in
    grad_attn = grad_second.astype(jnp.bfloat16)
    grad_heads = transposed_times(mixed, grad_attn)
    grad_mixed = (
        times_transposed(grad_attn, back_heads)
        .astype(jnp.bfloat16)
        .reshape(frame_count, heads, head_dim)
    )
    scores = masked_scores(query, keyset, same, score_scale)
    prob = jnp.exp(scores - log_total)
    grad_values = jnp.einsum(
        "hqk,qhd->khd", prob.astype(jnp.bfloat16), grad_mixed, preferred_element_type=jnp.float32
    )
    grad_prob = jnp.einsum("qhd,khd->hqk", grad_mixed, values, preferred_element_type=jnp.float32)
    grad_scores = (prob * (grad_prob - jnp.sum(prob * grad_prob, axis=-1, keepdims=True))).astype(
        jnp.bfloat16
    )
    grad_query = (
        jnp.einsum("hqk,khd->qhd", grad_scores, keyset, preferred_element_type=jnp.float32)
        * score_scale
    )
    grad_key = (
        jnp.einsum("hqk,qhd->khd", grad_scores, query, preferred_element_type=jnp.float32)
        * score_scale
    )
    grad_packed = jnp.stack(
        [unrotate(grad_query, cosine, sine), unrotate(grad_key, cosine, sine), grad_values], axis=1
    )
    grad_packed = grad_packed.reshape(frame_count, 3 * width).astype(jnp.bfloat16)
    grad_attend = transposed_times(attn_hidden, grad_packed)
    grad_attn_in, gain_attn, bias_attn = norm_back(
        times_transposed(grad_packed, back_attend), norms_back[2], attn_normed, attn_scale
    )
    grad_first = grad_second + grad_attn_in
    frames_grad, grad_in_one, grad_out_one, gain_one, bias_one = feed_back(
        grad_first, back_expand[0], back_shrink[0], norms_back[0], saved_one
    )
    grad_expand = jnp.stack([grad_in_one, grad_in_two])
    grad_shrink = jnp.stack([grad_out_one, grad_out_two])
    grad_norms = jnp.stack(
        [
            gain_one,
            bias_one,
            gain_attn,
            bias_attn,
            gain_conv,
            bias_conv,
            local_gain,
            local_bias,
            gain_four,
            bias_four,
            gain_last,
            bias_last,
        ]
    )
    gradients = (
        grad_expand,
        grad_shrink,
        grad_attend,
        grad_heads,
        grad_point,
        grad_point_out,
        grad_kernel,
        grad_norms,
    )
    shards = (
        lax.psum_scatter(gradients[0], "fsdp", scatter_dimension=1, tiled=True),
        lax.psum_scatter(gradients[1], "fsdp", scatter_dimension=1, tiled=True),
        lax.psum_scatter(gradients[2], "fsdp", scatter_dimension=0, tiled=True),
        lax.psum_scatter(gradients[3], "fsdp", scatter_dimension=0, tiled=True),
        lax.psum_scatter(gradients[4], "fsdp", scatter_dimension=0, tiled=True),
        lax.psum_scatter(gradients[5], "fsdp", scatter_dimension=0, tiled=True),
        lax.psum_scatter(gradients[6], "fsdp", scatter_dimension=1, tiled=True),
        lax.psum_scatter(gradients[7], "fsdp", scatter_dimension=1, tiled=True),
    )
    reduced = lax.psum(
        (shards[0], shards[1], shards[2], shards[3], shards[4], shards[5], shards[6], shards[7]),
        "dp",
    )
    firsts = (
        expand_first,
        shrink_first,
        attend_first,
        heads_out_first,
        pointwise_first,
        pointwise_out_first,
        depthwise_first,
        norm_table_first,
    )
    seconds = (
        expand_second,
        shrink_second,
        attend_second,
        heads_out_second,
        pointwise_second,
        pointwise_out_second,
        depthwise_second,
        norm_table_second,
    )
    updates = []
    for index in range(7):
        updates.extend(
            adam_update(masters[index], firsts[index], seconds[index], reduced[index], decay_rate)
        )
    norm_first_new, norm_second_new = moments_only(firsts[7], seconds[7], reduced[7])
    updates.extend((reduced[7], norm_first_new, norm_second_new))
    return (
        layer_output,
        frames_grad,
        updates[0],
        updates[1],
        updates[2],
        updates[3],
        updates[4],
        updates[5],
        updates[6],
        updates[7],
        updates[8],
        updates[9],
        updates[10],
        updates[11],
        updates[12],
        updates[13],
        updates[14],
        updates[15],
        updates[16],
        updates[17],
        updates[18],
        updates[19],
        updates[20],
        updates[21],
        updates[22],
        updates[23],
    )


def solution(mesh):
    return jax.shard_map(
        per_device,
        mesh=mesh,
        in_specs=(
            P(("dp", "fsdp"), None),
            P(("dp", "fsdp"), None),
            P(("dp", "fsdp"), None),
            P(None, "fsdp", None),
            P(None, "fsdp", None),
            P(None, "fsdp", None),
            P(None, "fsdp", None),
            P(None, "fsdp", None),
            P(None, "fsdp", None),
            P("fsdp", None),
            P("fsdp", None),
            P("fsdp", None),
            P("fsdp", None),
            P("fsdp", None),
            P("fsdp", None),
            P("fsdp", None),
            P("fsdp", None),
            P("fsdp", None),
            P("fsdp", None),
            P("fsdp", None),
            P("fsdp", None),
            P(None, "fsdp"),
            P(None, "fsdp"),
            P(None, "fsdp"),
            P(None, "fsdp"),
            P(None, "fsdp"),
            P(None, "fsdp"),
        ),
        out_specs=(
            P(("dp", "fsdp"), None),
            P(("dp", "fsdp"), None),
            P(None, "fsdp", None),
            P(None, "fsdp", None),
            P(None, "fsdp", None),
            P(None, "fsdp", None),
            P(None, "fsdp", None),
            P(None, "fsdp", None),
            P("fsdp", None),
            P("fsdp", None),
            P("fsdp", None),
            P("fsdp", None),
            P("fsdp", None),
            P("fsdp", None),
            P("fsdp", None),
            P("fsdp", None),
            P("fsdp", None),
            P("fsdp", None),
            P("fsdp", None),
            P("fsdp", None),
            P(None, "fsdp"),
            P(None, "fsdp"),
            P(None, "fsdp"),
            P(None, "fsdp"),
            P(None, "fsdp"),
            P(None, "fsdp"),
        ),
        check_vma=False,
    )
```

profile of v0, /device:TPU:0, one launch (start us, length us, event | category | flops | bytes accessed | tf_op | source)
XLA Modules:
  0.0 937.5 jit_solution(10393054719977175712)
XLA Ops:
  13.7 6.1 all_gather.37
  24.8 5.5 all_gather.32
  51.7 7.9 all_gather.39
  59.6 11.2 %all_gather.36 = bf16[512,512]{1,0:T(8,128)(2,1)} all-gather(bf16[128,512]{1,0:T(8,128)(2,1)S(1)} %convert_element_type.276), channel_id=1, replica_groups=mesh['dp'=8,'fsdp'=4] {'fsdp'}, dimensions={0}, use_global_device_ids=true | all-gather | bytes 655360 | tf_op jit(solution)/shard_map/all_gather | solution.py:213
  74.0 8.4 multiply_convert_fusion.4
  82.3 4.7 all-gather.7.cloned.1.call-done
  87.1 5.3 fusion.243
  92.7 16.2 %all-gather.9.cloned.1.call-done = bf16[512,1536]{1,0:T(8,128)(2,1)} async-done(((bf16[128,1536]{1,0:T(8,128)(2,1)}), bf16[512,1536]{1,0:T(8,128)(2,1)}) %all-gather.9.cloned.1.call-update) | async-done | bytes 1572880 | tf_op jit(solution)/shard_map/all_gather | solution.py:212
  108.9 3.4 fusion.228
  116.2 14.3 %fusion.244 = (f32[8,1024]{1,0:T(8,128)S(1)}, f32[8,1024,1024]{1,2,0:T(8,128)}) fusion(bf16[1024,8,32]{0,2,1:T(8,128)(2,1)S(1)} %get-tuple-element.210, bf16[1024,8,32]{0,2,1:T(8,128)(2,1)S(1)} %get-tuple-element.211, bf16[1024,8,32]{0,2,1:T(8,128)(2,1)S(1)} %get-tuple-element.203, bf16[1024,8,32]{0,2,1:T(8,128)(2,1)S(1)} %get-tuple-element.202, ...), kind=kOutput, calls=%fused_computation.535 | convolution fusion | flops 1103093760 | bytes 36732928 | tf_op jit(solution)/shard_map/qhd,khd->hqk/dot_general | solution.py:156
  130.5 13.1 %fusion = f32[8,1024]{1,0:T(8,128)S(1)} fusion(f32[8,1024,1024]{1,2,0:T(8,128)} %get-tuple-element.298, f32[8,1024]{1,0:T(8,128)S(1)} %get-tuple-element.297), kind=kLoop, calls=%fused_computation.6 | loop fusion | flops 16769024 | bytes 33619968 | tf_op jit(solution)/shard_map/reduce_sum | solution.py:253
  143.6 14.2 %fusion.131 = bf16[8,64,1024]{2,1,0:T(8,128)(2,1)S(1)} fusion(f32[8,1024,1024]{1,2,0:T(8,128)} %get-tuple-element.298, f32[8,1024]{1,0:T(8,128)S(1)} %fusion, f32[8,1024]{1,0:T(8,128)S(1)} %get-tuple-element.297, f32[1024,3,8,64]{0,3,2,1:T(8,128)} %bitcast.250), kind=kOutput, calls=%fused_computation.310 | convolution fusion | flops 1099431936 | bytes 35717120 | tf_op jit(solution)/shard_map/hqk,khd->qhd/dot_general | solution.py:256
  165.3 22.4 %multiply_reduce_fusion.1 = (f32[512]{0:T(512)S(1)}, f32[512]{0:T(512)S(1)}, f32[1024,512]{0,1:T(8,128)}) fusion(f32[1024]{0:T(1024)S(1)} %get-tuple-element.278, f32[1024]{0:T(1024)S(1)} %get-tuple-element.291, f32[512]{0:T(512)S(1)} %bitcast.368, f32[1024]{0:T(1024)S(1)} %get-tuple-element.261, f32[512]{0:T(512)S(1)} %bitcast.366, ...), kind=kLoop, calls=%fused_computation.30 | loop fusion | flops 51379200 | bytes 4395008 | tf_op jit(solution)/shard_map/reduce_sum | solution.py:272
  187.7 39.7 %all-reduce.35 = (f32[512]{0:T(512)S(1)}, f32[]{:T(128)}, f32[512]{0:T(512)S(1)}) all-reduce(f32[512]{0:T(512)S(1)} %get-tuple-element.147, f32[]{:T(128)} %fusion.224, f32[512]{0:T(512)S(1)} %get-tuple-element.146), channel_id=1, replica_groups=mesh['dp'=8,'fsdp'=4] {'dp','fsdp'}, use_global_device_ids=true, to_apply=%region_16.17 | all-reduce | flops 1025 | bytes 8200 | tf_op jit(solution)/shard_map/psum | solution.py:270
  234.0 3.9 multiply_convert_fusion.3
  244.0 5.2 multiply_convert_fusion.2
  249.2 4.2 fusion.251
  256.3 3.6 multiply_reduce_fusion.3
  260.0 4.1 multiply_add_fusion.4
  267.2 5.1 fusion.230
  272.3 41.2 %all-reduce.34 = (f32[512]{0:T(512)S(1)}, f32[512]{0:T(512)S(1)}) all-reduce(f32[512]{0:T(512)S(1)} %get-tuple-element.153, f32[512]{0:T(512)S(1)} %get-tuple-element.152), channel_id=1, replica_groups=mesh['dp'=8,'fsdp'=4] {'dp','fsdp'}, use_global_device_ids=true, to_apply=%region_28.29 | all-reduce | flops 1024 | bytes 8192 | tf_op jit(solution)/shard_map/psum | solution.py:324
  313.9 10.5 %multiply_reduce_fusion.6 = (f32[512]{0:T(512)}, f32[512]{0:T(512)}, f32[512]{0:T(512)}, f32[512]{0:T(512)}, f32[512]{0:T(512)}, /*index=5*/f32[512]{0:T(512)}, ...) fusion(f32[1024,512]{0,1:T(8,128)S(1)} %slice_multiply_fusion, f32[1024]{0:T(1024)S(1)} %get-tuple-element.291, ...), kind=kLoop, calls=%fused_computation.219 | loop fusion | flops 18345472 | bytes 8458244 | tf_op jit(solution)/shard_map/reduce_sum | solution.py:125
  324.7 21.7 %multiply_convert_fusion.7 = (bf16[1024,512]{0,1:T(8,128)(2,1)S(1)}, f32[1024,512]{0,1:T(8,128)S(1)}) fusion(f32[1024,1024]{0,1:T(8,128)S(1)} %copy-done.16, f32[1024]{0:T(1024)S(1)} %bitcast.374, f32[512]{0:T(512)S(1)} %bitcast.369, f32[1024]{0:T(1024)S(1)} %bitcast.403, f32[512]{0:T(512)S(1)} %bitcast.367, f32[1024]{0:T(1024)S(1)} %bitcast.402, ...), kind=kLoop, calls=%fused_computation.263 | loop fusion | flops 51904512 | bytes 7532544 | tf_op jit(solution)/shard_map/convert.11
  348.0 3.2 fusion.250
  366.3 23.2 %multiply_reduce_fusion = (f32[8,1024]{1,0:T(8,128)S(1)}, f32[8,1024,1024]{1,2,0:T(8,128)}) fusion(f32[8,1024,1024]{1,2,0:T(8,128)} %get-tuple-element.298, f32[8,1024]{1,0:T(8,128)S(1)} %log_add_fusion, bf16[1024,8,64]{0,2,1:T(8,128)(2,1)S(1)} %bitcast.247, f32[1024,3,8,64]{0,3,2,1:T(8,128)} %bitcast.251), kind=kOutput, calls=%fused_computation.1 | convolution fusion | flops 1098899456 | bytes 69271552 | tf_op jit(solution)/shard_map/qhd,khd->hqk/dot_general | solution.py:351
  389.5 29.2 %multiply_convert_fusion = bf16[8,1024,1024]{1,2,0:T(8,128)(2,1)} fusion(f32[8,1024,1024]{1,2,0:T(8,128)} %get-tuple-element.309, f32[8,1024,1024]{1,2,0:T(8,128)} %get-tuple-element.298, f32[8,1024]{1,0:T(8,128)S(1)} %get-tuple-element.308, f32[8,1024]{1,0:T(8,128)S(1)} %log_add_fusion), kind=kLoop, calls=%fused_computation | loop fusion | flops 33554432 | bytes 83951616 | tf_op jit(solution)/shard_map/convert_element_type | solution.py:352
  418.7 11.3 %multiply_bitcast_fusion = f32[1024,8,64]{0,2,1:T(8,128)S(1)} fusion(bf16[8,1024,1024]{1,2,0:T(8,128)(2,1)} %multiply_convert_fusion, bf16[1024,8,32]{0,2,1:T(8,128)(2,1)} %copy-done.50, bf16[1024,8,32]{0,2,1:T(8,128)(2,1)} %copy-done.49), kind=kOutput, calls=%fused_computation.258 | convolution fusion | flops 1076363264 | bytes 19922944 | tf_op jit(solution)/shard_map/hqk,qhd->khd/dot_general | solution.py:360
  430.1 9.2 multiply_bitcast_fusion.1
  442.1 14.5 %fusion.132 = bf16[1024,1,8,64]{0,3,2,1:T(8,128)(2,1)} fusion(bf16[1024,8,64]{0,2,1:T(8,128)(2,1)S(1)} %bitcast.248, f32[8,1024,1024]{1,2,0:T(8,128)} %get-tuple-element.298, f32[8,1024]{1,0:T(8,128)S(1)} %log_add_fusion), kind=kOutput, calls=%fused_computation.311 | convolution fusion | flops 1091043328 | bytes 35684352 | tf_op jit(solution)/shard_map/hqk,qhd->khd/dot_general | solution.py:348
  460.7 3.6 fusion.227
  464.3 5.5 fusion.249
  484.8 4.3 pad_maximum_fusion.1
  490.8 7.3 multiply_convert_fusion.1
  505.5 3.9 pad_maximum_fusion
  509.5 5.9 fusion.248
  517.5 3.1 fusion.111
  522.1 7.9 multiply_reduce_fusion.24
  530.1 5.9 multiply_reduce_fusion.15
  536.2 4.8 multiply_reduce_fusion.33
  543.8 32.8 %reduce-scatter.11.cloned.1.call-done = f32[2,512,512]{2,1,0:T(8,128)} async-done(((f32[2,2048,512]{2,1,0:T(8,128)}), f32[2,512,512]{2,1,0:T(8,128)}) %reduce-scatter.11.cloned.1.call-update) | async-done | bytes 2097168 | tf_op jit(solution)/shard_map/reduce_scatter | solution.py:405
  576.6 74.3 %reduce-scatter.9.cloned.1.call-done = f32[2,128,2048]{2,1,0:T(8,128)} async-done(((f32[2,512,2048]{2,1,0:T(8,128)}), f32[2,128,2048]{2,1,0:T(8,128)}) %reduce-scatter.9.cloned.1.call-update) | async-done | bytes 2097168 | tf_op jit(solution)/shard_map/reduce_scatter | solution.py:404
  653.5 3.6 fusion.110
  660.2 13.2 %reduce-scatter.23.cloned.1.call-done = f32[12,128]{1,0:T(8,128)} async-done(((f32[12,512]{1,0:T(8,128)}), f32[12,128]{1,0:T(8,128)}) %reduce-scatter.23.cloned.1.call-update) | async-done | bytes 6160 | tf_op jit(solution)/shard_map/reduce_scatter | solution.py:411
  673.4 22.4 %reduce-scatter.21.cloned.1.call-done = f32[32,128]{1,0:T(8,128)} async-done(((f32[32,512]{1,0:T(8,128)}), f32[32,128]{1,0:T(8,128)}) %reduce-scatter.21.cloned.1.call-update) | async-done | bytes 16400 | tf_op jit(solution)/shard_map/reduce_scatter | solution.py:410
  695.8 40.0 %all-reduce.36 = (f32[32,128]{1,0:T(8,128)S(1)}, f32[12,128]{1,0:T(8,128)S(1)}) all-reduce(f32[32,128]{1,0:T(8,128)} %reduce-scatter.21.cloned.1.call-done, f32[12,128]{1,0:T(8,128)} %reduce-scatter.23.cloned.1.call-done), channel_id=1, replica_groups=mesh['dp'=8,'fsdp'=4] {'dp'}, use_global_device_ids=true, to_apply=%region_81.82 | all-reduce | flops 5632 | bytes 45056 | tf_op jit(solution)/shard_map/psum | solution.py:413
  737.1 174.0 %all-reduce.40.cloned.1.call-done = (f32[2,128,2048]{2,1,0:T(8,128)}, f32[2,512,512]{2,1,0:T(8,128)}, f32[128,1536]{1,0:T(8,128)}, f32[128,512]{1,0:T(8,128)}, f32[128,1024]{1,0:T(8,128)}, /*index=5*/f32[128,512]{1,0:T(8,128)}) async-done(((f32[2,128,2048]{2,1,0:T(8,128)}, f32[2,512,512]{2,1,0:T(8,128)}, f32[128,1536]{1,0:T(8,128)}, f32[128,512]{1,0:T(8,128)}, f32[128,1024]{1,0:T(8,128)}, ...) | async-done | bytes 6029328 | tf_op jit(solution)/shard_map/psum | solution.py:413
  921.1 4.2 multiply_subtract_fusion.1
  926.8 3.9 multiply_subtract_fusion
  (647 shorter events, 136.9 us)
Async XLA Ops:
  7.2 66.7 %all-gather.5.cloned.1.call-start = ((), (), s32[]{:S(2)}) async-start(), calls=%async_computation.8 | async-start | bytes 5242880 | tf_op jit(solution)/shard_map/all_gather | solution.py:210
  10.2 76.9 %all-gather.7.cloned.1.call-start = ((), (), s32[]{:S(2)}) async-start(), calls=%async_computation.9 | async-start | bytes 5242880 | tf_op jit(solution)/shard_map/all_gather | solution.py:211
  11.4 97.5 %all-gather.9.cloned.1.call-start = ((), (), s32[]{:S(2)}) async-start(), calls=%async_computation.10 | async-start | bytes 1966080 | tf_op jit(solution)/shard_map/all_gather | solution.py:212
  12.2 146.8 %all-gather.11.cloned.1.call-start = ((), (), s32[]{:S(2)}) async-start(), calls=%async_computation.11 | async-start | bytes 1310720 | tf_op jit(solution)/shard_map/all_gather | solution.py:214
  13.1 530.6 %reduce-scatter.19.cloned.1.call-start = ((), (), s32[]{:S(2)}) async-start(), calls=%async_computation.17 | async-start | bytes 1310720 | tf_op jit(solution)/shard_map/reduce_scatter | solution.py:409
  22.1 142.6 %copy-start.81 = (f32[1024]{0:T(1024)}, f32[1024]{0:T(1024)S(1)}, u32[]{:S(2)}) copy-start(f32[1024]{0:T(1024)S(1)} %get-tuple-element.279) | copy-start | bytes 12292
  22.2 142.6 %copy-start.83 = (f32[1024]{0:T(1024)}, f32[1024]{0:T(1024)S(1)}, u32[]{:S(2)}) copy-start(f32[1024]{0:T(1024)S(1)} %get-tuple-element.288) | copy-start | bytes 12292
  22.2 142.6 %copy-start.85 = (f32[1024]{0:T(1024)}, f32[1024]{0:T(1024)S(1)}, u32[]{:S(2)}) copy-start(f32[1024]{0:T(1024)S(1)} %get-tuple-element.289) | copy-start | bytes 12292
  22.2 142.6 %copy-start.87 = (f32[1024]{0:T(1024)}, f32[1024]{0:T(1024)S(1)}, u32[]{:S(2)}) copy-start(f32[1024]{0:T(1024)S(1)} %get-tuple-element.290) | copy-start | bytes 12292
  22.2 142.6 %copy-start.89 = (f32[1024]{0:T(1024)}, f32[1024]{0:T(1024)S(1)}, u32[]{:S(2)}) copy-start(f32[1024]{0:T(1024)S(1)} %get-tuple-element.280) | copy-start | bytes 12292
  22.2 142.6 %copy-start.91 = (f32[1024]{0:T(1024)}, f32[1024]{0:T(1024)S(1)}, u32[]{:S(2)}) copy-start(f32[1024]{0:T(1024)S(1)} %get-tuple-element.281) | copy-start | bytes 12292
  22.2 142.6 %copy-start.93 = (f32[1024]{0:T(1024)}, f32[1024]{0:T(1024)S(1)}, u32[]{:S(2)}) copy-start(f32[1024]{0:T(1024)S(1)} %get-tuple-element.282) | copy-start | bytes 12292
  22.2 142.6 %copy-start.95 = (f32[1024]{0:T(1024)}, f32[1024]{0:T(1024)S(1)}, u32[]{:S(2)}) copy-start(f32[1024]{0:T(1024)S(1)} %get-tuple-element.283) | copy-start | bytes 12292
  22.2 142.6 %copy-start.97 = (f32[1024]{0:T(1024)}, f32[1024]{0:T(1024)S(1)}, u32[]{:S(2)}) copy-start(f32[1024]{0:T(1024)S(1)} %get-tuple-element.284) | copy-start | bytes 12292
  22.2 142.6 %copy-start.99 = (f32[1024]{0:T(1024)}, f32[1024]{0:T(1024)S(1)}, u32[]{:S(2)}) copy-start(f32[1024]{0:T(1024)S(1)} %get-tuple-element.285) | copy-start | bytes 12292
  22.2 142.6 %copy-start.101 = (f32[1024]{0:T(1024)}, f32[1024]{0:T(1024)S(1)}, u32[]{:S(2)}) copy-start(f32[1024]{0:T(1024)S(1)} %get-tuple-element.286) | copy-start | bytes 12292
  22.3 142.6 %copy-start.103 = (f32[1024]{0:T(1024)}, f32[1024]{0:T(1024)S(1)}, u32[]{:S(2)}) copy-start(f32[1024]{0:T(1024)S(1)} %get-tuple-element.287) | copy-start | bytes 12292
  22.4 142.5 %copy-start.105 = (f32[1024]{0:T(1024)}, f32[1024]{0:T(1024)S(1)}, u32[]{:S(2)}) copy-start(f32[1024]{0:T(1024)S(1)} %get-tuple-element.260) | copy-start | bytes 12292
  22.4 142.5 %copy-start.107 = (f32[1024]{0:T(1024)}, f32[1024]{0:T(1024)S(1)}, u32[]{:S(2)}) copy-start(f32[1024]{0:T(1024)S(1)} %get-tuple-element.277) | copy-start | bytes 12292
  22.4 142.5 %copy-start.111 = (f32[1024]{0:T(1024)}, f32[1024]{0:T(1024)S(1)}, u32[]{:S(2)}) copy-start(f32[1024]{0:T(1024)S(1)} %get-tuple-element.269) | copy-start | bytes 12292
  22.4 142.5 %copy-start.113 = (f32[1024]{0:T(1024)}, f32[1024]{0:T(1024)S(1)}, u32[]{:S(2)}) copy-start(f32[1024]{0:T(1024)S(1)} %get-tuple-element.270) | copy-start | bytes 12292
  22.4 142.5 %copy-start.115 = (f32[1024]{0:T(1024)}, f32[1024]{0:T(1024)S(1)}, u32[]{:S(2)}) copy-start(f32[1024]{0:T(1024)S(1)} %get-tuple-element.271) | copy-start | bytes 12292
  22.4 142.5 %copy-start.117 = (f32[1024]{0:T(1024)}, f32[1024]{0:T(1024)S(1)}, u32[]{:S(2)}) copy-start(f32[1024]{0:T(1024)S(1)} %get-tuple-element.272) | copy-start | bytes 12292
  22.4 142.5 %copy-start.119 = (f32[1024]{0:T(1024)}, f32[1024]{0:T(1024)S(1)}, u32[]{:S(2)}) copy-start(f32[1024]{0:T(1024)S(1)} %get-tuple-element.273) | copy-start | bytes 12292
  22.4 142.5 %copy-start.121 = (f32[1024]{0:T(1024)}, f32[1024]{0:T(1024)S(1)}, u32[]{:S(2)}) copy-start(f32[1024]{0:T(1024)S(1)} %get-tuple-element.274) | copy-start | bytes 12292
  22.4 142.5 %copy-start.123 = (f32[1024]{0:T(1024)}, f32[1024]{0:T(1024)S(1)}, u32[]{:S(2)}) copy-start(f32[1024]{0:T(1024)S(1)} %get-tuple-element.275) | copy-start | bytes 12292
  22.4 142.5 %copy-start.125 = (f32[1024]{0:T(1024)}, f32[1024]{0:T(1024)S(1)}, u32[]{:S(2)}) copy-start(f32[1024]{0:T(1024)S(1)} %get-tuple-element.276) | copy-start | bytes 12292
  164.7 148.8 %copy-start = (f32[1024,512]{0,1:T(8,128)}, f32[1024,512]{0,1:T(8,128)S(1)}, u32[]{:S(2)}) copy-start(f32[1024,512]{0,1:T(8,128)S(1)} %slice_multiply_fusion) | copy-start | bytes 6291460
  272.3 271.5 %reduce-scatter.15.cloned.1.call-start = ((), (), s32[]{:S(2)}) async-start(), calls=%async_computation.15 | async-start | bytes 1310720 | tf_op jit(solution)/shard_map/reduce_scatter | solution.py:407
  360.8 183.0 %reduce-scatter.17.cloned.1.call-start = ((), (), s32[]{:S(2)}) async-start(), calls=%async_computation.16 | async-start | bytes 2621440 | tf_op jit(solution)/shard_map/reduce_scatter | solution.py:408
  366.2 177.6 %reduce-scatter.13.cloned.1.call-start = ((), (), s32[]{:S(2)}) async-start(), calls=%async_computation.14 | async-start | bytes 3932160 | tf_op jit(solution)/shard_map/reduce_scatter | solution.py:406
  464.3 112.4 %reduce-scatter.11.cloned.1.call-start = ((), (), s32[]{:S(2)}) async-start(), calls=%async_computation.13 | async-start | bytes 10485760 | tf_op jit(solution)/shard_map/reduce_scatter | solution.py:405
  489.2 161.8 %reduce-scatter.9.cloned.1.call-start = ((), (), s32[]{:S(2)}) async-start(), calls=%async_computation.12 | async-start | bytes 10485760 | tf_op jit(solution)/shard_map/reduce_scatter | solution.py:404
  509.4 163.9 %reduce-scatter.23.cloned.1.call-start = ((), (), s32[]{:S(2)}) async-start(), calls=%async_computation.19 | async-start | bytes 40960 | tf_op jit(solution)/shard_map/reduce_scatter | solution.py:411
  536.1 159.7 %reduce-scatter.21.cloned.1.call-start = ((), (), s32[]{:S(2)}) async-start(), calls=%async_computation.18 | async-start | bytes 81920 | tf_op jit(solution)/shard_map/reduce_scatter | solution.py:410
  543.7 367.4 %all-reduce.40.cloned.1.call-start = ((), (), s32[]{:S(2)}) async-start(), calls=%async_computation.20 | async-start | bytes 12058624 | tf_op jit(solution)/shard_map/psum | solution.py:413
  657.0 79.4 %copy-start.110 = (f32[32,128]{1,0:T(8,128)S(1)}, f32[32,128]{1,0:T(8,128)}, u32[]{:S(2)}) copy-start(f32[32,128]{1,0:T(8,128)} %param.48) | copy-start | bytes 49156
  657.0 79.4 %copy-start.200 = (f32[32,128]{1,0:T(8,128)S(1)}, f32[32,128]{1,0:T(8,128)}, u32[]{:S(2)}) copy-start(f32[32,128]{1,0:T(8,128)} %param.49) | copy-start | bytes 49156
  657.0 254.0 %copy-start.60 = (f32[128,512]{1,0:T(8,128)S(1)}, f32[128,512]{1,0:T(8,128)}, u32[]{:S(2)}) copy-start(f32[128,512]{1,0:T(8,128)} %param.39) | copy-start | bytes 786436
  657.1 254.0 %copy-start.73 = (f32[128,512]{1,0:T(8,128)S(1)}, f32[128,512]{1,0:T(8,128)}, u32[]{:S(2)}) copy-start(f32[128,512]{1,0:T(8,128)} %param.40) | copy-start | bytes 786436
  657.1 254.0 %copy-start.74 = (f32[128,512]{1,0:T(8,128)S(1)}, f32[128,512]{1,0:T(8,128)}, u32[]{:S(2)}) copy-start(f32[128,512]{1,0:T(8,128)} %param.41) | copy-start | bytes 786436
  657.1 256.0 %copy-start.62 = (f32[128,512]{1,0:T(8,128)S(1)}, f32[128,512]{1,0:T(8,128)}, u32[]{:S(2)}) copy-start(f32[128,512]{1,0:T(8,128)} %param.45) | copy-start | bytes 786436
  657.1 256.0 %copy-start.75 = (f32[128,512]{1,0:T(8,128)S(1)}, f32[128,512]{1,0:T(8,128)}, u32[]{:S(2)}) copy-start(f32[128,512]{1,0:T(8,128)} %param.46) | copy-start | bytes 786436
  657.1 256.0 %copy-start.76 = (f32[128,512]{1,0:T(8,128)S(1)}, f32[128,512]{1,0:T(8,128)}, u32[]{:S(2)}) copy-start(f32[128,512]{1,0:T(8,128)} %param.47) | copy-start | bytes 786436
  657.1 258.1 %copy-start.72 = (f32[128,1024]{1,0:T(8,128)S(1)}, f32[128,1024]{1,0:T(8,128)}, u32[]{:S(2)}) copy-start(f32[128,1024]{1,0:T(8,128)} %param.44) | copy-start | bytes 1572868
  660.2 255.1 %copy-start.52 = (f32[128,1024]{1,0:T(8,128)S(1)}, f32[128,1024]{1,0:T(8,128)}, u32[]{:S(2)}) copy-start(f32[128,1024]{1,0:T(8,128)} %param.42) | copy-start | bytes 1572868
  660.2 255.1 %copy-start.71 = (f32[128,1024]{1,0:T(8,128)S(1)}, f32[128,1024]{1,0:T(8,128)}, u32[]{:S(2)}) copy-start(f32[128,1024]{1,0:T(8,128)} %param.43) | copy-start | bytes 1572868
  735.8 182.1 %copy-start.207 = (f32[12,128]{1,0:T(8,128)}, f32[12,128]{1,0:T(8,128)S(1)}, u32[]{:S(2)}) copy-start(f32[12,128]{1,0:T(8,128)S(1)} %get-tuple-element.162) | copy-start | bytes 18436
  (211 other events, 1871.9 us)
Sparse Core Ops, SparseCore 0:
  10.3 37.2 all-gather.4
  49.7 37.3 all-gather.6
  89.2 19.6 all-gather.8
  110.9 16.7 all-gather.10
  272.4 25.8 reduce-scatter.18
  360.9 24.6 reduce-scatter.14
  388.7 31.4 reduce-scatter.16
  464.4 37.8 reduce-scatter.12
  504.9 71.7 reduce-scatter.10
  579.2 71.6 reduce-scatter.8
  654.0 19.3 reduce-scatter.22
  676.3 19.4 reduce-scatter.20
  700.9 210.1 all-reduce.39
where the time goes:
time: 941 us; the launch traced here: 937 us
  waiting for transfers between devices  338 us (36%)
  other arithmetic  186 us (20%)
  matrix products  175 us (19%)
  blocking collectives  152 us (16%)
  local copies, waits for them, and re-layouts  68.8 us (7%)
  between operations  17.4 us (2%)
    psum x1, waiting for transfers between devices, per_device(): lax.psum((shards[0], shards[1], shards[2], shards[3], shards[4], shards[5...  174 us
    reduce_scatter x1, waiting for transfers between devices, per_device(): lax.psum_scatter(gradients[0], 'fsdp', scatter_dimension=1, tiled=True)  74.3 us
    psum x1, blocking collectives, per_device(): totals = lax.psum((local_bias, local_gain), ('dp', 'fsdp'))  41.2 us
    psum x1, blocking collectives, per_device(): lax.psum((shards[0], shards[1], shards[2], shards[3], shards[4], shards[5...  40 us
    psum x1, blocking collectives, per_device(): lax.psum((jnp.sum(valid_col * convolution_module, axis=0), jnp.sum(valid_...  39.7 us
    dot_general x8, matrix products, times_transposed(): lax.dot_general(left, right, (((1,), (1,)), ((), ())), preferred_element_...  39.1 us
    reduce_scatter x1, waiting for transfers between devices, per_device(): lax.psum_scatter(gradients[1], 'fsdp', scatter_dimension=1, tiled=True)  32.8 us
    unnamed x496, local copies, waits for them, and re-layouts  31 us
  transfers between devices with their start and end apart: 13, of which 7 were waited for; matrix products, arithmetic and copies ran while one was open for 34% of the time, Pallas kernels for 0%

commit v1 on v0

--- a/solution.py
+++ b/solution.py
@@ -173,6 +173,88 @@
     first_new = beta_first * first + (1.0 - beta_first) * grad
     second_new = beta_second * second_block + (1.0 - beta_second) * grad * grad
     return (first_new, second_new)
+
+
+def bits_of(size):
+    return int(size).bit_length() - 1
+
+
+def swap(value, axis, size, bit):
+    pairs = [(k, k ^ (1 << bit)) for k in range(size)]
+    return lax.ppermute(value, axis, pairs)
+
+
+def gather_shards(own, fs):
+    me = lax.axis_index("fsdp")
+    pieces, rel = own[None], [0]
+    for bit in reversed(range(bits_of(fs))):
+        other = swap(pieces, "fsdp", fs, bit)
+        pieces = jnp.concatenate([pieces, other], axis=0)
+        rel = rel + [r ^ (1 << bit) for r in rel]
+    full = jnp.zeros((fs,) + own.shape, own.dtype)
+    for k, r in enumerate(rel):
+        full = lax.dynamic_update_slice_in_dim(full, pieces[k : k + 1], me ^ r, 0)
+    return full
+
+
+def halve(value, axis, size, bit, side):
+    send = lax.dynamic_index_in_dim(value, 1 - side, 0, keepdims=False)
+    keep = lax.dynamic_index_in_dim(value, side, 0, keepdims=False)
+    got = swap(send, axis, size, bit)
+    return (keep.astype(jnp.float32) + got.astype(jnp.float32)).astype(value.dtype)
+
+
+def reduce_all(grad, fs, dp):
+    me = lax.axis_index("fsdp")
+    pack = lax.axis_index("dp")
+    part = grad
+    for bit in range(bits_of(fs)):
+        shape = part.shape
+        pairs = part.reshape((shape[0] // 2, 2) + shape[1:]).swapaxes(0, 1)
+        part = halve(pairs, "fsdp", fs, bit, (me >> bit) & 1)
+    part = part[0]
+    for bit in range(bits_of(dp)):
+        rows = part.shape[0]
+        part = halve(part.reshape((2, rows // 2) + part.shape[1:]), "dp", dp, bit, (pack >> bit) & 1)
+    for bit in reversed(range(bits_of(dp))):
+        other = swap(part, "dp", dp, bit)
+        side = (pack >> bit) & 1
+        both = jnp.zeros((2,) + part.shape, part.dtype)
+        both = lax.dynamic_update_slice_in_dim(both, part[None], side, 0)
+        both = lax.dynamic_update_slice_in_dim(both, other[None], 1 - side, 0)
+        part = both.reshape((2 * part.shape[0],) + part.shape[1:])
+    return part
+
+
+def total_over_all(rows):
+    axes = ("dp", "fsdp")
+    count = lax.axis_size(axes)
+    spread = jnp.broadcast_to(rows[None], (count,) + rows.shape)
+    got = lax.all_to_all(spread, axes, 0, 0, tiled=True)
+    return jnp.sum(got, axis=0)
+
+
+def to_rows(block):
+    r, c = block.shape
+    k = c // 512
+    return block.reshape(r, k, 512).swapaxes(0, 1).reshape(k * r, 512)
+
+
+def from_rows(rows, r, c):
+    k = c // 512
+    return rows.reshape(k, r, 512).swapaxes(0, 1).reshape(r, c)
+
+
+def owners_rows(grad, fs):
+    r = grad.shape[0] // fs
+    k = grad.shape[1] // 512
+    return grad.astype(jnp.bfloat16).reshape(fs, r, k, 512).swapaxes(1, 2).reshape(fs, k * r, 512)
+
+
+def full_of(rows, r, c):
+    fs = rows.shape[0]
+    k = c // 512
+    return rows.reshape(fs, k, r, 512).swapaxes(1, 2).reshape(fs * r, c)
 
 
 def per_device(
@@ -206,26 +288,31 @@
 ):
     masters = (expand, shrink, attend, heads_out, pointwise, pointwise_out, depthwise, norm_table)
     rounded_value = [master.astype(jnp.bfloat16) for master in masters]
-    fetched = (
-        lax.all_gather(rounded_value[0], "fsdp", axis=1, tiled=True),
-        lax.all_gather(rounded_value[1], "fsdp", axis=1, tiled=True),
-        lax.all_gather(rounded_value[2], "fsdp", axis=0, tiled=True),
-        lax.all_gather(rounded_value[3], "fsdp", axis=0, tiled=True),
-        lax.all_gather(rounded_value[4], "fsdp", axis=0, tiled=True),
-        lax.all_gather(rounded_value[5], "fsdp", axis=0, tiled=True),
-        lax.all_gather(rounded_value[6], "fsdp", axis=1, tiled=True),
-        lax.all_gather(rounded_value[7], "fsdp", axis=1, tiled=True),
-    )
-    (
-        full_expand,
-        full_shrink,
-        full_attend,
-        full_heads,
-        full_point,
-        full_point_out,
-        full_depth,
-        full_norms,
-    ) = fetched
+    fs, dp = (lax.axis_size("fsdp"), lax.axis_size("dp"))
+    er, sr, ar = expand.shape[1], shrink.shape[1], attend.shape[0]
+    dr = depthwise.shape[1]
+    small = jnp.concatenate([rounded_value[6], rounded_value[7]], axis=0)
+    tiny_rows = small.shape[0]
+    in_zero = gather_shards(to_rows(rounded_value[0][0]), fs)
+    small_full = gather_shards(small, fs)
+    out_zero = gather_shards(rounded_value[1][0], fs)
+    attn_full = gather_shards(
+        jnp.concatenate([to_rows(rounded_value[2]), rounded_value[3]], axis=0), fs
+    )
+    conv_full = gather_shards(
+        jnp.concatenate([to_rows(rounded_value[4]), rounded_value[5]], axis=0), fs
+    )
+    ff_one = gather_shards(
+        jnp.concatenate([to_rows(rounded_value[0][1]), rounded_value[1][1]], axis=0), fs
+    )
+    full_expand = (full_of(in_zero, er, 2048), full_of(ff_one[:, : 4 * er], er, 2048))
+    full_shrink = (out_zero.reshape(fs * sr, 512), ff_one[:, 4 * er :].reshape(fs * sr, 512))
+    full_attend = full_of(attn_full[:, : 3 * ar], ar, 1536)
+    full_heads = attn_full[:, 3 * ar :].reshape(fs * ar, 512)
+    full_point = full_of(conv_full[:, : 2 * ar], ar, 1024)
+    full_point_out = conv_full[:, 2 * ar :].reshape(fs * ar, 512)
+    small_cols = small_full.swapaxes(0, 1).reshape(tiny_rows, fs * dr)
+    full_depth, full_norms = (small_cols[:32], small_cols[32:])
     norm_entries = full_norms.astype(jnp.float32)
     kernel = full_depth.astype(jnp.float32)
     value = frames.astype(jnp.float32)
@@ -267,13 +354,15 @@
     sigma = jax.nn.sigmoid(gates[:, width:])
     glu = half_value * sigma
     convolution_module, padded_glu = depth_forward(glu, kernel, masks)
-    stats = lax.psum(
-        (
-            jnp.sum(valid_col * convolution_module, axis=0),
-            jnp.sum(valid_col * convolution_module * convolution_module, axis=0),
-            jnp.sum(valid_col),
-        ),
-        ("dp", "fsdp"),
+    masked = valid_col * convolution_module
+    stats = total_over_all(
+        jnp.stack(
+            [
+                jnp.sum(masked, axis=0),
+                jnp.sum(masked * convolution_module, axis=0),
+                jnp.broadcast_to(jnp.sum(valid_col), (width,)),
+            ]
+        )
     )
     valid_count = stats[2]
     masked_mean = stats[0] / valid_count
@@ -289,26 +378,18 @@
         fourth_block, norm_entries[10], norm_entries[11]
     )
     layer_output = (last_out * valid_col).astype(jnp.bfloat16)
-    refetched = (
-        lax.all_gather(rounded_value[0], "fsdp", axis=1, tiled=True),
-        lax.all_gather(rounded_value[1], "fsdp", axis=1, tiled=True),
-        lax.all_gather(rounded_value[2], "fsdp", axis=0, tiled=True),
-        lax.all_gather(rounded_value[3], "fsdp", axis=0, tiled=True),
-        lax.all_gather(rounded_value[4], "fsdp", axis=0, tiled=True),
-        lax.all_gather(rounded_value[5], "fsdp", axis=0, tiled=True),
-        lax.all_gather(rounded_value[6], "fsdp", axis=1, tiled=True),
-        lax.all_gather(rounded_value[7], "fsdp", axis=1, tiled=True),
-    )
-    (
-        back_expand,
-        back_shrink,
-        back_attend,
-        back_heads,
-        back_point,
-        back_point_out,
-        back_depth,
-        back_norms,
-    ) = refetched
+    back_expand, back_shrink, back_attend, back_heads = (
+        full_expand,
+        full_shrink,
+        full_attend,
+        full_heads,
+    )
+    back_point, back_point_out, back_depth, back_norms = (
+        full_point,
+        full_point_out,
+        full_depth,
+        full_norms,
+    )
     norms_back = back_norms.astype(jnp.float32)
     kernel_back = back_depth.astype(jnp.float32)
     grad_y = cotangent.astype(jnp.float32) * valid_col
@@ -321,7 +402,7 @@
     grad_zed = times_transposed(grad_branch, back_point_out) * swish_slope(zed)
     local_bias = jnp.sum(grad_zed, axis=0)
     local_gain = jnp.sum(grad_zed * zhat, axis=0)
-    totals = lax.psum((local_bias, local_gain), ("dp", "fsdp"))
+    totals = total_over_all(jnp.stack([local_bias, local_gain]))
     grad_conv = (
         batch_norm_scale
         * norms_back[6]
@@ -372,8 +453,6 @@
     frames_grad, grad_in_one, grad_out_one, gain_one, bias_one = feed_back(
         grad_first, back_expand[0], back_shrink[0], norms_back[0], saved_one
     )
-    grad_expand = jnp.stack([grad_in_one, grad_in_two])
-    grad_shrink = jnp.stack([grad_out_one, grad_out_two])
     grad_norms = jnp.stack(
         [
             gain_one,
@@ -390,30 +469,43 @@
             bias_last,
         ]
     )
-    gradients = (
-        grad_expand,
-        grad_shrink,
-        grad_attend,
-        grad_heads,
-        grad_point,
-        grad_point_out,
-        grad_kernel,
-        grad_norms,
-    )
-    shards = (
-        lax.psum_scatter(gradients[0], "fsdp", scatter_dimension=1, tiled=True),
-        lax.psum_scatter(gradients[1], "fsdp", scatter_dimension=1, tiled=True),
-        lax.psum_scatter(gradients[2], "fsdp", scatter_dimension=0, tiled=True),
-        lax.psum_scatter(gradients[3], "fsdp", scatter_dimension=0, tiled=True),
-        lax.psum_scatter(gradients[4], "fsdp", scatter_dimension=0, tiled=True),
-        lax.psum_scatter(gradients[5], "fsdp", scatter_dimension=0, tiled=True),
-        lax.psum_scatter(gradients[6], "fsdp", scatter_dimension=1, tiled=True),
-        lax.psum_scatter(gradients[7], "fsdp", scatter_dimension=1, tiled=True),
-    )
-    reduced = lax.psum(
-        (shards[0], shards[1], shards[2], shards[3], shards[4], shards[5], shards[6], shards[7]),
-        "dp",
-    )
+    small_grad = jnp.concatenate([grad_kernel, grad_norms], axis=0).astype(jnp.bfloat16)
+    small_grad = small_grad.reshape(tiny_rows, fs, dr).swapaxes(0, 1)
+    small_size = tiny_rows * dr
+    small_pad = -small_size % (512 * dp)
+    small_grad = jnp.pad(small_grad.reshape(fs, small_size), ((0, 0), (0, small_pad)))
+    small_grad = small_grad.reshape(fs, -1, 512)
+    red_ff_one = reduce_all(
+        jnp.concatenate([owners_rows(grad_in_two, fs), owners_rows(grad_out_two, fs)], axis=1),
+        fs,
+        dp,
+    )
+    red_conv = reduce_all(
+        jnp.concatenate([owners_rows(grad_point, fs), owners_rows(grad_point_out, fs)], axis=1),
+        fs,
+        dp,
+    )
+    red_attn = reduce_all(
+        jnp.concatenate([owners_rows(grad_attend, fs), owners_rows(grad_heads, fs)], axis=1),
+        fs,
+        dp,
+    )
+    red_out_zero = reduce_all(owners_rows(grad_out_one, fs), fs, dp)
+    red_in_zero = reduce_all(
+        jnp.concatenate([owners_rows(grad_in_one, fs), small_grad], axis=1), fs, dp
+    )
+    red_small = red_in_zero[4 * er :].reshape(-1)[:small_size].reshape(tiny_rows, dr)
+    reduced = (
+        jnp.stack([from_rows(red_in_zero[: 4 * er], er, 2048), from_rows(red_ff_one[: 4 * er], er, 2048)]),
+        jnp.stack([red_out_zero, red_ff_one[4 * er :]]),
+        from_rows(red_attn[: 3 * ar], ar, 1536),
+        red_attn[3 * ar :],
+        from_rows(red_conv[: 2 * ar], ar, 1024),
+        red_conv[2 * ar :],
+        red_small[:32],
+        red_small[32:],
+    )
+    reduced = tuple(value.astype(jnp.float32) for value in reduced)
     firsts = (
         expand_first,
         shrink_first,

time: 941 us -> 689 us (0.73)
  waiting for transfers between devices: 338 us -> 94.9 us
  blocking collectives: 152 us -> 0 us
  local copies, waits for them, and re-layouts: 68.8 us -> 172 us
  starting transfers between devices: 0.54 us -> 53.9 us
  matrix products: 175 us -> 157 us
  between operations: 17.4 us -> 5.86 us
  other arithmetic: 186 us -> 197 us
    psum x1 -> x0, waiting for transfers between devices: 174 us -> none  [per_device(): lax.psum((shards[0], shards[1], shards[2], shards[3], shards[4], shards[5...]
    reduce_scatter x8 -> x0, waiting for transfers between devices: 143 us -> none  [the longest x1 74.3 us: per_device(): lax.psum_scatter(gradients[0], 'fsdp', scatter_dimension=1, tiled=True)]
    psum x3 -> x0, blocking collectives: 121 us -> none  [the longest x1 41.2 us: per_device(): totals = lax.psum((local_bias, local_gain), ('dp', 'fsdp'))]
    ppermute x0 -> x52, waiting for transfers between devices: none -> 91.8 us  [swap(): return lax.ppermute(value, axis, pairs)]
    ppermute x0 -> x52, starting transfers between devices: none -> 43 us  [swap(): return lax.ppermute(value, axis, pairs)]
    all_gather x4 -> x0, blocking collectives: 30.7 us -> none  [the longest x1 11.2 us: per_device(): lax.all_gather(rounded_value[3], 'fsdp', axis=0, tiled=True)]
    dynamic_update_slice x0 -> x44, local copies, waits for them, and re-layouts: none -> 24.5 us  [the longest x19 17.6 us: gather_shards(): full = lax.dynamic_update_slice_in_dim(full, pieces[k:k + 1], me ^ r, 0)]
    reshape x0 -> x13, local copies, waits for them, and re-layouts: none -> 21.3 us  [the longest x7 18.4 us: owners_rows(): grad.astype(jnp.bfloat16).reshape(fs, r, k, 512).swapaxes(1, 2)]
  transfers between devices with their start and end apart: 13 -> 54, of which waited for: 7 -> 23; matrix products, arithmetic and copies ran while one was open for 34% -> 62% of each run, Pallas kernels for 0% -> 0%
where the time goes in v1:
time: 689 us; the launch traced here: 680 us
  other arithmetic  197 us (29%)
  local copies, waits for them, and re-layouts  172 us (25%)
  matrix products  157 us (23%)
  waiting for transfers between devices  94.9 us (14%)
  starting transfers between devices  53.9 us (8%)
    ppermute x52, waiting for transfers between devices, swap(): return lax.ppermute(value, axis, pairs)  91.8 us
    unnamed x621, local copies, waits for them, and re-layouts  50.9 us
    ppermute x52, starting transfers between devices, swap(): return lax.ppermute(value, axis, pairs)  43 us
    dot_general x8, matrix products, times_transposed(): lax.dot_general(left, right, (((1,), (1,)), ((), ())), preferred_element_...  28.3 us
    convert_element_type x1, other arithmetic, per_device(): (prob * (grad_prob - jnp.sum(prob * grad_prob, axis=-1, keepdims=True)))....  28.1 us
    reduce_sum x4, other arithmetic, depth_backward(): jnp.sum(grad * masks[offset] * padded[offset:offset + frames], axis=0)  25.2 us
    another operation x4, other arithmetic  24.6 us
    reduce_sum x1, other arithmetic, per_device(): jnp.sum(masked, axis=0)  23.6 us
  transfers between devices with their start and end apart: 54, of which 23 were waited for; matrix products, arithmetic and copies ran while one was open for 62% of the time, Pallas kernels for 0%

profile of v1, /device:TPU:0, one launch (start us, length us, event | category | flops | bytes accessed | tf_op | source)
XLA Modules:
  0.0 680.4 jit_solution(4048364255072650501)
XLA Ops:
  80.0 10.9 %collective-permute-done.10 = bf16[1,1024,512]{2,1,0:T(8,128)(2,1)} collective-permute-done((bf16[1,1024,512]{2,1,0:T(8,128)(2,1)}, bf16[1,1024,512]{2,1,0:T(8,128)(2,1)}, u32[]{:S(2)}, u32[]{:S(2)}) %collective-permute-start.10) | collective-permute-done | bytes 1048608 | tf_op jit(solution)/shard_map/ppermute | solution.py:184
  110.9 6.0 multiply_convert_fusion.4
  125.8 13.7 %fusion.289 = (f32[8,1024]{1,0:T(8,128)S(1)}, f32[8,1024,1024]{1,2,0:T(8,128)}) fusion(bf16[1024,8,32]{0,2,1:T(8,128)(2,1)S(1)} %get-tuple-element.269, bf16[1024,8,32]{0,2,1:T(8,128)(2,1)S(1)} %get-tuple-element.270, bf16[1024,8,32]{0,2,1:T(8,128)(2,1)S(1)} %get-tuple-element.255, bf16[1024,8,32]{0,2,1:T(8,128)(2,1)S(1)} %get-tuple-element.254, ...), kind=kOutput, calls=%fused_computation.793 | convolution fusion | flops 1103093760 | bytes 36732928 | tf_op jit(solution)/shard_map/qhd,khd->hqk/dot_general | solution.py:156
  139.5 13.1 %fusion = f32[8,1024]{1,0:T(8,128)S(1)} fusion(f32[8,1024,1024]{1,2,0:T(8,128)} %get-tuple-element.362, f32[8,1024]{1,0:T(8,128)S(1)} %get-tuple-element.361), kind=kLoop, calls=%fused_computation.6 | loop fusion | flops 16769024 | bytes 33619968 | tf_op jit(solution)/shard_map/reduce_sum | solution.py:340
  152.6 14.2 %fusion.136 = bf16[8,64,1024]{2,1,0:T(8,128)(2,1)S(1)} fusion(f32[8,1024,1024]{1,2,0:T(8,128)} %get-tuple-element.362, f32[8,1024]{1,0:T(8,128)S(1)} %fusion, f32[8,1024]{1,0:T(8,128)S(1)} %get-tuple-element.361, f32[1024,3,8,64]{0,3,2,1:T(8,128)} %copy-done.36), kind=kOutput, calls=%fused_computation.337 | convolution fusion | flops 1099431936 | bytes 35717120 | tf_op jit(solution)/shard_map/hqk,khd->qhd/dot_general | solution.py:343
  173.7 23.6 %multiply_reduce_fusion.1 = (f32[512]{0:T(512)S(1)}, f32[512]{0:T(512)S(1)}, f32[1024,512]{0,1:T(8,128)}) fusion(f32[1024]{0:T(1024)S(1)} %get-tuple-element.343, f32[1024]{0:T(1024)S(1)} %copy-done.116, f32[512]{0:T(512)S(1)} %get-tuple-element.272, f32[1024]{0:T(1024)S(1)} %copy-done.138, f32[512]{0:T(512)S(1)} %get-tuple-element.273, ...), kind=kLoop, calls=%fused_computation.30 | loop fusion | flops 51379200 | bytes 4395008 | tf_op jit(solution)/shard_map/reduce_sum | solution.py:361
  198.9 5.0 all-to-all-start
  228.7 3.9 multiply_convert_fusion.3
  238.8 4.3 convolution_convert_fusion.1
  243.1 4.8 multiply_convert_fusion.2
  247.9 4.2 fusion.296
  252.1 3.8 convolution_convert_fusion.2
  255.9 4.6 reshape.868
  266.8 3.6 multiply_reduce_fusion.3
  270.4 4.4 multiply_add_fusion.2
  277.5 5.1 fusion.263
  283.3 5.8 all-to-all-start.1
  297.6 9.3 %multiply_reduce_fusion.6 = (bf16[512]{0:T(512)(128)(2,1)S(1)}, bf16[512]{0:T(512)(128)(2,1)S(1)}, bf16[512]{0:T(512)(128)(2,1)S(1)}, bf16[512]{0:T(512)(128)(2,...) fusion(f32[1024,512]{0,1:T(8,128)S(1)} %slice_multiply_fusion, ...), kind=kLoop, calls=%fused_computation.246 | loop fusion | flops 18345472 | bytes 8451072 | tf_op jit(solution)/shard_map/reduce_sum | solution.py:125
  307.0 6.6 multiply_reduce_fusion.24
  313.6 5.7 multiply_reduce_fusion.15
  319.7 3.6 multiply_reduce_fusion.33
  323.7 22.9 %multiply_convert_fusion.7 = (bf16[1024,512]{0,1:T(8,128)(2,1)S(1)}, f32[1024,512]{0,1:T(8,128)S(1)}) fusion(f32[1024,1024]{0,1:T(8,128)S(1)} %copy-done.10, f32[1024]{0:T(1024)S(1)} %bitcast.785, f32[512]{0:T(512)S(1)} %copy-done.209, f32[1024]{0:T(1024)} %bitcast.814, f32[512]{0:T(512)S(1)} %copy-done.211, f32[1024]{0:T(1024)} %bitcast.813, ...), kind=kLoop, calls=%fused_computation.286 | loop fusion | flops 51904512 | bytes 7532544 | tf_op jit(solution)/shard_map/convert.116
  362.2 14.3 %fusion.132 = bf16[1024,1,8,64]{0,3,2,1:T(8,128)(2,1)} fusion(bf16[1024,8,64]{0,2,1:T(8,128)(2,1)S(1)} %bitcast.639, f32[8,1024,1024]{1,2,0:T(8,128)} %get-tuple-element.362, f32[8,1024]{1,0:T(8,128)S(1)} %log_add_fusion), kind=kOutput, calls=%fused_computation.329 | convolution fusion | flops 1090519040 | bytes 35684352 | tf_op jit(solution)/shard_map/hqk,qhd->khd/dot_general | solution.py:429
  376.5 23.0 %multiply_reduce_fusion = (f32[8,1024]{1,0:T(8,128)S(1)}, f32[8,1024,1024]{1,2,0:T(8,128)}) fusion(f32[8,1024,1024]{1,2,0:T(8,128)} %get-tuple-element.362, f32[8,1024]{1,0:T(8,128)S(1)} %log_add_fusion, bf16[1024,8,64]{0,2,1:T(8,128)(2,1)S(1)} %bitcast.640, f32[1024,3,8,64]{0,3,2,1:T(8,128)} %copy-done.36), kind=kOutput, calls=%fused_computation.1 | convolution fusion | flops 1098899456 | bytes 69271552 | tf_op jit(solution)/shard_map/qhd,khd->hqk/dot_general | solution.py:432
  399.5 28.1 %multiply_convert_fusion = bf16[8,1024,1024]{1,2,0:T(8,128)(2,1)} fusion(f32[8,1024,1024]{1,2,0:T(8,128)} %get-tuple-element.373, f32[8,1024,1024]{1,2,0:T(8,128)} %get-tuple-element.362, f32[8,1024]{1,0:T(8,128)S(1)} %get-tuple-element.372, f32[8,1024]{1,0:T(8,128)S(1)} %log_add_fusion), kind=kLoop, calls=%fused_computation | loop fusion | flops 33554432 | bytes 83951616 | tf_op jit(solution)/shard_map/convert_element_type | solution.py:433
  427.6 11.3 %multiply_bitcast_fusion = f32[1024,8,64]{0,2,1:T(8,128)S(1)} fusion(bf16[8,1024,1024]{1,2,0:T(8,128)(2,1)} %multiply_convert_fusion, bf16[1024,8,32]{0,2,1:T(8,128)(2,1)} %copy-done.61, bf16[1024,8,32]{0,2,1:T(8,128)(2,1)} %copy-done.60), kind=kOutput, calls=%fused_computation.281 | convolution fusion | flops 1076363264 | bytes 19922944 | tf_op jit(solution)/shard_map/hqk,qhd->khd/dot_general | solution.py:441
  439.0 9.0 %multiply_bitcast_fusion.1 = f32[1024,8,64]{0,2,1:T(8,128)S(1)} fusion(bf16[8,1024,1024]{1,2,0:T(8,128)(2,1)} %multiply_convert_fusion, bf16[1024,8,32]{0,2,1:T(8,128)(2,1)S(1)} %copy-done.58, bf16[1024,8,32]{0,2,1:T(8,128)(2,1)} %copy-done.59), kind=kOutput, calls=%fused_computation.282 | convolution fusion | flops 1076363264 | bytes 19922944 | tf_op jit(solution)/shard_map/hqk,khd->qhd/dot_general | solution.py:437
  465.7 3.7 convolution_convert_fusion
  470.3 4.0 multiply_convert_fusion.1
  474.4 3.7 fusion.293
  478.1 3.8 convolution_convert_fusion.3
  501.8 4.5 reshape.860
  518.0 8.3 %collective-permute-done.45 = bf16[1,384,512]{2,1,0:T(8,128)(2,1)S(1)} collective-permute-done((bf16[1,384,512]{2,1,0:T(8,128)(2,1)S(1)}, bf16[1,384,512]{2,1,0:T(8,128)(2,1)S(1)}, u32[]{:S(2)}, u32[]{:S(2)}) %collective-permute-start.45) | collective-permute-done | bytes 393248 | tf_op jit(solution)/shard_map/ppermute | solution.py:184
  528.7 3.4 collective-permute-done.46
  533.5 3.4 collective-permute-done.47
  538.1 5.1 collective-permute-done.48
  544.0 4.3 collective-permute-done.49
  551.0 8.6 %collective-permute-done.13 = bf16[1,528,512]{2,1,0:T(8,128)(2,1)S(1)} collective-permute-done((bf16[1,528,512]{2,1,0:T(8,128)(2,1)S(1)}, bf16[1,528,512]{2,1,0:T(8,128)(2,1)S(1)}, u32[]{:S(2)}, u32[]{:S(2)}) %collective-permute-start.13) | collective-permute-done | bytes 540704 | tf_op jit(solution)/shard_map/ppermute | solution.py:184
  584.2 3.4 collective-permute-done.32
  622.1 5.7 collective-permute-done.22
  631.1 4.4 collective-permute-done.23
  638.3 4.5 collective-permute-done.24
  644.3 4.6 collective-permute-done.25
  651.1 4.3 collective-permute-done.26
  655.6 4.3 collective-permute-start.27
  661.3 5.8 collective-permute-done.27
  669.6 6.5 multiply_subtract_fusion.1
  676.1 3.9 multiply_subtract_fusion
  (1026 shorter events, 309.6 us)
Async XLA Ops:
  2.2 59.1 %collective-permute-start = (bf16[1,44,128]{2,1,0:T(8,128)(2,1)S(1)}, bf16[1,44,128]{2,1,0:T(8,128)(2,1)}, u32[]{:S(2)}, u32[]{:S(2)}) collective-permute-start(bf16[1,44,128]{2,1,0:T(8,128)(2,1)S(1)} %maximum_bitcast_fusion.5), channel_id=1, source_target_pairs={{0,2},{1,3},{2,0},{3,1},{4,6},{5,7},{6,4},{7,5},{8,10},{9,11},{10,... | collective-permute-start | bytes 33800 | tf_op jit(solution)/shard_map/ppermute | solution.py:184
  8.4 59.1 %collective-permute-start.8 = (bf16[1,384,512]{2,1,0:T(8,128)(2,1)}, bf16[1,384,512]{2,1,0:T(8,128)(2,1)}, u32[]{:S(2)}, u32[]{:S(2)}) collective-permute-start(bf16[1,384,512]{2,1,0:T(8,128)(2,1)} %maximum_bitcast_fusion.4), channel_id=1, source_target_pairs={{0,2},{1,3},{2,0},{3,1},{4,6},{5,7},{6,4},{7,5},{8,10},{9,11},{10,... | collective-permute-start | bytes 1179656 | tf_op jit(solution)/shard_map/ppermute | solution.py:184
  12.9 58.2 %collective-permute-start.6 = (bf16[1,512,512]{2,1,0:T(8,128)(2,1)}, bf16[1,512,512]{2,1,0:T(8,128)(2,1)}, u32[]{:S(2)}, u32[]{:S(2)}) collective-permute-start(bf16[1,512,512]{2,1,0:T(8,128)(2,1)} %maximum_bitcast_fusion.3), channel_id=1, source_target_pairs={{0,2},{1,3},{2,0},{3,1},{4,6},{5,7},{6,4},{7,5},{8,10},{9,11},{10,... | collective-permute-start | bytes 1572872 | tf_op jit(solution)/shard_map/ppermute | solution.py:184
  18.4 55.9 %collective-permute-start.2 = (bf16[1,512,512]{2,1,0:T(8,128)(2,1)}, bf16[1,512,512]{2,1,0:T(8,128)(2,1)}, u32[]{:S(2)}, u32[]{:S(2)}) collective-permute-start(bf16[1,512,512]{2,1,0:T(8,128)(2,1)} %bitcast.5), channel_id=1, source_target_pairs={{0,2},{1,3},{2,0},{3,1},{4,6},{5,7},{6,4},{7,5},{8,10},{9,11},{10,... | collective-permute-start | bytes 1572872 | tf_op jit(solution)/shard_map/ppermute | solution.py:184
  21.2 51.3 %collective-permute-start.4 = (bf16[1,512,512]{2,1,0:T(8,128)(2,1)}, bf16[1,512,512]{2,1,0:T(8,128)(2,1)}, u32[]{:S(2)}, u32[]{:S(2)}) collective-permute-start(bf16[1,512,512]{2,1,0:T(8,128)(2,1)} %get-tuple-element.266), channel_id=1, source_target_pairs={{0,2},{1,3},{2,0},{3,1},{4,6},{5,7},{6,4},{7,5},{8,10},{9,11},{10,... | collective-permute-start | bytes 1572872 | tf_op jit(solution)/shard_map/ppermute | solution.py:184
  64.9 25.9 %collective-permute-start.10 = (bf16[1,1024,512]{2,1,0:T(8,128)(2,1)}, bf16[1,1024,512]{2,1,0:T(8,128)(2,1)}, u32[]{:S(2)}, u32[]{:S(2)}) collective-permute-start(bf16[1,1024,512]{2,1,0:T(8,128)(2,1)} %maximum_bitcast_fusion.2), channel_id=1, source_target_pairs={{0,2},{1,3},{2,0},{3,1},{4,6},{5,7},{6,4},{7,5},{8,10},{9,11},{10,... | collective-permute-start | bytes 3145736 | tf_op jit(solution)/shard_map/ppermute | solution.py:184
  68.7 24.9 %collective-permute-start.9 = (bf16[2,384,512]{2,1,0:T(8,128)(2,1)S(1)}, bf16[2,384,512]{2,1,0:T(8,128)(2,1)S(1)}, u32[]{:S(2)}, u32[]{:S(2)}) collective-permute-start(bf16[2,384,512]{2,1,0:T(8,128)(2,1)S(1)} %pad_maximum_fusion.11), channel_id=1, source_target_pairs={{0,1},{1,0},{2,3},{3,2},{4,5},{5,4},{6,7},{7,6},{8,9},{9,8},{10,11... | collective-permute-start | bytes 2359304 | tf_op jit(solution)/shard_map/ppermute | solution.py:184
  72.4 26.4 %collective-permute-start.7 = (bf16[2,512,512]{2,1,0:T(8,128)(2,1)S(1)}, bf16[2,512,512]{2,1,0:T(8,128)(2,1)S(1)}, u32[]{:S(2)}, u32[]{:S(2)}) collective-permute-start(bf16[2,512,512]{2,1,0:T(8,128)(2,1)S(1)} %pad_maximum_fusion.6), channel_id=1, source_target_pairs={{0,1},{1,0},{2,3},{3,2},{4,5},{5,4},{6,7},{7,6},{8,9},{9,8},{10,11... | collective-permute-start | bytes 3145736 | tf_op jit(solution)/shard_map/ppermute | solution.py:184
  73.9 24.9 %collective-permute-start.5 = (bf16[2,512,512]{2,1,0:T(8,128)(2,1)S(1)}, bf16[2,512,512]{2,1,0:T(8,128)(2,1)S(1)}, u32[]{:S(2)}, u32[]{:S(2)}) collective-permute-start(bf16[2,512,512]{2,1,0:T(8,128)(2,1)S(1)} %pad_maximum_fusion.5), channel_id=1, source_target_pairs={{0,1},{1,0},{2,3},{3,2},{4,5},{5,4},{6,7},{7,6},{8,9},{9,8},{10,11... | collective-permute-start | bytes 3145736 | tf_op jit(solution)/shard_map/ppermute | solution.py:184
  75.7 26.2 %collective-permute-start.3 = (bf16[2,512,512]{2,1,0:T(8,128)(2,1)S(1)}, bf16[2,512,512]{2,1,0:T(8,128)(2,1)S(1)}, u32[]{:S(2)}, u32[]{:S(2)}) collective-permute-start(bf16[2,512,512]{2,1,0:T(8,128)(2,1)S(1)} %pad_maximum_fusion.4), channel_id=1, source_target_pairs={{0,1},{1,0},{2,3},{3,2},{4,5},{5,4},{6,7},{7,6},{8,9},{9,8},{10,11... | collective-permute-start | bytes 3145736 | tf_op jit(solution)/shard_map/ppermute | solution.py:184
  93.6 125.3 %collective-permute-start.11 = (bf16[2,1024,512]{2,1,0:T(8,128)(2,1)}, bf16[2,1024,512]{2,1,0:T(8,128)(2,1)}, u32[]{:S(2)}, u32[]{:S(2)}) collective-permute-start(bf16[2,1024,512]{2,1,0:T(8,128)(2,1)} %pad_maximum_fusion), channel_id=1, source_target_pairs={{0,1},{1,0},{2,3},{3,2},{4,5},{5,4},{6,7},{7,6},{8,9},{9,8},{10,11... | collective-permute-start | bytes 6291464 | tf_op jit(solution)/shard_map/ppermute | solution.py:184
  198.9 16.1 %all-to-all-start = ((f32[32,3,512]{2,1,0:T(4,128)}), f32[32,3,512]{2,1,0:T(4,128)S(1)}, u32[]{:S(2)}, u32[]{:S(2)}) async-start(f32[32,3,512]{2,1,0:T(4,128)} %broadcast_in_dim.271), calls=%async_computation | async-start | bytes 524288 | tf_op jit(solution)/shard_map/all_to_all | solution.py:233
  283.3 14.1 %all-to-all-start.1 = ((f32[32,2,512]{2,1,0:T(2,128)}), f32[32,2,512]{2,1,0:T(2,128)S(1)}, u32[]{:S(2)}, u32[]{:S(2)}) async-start(f32[32,2,512]{2,1,0:T(2,128)} %broadcast_in_dim.274), calls=%async_computation.1 | async-start | bytes 262144 | tf_op jit(solution)/shard_map/all_to_all | solution.py:233
  292.3 272.7 %collective-permute-start.20 = (bf16[2,1024,512]{2,1,0:T(8,128)(2,1)}, bf16[2,1024,512]{2,1,0:T(8,128)(2,1)}, u32[]{:S(2)}, u32[]{:S(2)}) collective-permute-start(bf16[2,1024,512]{2,1,0:T(8,128)(2,1)} %fusion.121), channel_id=1, source_target_pairs={{0,1},{1,0},{2,3},{3,2},{4,5},{5,4},{6,7},{7,6},{8,9},{9,8},{10,11... | collective-permute-start | bytes 6291464 | tf_op jit(solution)/shard_map/ppermute | solution.py:184
  485.9 26.1 %collective-permute-start.44 = (bf16[2,384,512]{2,1,0:T(8,128)(2,1)}, bf16[2,384,512]{2,1,0:T(8,128)(2,1)}, u32[]{:S(2)}, u32[]{:S(2)}) collective-permute-start(bf16[2,384,512]{2,1,0:T(8,128)(2,1)} %fusion.152), channel_id=1, source_target_pairs={{0,1},{1,0},{2,3},{3,2},{4,5},{5,4},{6,7},{7,6},{8,9},{9,8},{10,11... | collective-permute-start | bytes 2359304 | tf_op jit(solution)/shard_map/ppermute | solution.py:184
  493.5 21.2 %collective-permute-start.36 = (bf16[2,512,512]{2,1,0:T(8,128)(2,1)}, bf16[2,512,512]{2,1,0:T(8,128)(2,1)}, u32[]{:S(2)}, u32[]{:S(2)}) collective-permute-start(bf16[2,512,512]{2,1,0:T(8,128)(2,1)} %fusion.144), channel_id=1, source_target_pairs={{0,1},{1,0},{2,3},{3,2},{4,5},{5,4},{6,7},{7,6},{8,9},{9,8},{10,11... | collective-permute-start | bytes 3145736 | tf_op jit(solution)/shard_map/ppermute | solution.py:184
  496.0 31.2 %collective-permute-start.28 = (bf16[2,512,512]{2,1,0:T(8,128)(2,1)}, bf16[2,512,512]{2,1,0:T(8,128)(2,1)}, u32[]{:S(2)}, u32[]{:S(2)}) collective-permute-start(bf16[2,512,512]{2,1,0:T(8,128)(2,1)} %dynamic-slice_bitcast_fusion), channel_id=1, source_target_pairs={{0,1},{1,0},{2,3},{3,2},{4,5},{5,4},{6,7},{7,6},{8,9},{9,8},{10,11... | collective-permute-start | bytes 3145736 | tf_op jit(solution)/shard_map/ppermute | solution.py:184
  511.7 26.1 %collective-permute-start.12 = (bf16[2,528,512]{2,1,0:T(8,128)(2,1)S(1)}, bf16[2,528,512]{2,1,0:T(8,128)(2,1)S(1)}, u32[]{:S(2)}, u32[]{:S(2)}) collective-permute-start(bf16[2,528,512]{2,1,0:T(8,128)(2,1)S(1)} %fusion.139), channel_id=1, source_target_pairs={{0,1},{1,0},{2,3},{3,2},{4,5},{5,4},{6,7},{7,6},{8,9},{9,8},{10,11... | collective-permute-start | bytes 3244040 | tf_op jit(solution)/shard_map/ppermute | solution.py:184
  514.2 12.0 %collective-permute-start.45 = (bf16[1,384,512]{2,1,0:T(8,128)(2,1)S(1)}, bf16[1,384,512]{2,1,0:T(8,128)(2,1)S(1)}, u32[]{:S(2)}, u32[]{:S(2)}) collective-permute-start(bf16[1,384,512]{2,1,0:T(8,128)(2,1)S(1)} %constant_dynamic-slice_fusion), channel_id=1, source_target_pairs={{0,2},{1,3},{2,0},{3,1},{4,6},{5,7},{6,4},{7,5},{8,10},{9,11},{10,... | collective-permute-start | bytes 1179656 | tf_op jit(solution)/shard_map/ppermute | solution.py:184
  516.4 32.0 %collective-permute-start.37 = (bf16[1,512,512]{2,1,0:T(8,128)(2,1)S(1)}, bf16[1,512,512]{2,1,0:T(8,128)(2,1)S(1)}, u32[]{:S(2)}, u32[]{:S(2)}) collective-permute-start(bf16[1,512,512]{2,1,0:T(8,128)(2,1)S(1)} %constant_dynamic-slice_fusion.1), channel_id=1, source_target_pairs={{0,2},{1,3},{2,0},{3,1},{4,6},{5,7},{6,4},{7,5},{8,10},{9,11},{10,... | collective-permute-start | bytes 1572872 | tf_op jit(solution)/shard_map/ppermute | solution.py:184
  533.0 16.3 %collective-permute-start.29 = (bf16[1,512,512]{2,1,0:T(8,128)(2,1)S(1)}, bf16[1,512,512]{2,1,0:T(8,128)(2,1)S(1)}, u32[]{:S(2)}, u32[]{:S(2)}) collective-permute-start(bf16[1,512,512]{2,1,0:T(8,128)(2,1)S(1)} %constant_dynamic-slice_fusion.2), channel_id=1, source_target_pairs={{0,2},{1,3},{2,0},{3,1},{4,6},{5,7},{6,4},{7,5},{8,10},{9,11},{10,... | collective-permute-start | bytes 1572872 | tf_op jit(solution)/shard_map/ppermute | solution.py:184
  537.0 6.3 collective-permute-start.48
  543.5 16.1 %collective-permute-start.13 = (bf16[1,528,512]{2,1,0:T(8,128)(2,1)S(1)}, bf16[1,528,512]{2,1,0:T(8,128)(2,1)S(1)}, u32[]{:S(2)}, u32[]{:S(2)}) collective-permute-start(bf16[1,528,512]{2,1,0:T(8,128)(2,1)S(1)} %constant_dynamic-slice_fusion.4), channel_id=1, source_target_pairs={{0,2},{1,3},{2,0},{3,1},{4,6},{5,7},{6,4},{7,5},{8,10},{9,11},{10,... | collective-permute-start | bytes 1622024 | tf_op jit(solution)/shard_map/ppermute | solution.py:184
  548.4 12.0 %collective-permute-start.50 = (bf16[96,512]{1,0:T(8,128)(2,1)S(1)}, bf16[96,512]{1,0:T(8,128)(2,1)S(1)}, u32[]{:S(2)}, u32[]{:S(2)}) collective-permute-start(bf16[96,512]{1,0:T(8,128)(2,1)S(1)} %bitcast.740), channel_id=1, source_target_pairs={{0,8},{4,12},{8,0},{12,4},{16,24},{20,28},{24,16},{28,20},{1,9},{5... | collective-permute-start | bytes 294920 | tf_op jit(solution)/shard_map/ppermute | solution.py:184
  548.6 13.5 %collective-permute-start.38 = (bf16[256,512]{1,0:T(8,128)(2,1)S(1)}, bf16[256,512]{1,0:T(8,128)(2,1)S(1)}, u32[]{:S(2)}, u32[]{:S(2)}) collective-permute-start(bf16[256,512]{1,0:T(8,128)(2,1)S(1)} %dynamic-slice_bitcast_fusion.3), channel_id=1, source_target_pairs={{0,4},{4,0},{8,12},{12,8},{16,20},{20,16},{24,28},{28,24},{1,5},{5... | collective-permute-start | bytes 786440 | tf_op jit(solution)/shard_map/ppermute | solution.py:184
  549.5 13.2 %collective-permute-start.30 = (bf16[256,512]{1,0:T(8,128)(2,1)S(1)}, bf16[256,512]{1,0:T(8,128)(2,1)S(1)}, u32[]{:S(2)}, u32[]{:S(2)}) collective-permute-start(bf16[256,512]{1,0:T(8,128)(2,1)S(1)} %dynamic-slice_bitcast_fusion.4), channel_id=1, source_target_pairs={{0,4},{4,0},{8,12},{12,8},{16,20},{20,16},{24,28},{28,24},{1,5},{5... | collective-permute-start | bytes 786440 | tf_op jit(solution)/shard_map/ppermute | solution.py:184
  559.8 14.7 %collective-permute-start.14 = (bf16[264,512]{1,0:T(8,128)(2,1)S(1)}, bf16[264,512]{1,0:T(8,128)(2,1)S(1)}, u32[]{:S(2)}, u32[]{:S(2)}) collective-permute-start(bf16[264,512]{1,0:T(8,128)(2,1)S(1)} %dynamic-slice_bitcast_fusion.2), channel_id=1, source_target_pairs={{0,4},{4,0},{8,12},{12,8},{16,20},{20,16},{24,28},{28,24},{1,5},{5... | collective-permute-start | bytes 811016 | tf_op jit(solution)/shard_map/ppermute | solution.py:184
  560.3 11.5 %collective-permute-start.51 = (bf16[192,512]{1,0:T(8,128)(2,1)S(1)}, bf16[192,512]{1,0:T(8,128)(2,1)S(1)}, u32[]{:S(2)}, u32[]{:S(2)}) collective-permute-start(bf16[192,512]{1,0:T(8,128)(2,1)S(1)} %bitcast.726), channel_id=1, source_target_pairs={{0,4},{4,0},{8,12},{12,8},{16,20},{20,16},{24,28},{28,24},{1,5},{5... | collective-permute-start | bytes 589832 | tf_op jit(solution)/shard_map/ppermute | solution.py:184
  562.1 12.8 %collective-permute-start.39 = (bf16[128,512]{1,0:T(8,128)(2,1)S(1)}, bf16[128,512]{1,0:T(8,128)(2,1)S(1)}, u32[]{:S(2)}, u32[]{:S(2)}) collective-permute-start(bf16[128,512]{1,0:T(8,128)(2,1)S(1)} %dynamic-slice_bitcast_fusion.8), channel_id=1, source_target_pairs={{0,8},{4,12},{8,0},{12,4},{16,24},{20,28},{24,16},{28,20},{1,9},{5... | collective-permute-start | bytes 393224 | tf_op jit(solution)/shard_map/ppermute | solution.py:184
  563.4 12.9 %collective-permute-start.31 = (bf16[128,512]{1,0:T(8,128)(2,1)}, bf16[128,512]{1,0:T(8,128)(2,1)}, u32[]{:S(2)}, u32[]{:S(2)}) collective-permute-start(bf16[128,512]{1,0:T(8,128)(2,1)} %dynamic-slice_bitcast_fusion.9), channel_id=1, source_target_pairs={{0,8},{4,12},{8,0},{12,4},{16,24},{20,28},{24,16},{28,20},{1,9},{5... | collective-permute-start | bytes 393224 | tf_op jit(solution)/shard_map/ppermute | solution.py:184
  568.3 42.9 %collective-permute-start.21 = (bf16[1,1024,512]{2,1,0:T(8,128)(2,1)}, bf16[1,1024,512]{2,1,0:T(8,128)(2,1)}, u32[]{:S(2)}, u32[]{:S(2)}) collective-permute-start(bf16[1,1024,512]{2,1,0:T(8,128)(2,1)} %constant_dynamic-slice_fusion.3), channel_id=1, source_target_pairs={{0,2},{1,3},{2,0},{3,1},{4,6},{5,7},{6,4},{7,5},{8,10},{9,11},{10,... | collective-permute-start | bytes 3145736 | tf_op jit(solution)/shard_map/ppermute | solution.py:184
  574.7 6.3 collective-permute-start.15
  575.0 9.0 %collective-permute-start.40 = (bf16[64,512]{1,0:T(8,128)(2,1)S(1)}, bf16[64,512]{1,0:T(8,128)(2,1)S(1)}, u32[]{:S(2)}, u32[]{:S(2)}) collective-permute-start(bf16[64,512]{1,0:T(8,128)(2,1)S(1)} %dynamic-slice_bitcast_fusion.13), channel_id=1, source_target_pairs={{0,16},{4,20},{8,24},{12,28},{16,0},{20,4},{24,8},{28,12},{1,17},{... | collective-permute-start | bytes 196616 | tf_op jit(solution)/shard_map/ppermute | solution.py:184
  577.3 10.3 %collective-permute-start.32 = (bf16[64,512]{1,0:T(8,128)(2,1)S(1)}, bf16[64,512]{1,0:T(8,128)(2,1)S(1)}, u32[]{:S(2)}, u32[]{:S(2)}) collective-permute-start(bf16[64,512]{1,0:T(8,128)(2,1)S(1)} %dynamic-slice_bitcast_fusion.14), channel_id=1, source_target_pairs={{0,16},{4,20},{8,24},{12,28},{16,0},{20,4},{24,8},{28,12},{1,17},{... | collective-permute-start | bytes 196616 | tf_op jit(solution)/shard_map/ppermute | solution.py:184
  581.1 8.1 %collective-permute-start.16 = (bf16[66,512]{1,0:T(8,128)(2,1)S(1)}, bf16[66,512]{1,0:T(8,128)(2,1)S(1)}, u32[]{:S(2)}, u32[]{:S(2)}) collective-permute-start(bf16[66,512]{1,0:T(8,128)(2,1)S(1)} %dynamic-slice_bitcast_fusion.12), channel_id=1, source_target_pairs={{0,16},{4,20},{8,24},{12,28},{16,0},{20,4},{24,8},{28,12},{1,17},{... | collective-permute-start | bytes 202760 | tf_op jit(solution)/shard_map/ppermute | solution.py:184
  584.1 8.1 %collective-permute-start.41 = (bf16[64,512]{1,0:T(8,128)(2,1)S(1)}, bf16[64,512]{1,0:T(8,128)(2,1)S(1)}, u32[]{:S(2)}, u32[]{:S(2)}) collective-permute-start(bf16[64,512]{1,0:T(8,128)(2,1)S(1)} %get-tuple-element.226), channel_id=1, source_target_pairs={{0,16},{4,20},{8,24},{12,28},{16,0},{20,4},{24,8},{28,12},{1,17},{... | collective-permute-start | bytes 196616 | tf_op jit(solution)/shard_map/ppermute | solution.py:184
  589.3 6.5 collective-permute-start.17
  592.1 6.5 collective-permute-start.42
  593.6 7.9 %collective-permute-start.34 = (bf16[128,512]{1,0:T(8,128)(2,1)S(1)}, bf16[128,512]{1,0:T(8,128)(2,1)}, u32[]{:S(2)}, u32[]{:S(2)}) collective-permute-start(bf16[128,512]{1,0:T(8,128)(2,1)S(1)} %bitcast.738), channel_id=1, source_target_pairs={{0,8},{4,12},{8,0},{12,4},{16,24},{20,28},{24,16},{28,20},{1,9},{5... | collective-permute-start | bytes 393224 | tf_op jit(solution)/shard_map/ppermute | solution.py:184
  595.8 10.1 %collective-permute-start.18 = (bf16[132,512]{1,0:T(8,128)(2,1)S(1)}, bf16[132,512]{1,0:T(8,128)(2,1)S(1)}, u32[]{:S(2)}, u32[]{:S(2)}) collective-permute-start(bf16[132,512]{1,0:T(8,128)(2,1)S(1)} %reshape.864), channel_id=1, source_target_pairs={{0,8},{4,12},{8,0},{12,4},{16,24},{20,28},{24,16},{28,20},{1,9},{5... | collective-permute-start | bytes 405512 | tf_op jit(solution)/shard_map/ppermute | solution.py:184
  598.7 9.4 %collective-permute-start.43 = (bf16[256,512]{1,0:T(8,128)(2,1)S(1)}, bf16[256,512]{1,0:T(8,128)(2,1)}, u32[]{:S(2)}, u32[]{:S(2)}) collective-permute-start(bf16[256,512]{1,0:T(8,128)(2,1)S(1)} %bitcast.716), channel_id=1, source_target_pairs={{0,4},{4,0},{8,12},{12,8},{16,20},{20,16},{24,28},{28,24},{1,5},{5... | collective-permute-start | bytes 786440 | tf_op jit(solution)/shard_map/ppermute | solution.py:184
  603.1 18.0 %collective-permute-start.35 = (bf16[256,512]{1,0:T(8,128)(2,1)}, bf16[256,512]{1,0:T(8,128)(2,1)}, u32[]{:S(2)}, u32[]{:S(2)}) collective-permute-start(bf16[256,512]{1,0:T(8,128)(2,1)} %bitcast.270), channel_id=1, source_target_pairs={{0,4},{4,0},{8,12},{12,8},{16,20},{20,16},{24,28},{28,24},{1,5},{5... | collective-permute-start | bytes 786440 | tf_op jit(solution)/shard_map/ppermute | solution.py:184
  606.7 30.5 %collective-permute-start.19 = (bf16[264,512]{1,0:T(8,128)(2,1)}, bf16[264,512]{1,0:T(8,128)(2,1)}, u32[]{:S(2)}, u32[]{:S(2)}) collective-permute-start(bf16[264,512]{1,0:T(8,128)(2,1)} %reshape.865), channel_id=1, source_target_pairs={{0,4},{4,0},{8,12},{12,8},{16,20},{20,16},{24,28},{28,24},{1,5},{5... | collective-permute-start | bytes 811016 | tf_op jit(solution)/shard_map/ppermute | solution.py:184
  613.8 14.1 %collective-permute-start.22 = (bf16[512,512]{1,0:T(8,128)(2,1)}, bf16[512,512]{1,0:T(8,128)(2,1)}, u32[]{:S(2)}, u32[]{:S(2)}) collective-permute-start(bf16[512,512]{1,0:T(8,128)(2,1)} %dynamic-slice_bitcast_fusion.1), channel_id=1, source_target_pairs={{0,4},{4,0},{8,12},{12,8},{16,20},{20,16},{24,28},{28,24},{1,5},{5... | collective-permute-start | bytes 1572872 | tf_op jit(solution)/shard_map/ppermute | solution.py:184
  629.1 6.4 collective-permute-start.23
  635.6 7.2 %collective-permute-start.24 = (bf16[128,512]{1,0:T(8,128)(2,1)S(1)}, bf16[128,512]{1,0:T(8,128)(2,1)S(1)}, u32[]{:S(2)}, u32[]{:S(2)}) collective-permute-start(bf16[128,512]{1,0:T(8,128)(2,1)S(1)} %dynamic-slice_bitcast_fusion.10), channel_id=1, source_target_pairs={{0,16},{4,20},{8,24},{12,28},{16,0},{20,4},{24,8},{28,12},{1,17},{... | collective-permute-start | bytes 393224 | tf_op jit(solution)/shard_map/ppermute | solution.py:184
  648.9 6.5 collective-permute-start.26
  655.6 11.5 %collective-permute-start.27 = (bf16[512,512]{1,0:T(8,128)(2,1)S(1)}, bf16[512,512]{1,0:T(8,128)(2,1)S(1)}, u32[]{:S(2)}, u32[]{:S(2)}) collective-permute-start(bf16[512,512]{1,0:T(8,128)(2,1)S(1)} %bitcast.697), channel_id=1, source_target_pairs={{0,4},{4,0},{8,12},{12,8},{16,20},{20,16},{24,28},{28,24},{1,5},{5... | collective-permute-start | bytes 1572872 | tf_op jit(solution)/shard_map/ppermute | solution.py:184
  (288 other events, 2877.2 us)

commit v2 on v0

v2 whole, which is shorter than its diff:
```python
import functools
import math

import jax
import jax.numpy as jnp
from jax import lax
from jax.experimental import pallas as pl
from jax.experimental.pallas import tpu as pltpu
from jax.sharding import PartitionSpec as P

HEADS = 8
STEP = 10
TAPS = 32
GAP = 16
LIMIT = 50 * 1024 * 1024
TILE = 256
WINDOWS = (512, 768)

norm_epsilon = 1e-05
batch_epsilon = 1e-05
masked_score = -1000000000.0
learn_rate = 0.1
beta_first = 0.9
beta_second = 0.98
adam_epsilon = 1e-08
decay_rate = 0.01

f32, bf16 = jnp.float32, jnp.bfloat16


def mm(a, b):
    return jnp.dot(a, b, preferred_element_type=f32)


def mm_nt(a, b):
    return lax.dot_general(a, b, (((1,), (1,)), ((), ())), preferred_element_type=f32)


def mm_tn(a, b):
    return lax.dot_general(a, b, (((0,), (0,)), ((), ())), preferred_element_type=f32)


def normalize(value):
    center = value - jnp.mean(value, axis=-1, keepdims=True)
    scale = lax.rsqrt(jnp.mean(center * center, axis=-1, keepdims=True) + norm_epsilon)
    return center * scale, scale


def norm_back(grad_out, gain, normed, scale):
    grad_norm = grad_out * gain
    return scale * (
        grad_norm
        - jnp.mean(grad_norm, axis=-1, keepdims=True)
        - normed * jnp.mean(grad_norm * normed, axis=-1, keepdims=True)
    )


def col_sum(value):
    return jnp.sum(value, axis=0, keepdims=True)


def sigmoid(value):
    return 0.5 * jnp.tanh(0.5 * value) + 0.5


def slope_of(value, sigma):
    return sigma * (1.0 + value * (1.0 - sigma))


def seg_of(places, ends):
    s = (places >= ends[0]).astype(jnp.int32)
    for j in range(1, 4):
        s = s + (places >= ends[j]).astype(jnp.int32)
    return s


def pick_last(values, count):
    out = values[0]
    for j in range(1, len(values)):
        out = jnp.where(count >= j, values[j], out)
    return out


def key_range(first, last, ends, rows):
    starts = [jnp.int32(0)] + ends
    stops = ends + [jnp.int32(rows)]
    return pick_last(starts, seg_of(first, ends)), pick_last(stops, seg_of(last, ends))


def in_window(lo, hi, rows, body):
    begin = (lo // 128) * 128
    done = jnp.bool_(False)
    for w in sorted({w for w in WINDOWS if w < rows} | {rows}):
        start = jnp.minimum(begin, rows - w)
        fits = jnp.logical_and(hi <= start + w, jnp.logical_not(done))

        @pl.when(fits)
        def _(start=start, w=w):
            body(pl.multiple_of(start, 128), w)

        done = jnp.logical_or(done, fits)


def partner(x):
    lane = lax.broadcasted_iota(jnp.int32, (1, 128), 1)
    return jnp.where((lane & 32) == 0, pltpu.roll(x, 96, 1), pltpu.roll(x, 32, 1))


def load_once(t, copies, sems):
    @pl.when(t == 0)
    def _():
        made = [pltpu.make_async_copy(s, d, sems.at[k]) for k, (s, d) in enumerate(copies)]
        for copy in made:
            copy.start()
        for copy in made:
            copy.wait()


def column_blocks(piece, owner, dst, rows, base=0):
    return [
        (
            piece.at[base + rows * j : base + rows * (j + 1), :],
            dst.at[pl.ds(owner * rows, rows), 512 * j : 512 * (j + 1)],
        )
        for j in range(dst.shape[1] // 512)
    ]


def row_block(piece, owner, dst, rows, base=0):
    return [(piece.at[base : base + rows, :], dst.at[pl.ds(owner * rows, rows), :])]


def row_spec(width):
    return "row"


def whole(*shape):
    return "whole"


def anywhere(count):
    return ["any"] * count


def out_shape(*shape, dtype=f32):
    return jax.ShapeDtypeStruct(shape, dtype)


def view(ref, kind, t):
    if kind == "row":
        return ref.at[pl.ds(pl.multiple_of(t * TILE, TILE), TILE), :]
    if kind == "col":
        return ref.at[:, pl.ds(pl.multiple_of(t * TILE, TILE), TILE)]
    if isinstance(kind, tuple):
        width = kind[1]
        return ref.at[:, pl.ds(pl.multiple_of(t * width, width), width)]
    return ref


def block_of(kind, shape, index=None):
    if kind == "any":
        return pl.BlockSpec(memory_space=pl.ANY)
    if kind == "row":
        return pl.BlockSpec((TILE, shape[1]), lambda i, *_: (i, 0))
    if kind == "col":
        return pl.BlockSpec((shape[0], TILE), lambda i, *_: (0, i))
    if isinstance(kind, tuple) and kind[0] == "lane":
        return pl.BlockSpec((shape[0], kind[1]), lambda i, *_: (0, i))
    if isinstance(kind, tuple):
        return pl.BlockSpec((None,) + shape[1:], lambda i, *_: (kind[1],) + (0,) * (len(shape) - 1))
    return pl.BlockSpec(shape, lambda i, *_: (0,) * len(shape))


def run(
    body, name, scalars, inputs, in_specs, out_specs, outs, scratch, grid, flops, count=0, piped=False
):
    size = sum(math.prod(o.shape) * o.dtype.itemsize for o in outs)
    size += sum(math.prod(o.shape) * o.dtype.itemsize for o in inputs)
    lead = len(scalars)
    cost = pl.CostEstimate(flops=int(flops), bytes_accessed=int(size), transcendentals=int(count))
    params = pltpu.CompilerParams(vmem_limit_bytes=LIMIT)
    if piped:
        return pl.pallas_call(
            lambda *refs: body(pl.program_id(0), *refs),
            grid_spec=pltpu.PrefetchScalarGridSpec(
                num_scalar_prefetch=lead,
                grid=grid,
                in_specs=[block_of(k, v.shape) for k, v in zip(in_specs, inputs)],
                out_specs=[block_of(k, v.shape) for k, v in zip(out_specs, outs)],
                scratch_shapes=scratch,
            ),
            out_shape=outs,
            cost_estimate=cost,
            compiler_params=params,
            name=name,
        )(*scalars, *inputs)
    kinds = list(in_specs) + list(out_specs)

    def kernel(*refs):
        held = refs[lead : lead + len(kinds)]
        rest = refs[lead + len(kinds) :]

        def step(t, carry):
            views = [view(ref, kind, t) for ref, kind in zip(held, kinds)]
            body(t, *refs[:lead], *views, *rest)
            return carry

        if grid[0] == 1:
            step(0, 0)
        else:
            lax.fori_loop(0, grid[0], step, 0)

    vmem = pl.BlockSpec(memory_space=pltpu.VMEM)
    place = lambda kind: pl.BlockSpec(memory_space=pl.ANY) if kind == "any" else vmem
    return pl.pallas_call(
        kernel,
        in_specs=[pl.BlockSpec(memory_space=pltpu.SMEM)] * lead + [place(k) for k in in_specs],
        out_specs=[vmem] * len(outs),
        out_shape=outs,
        scratch_shapes=scratch,
        cost_estimate=cost,
        compiler_params=params,
        name=name,
    )(*scalars, *inputs)


def ff_forward_body(t, me, x, norms, *refs, rel, er, sr):
    n = len(rel)
    parts = refs[:n]
    x1, hidden, before, active, w_in, w_out, sems = refs[n:]
    copies = []
    for k, r in enumerate(rel):
        copies += column_blocks(parts[k], me[0] ^ r, w_in, er)
        copies += row_block(parts[k], me[0] ^ r, w_out, sr, 4 * er)
    load_once(t, copies, sems)
    value = x[...].astype(f32)
    normed, _ = normalize(value)
    h = (normed * norms[0:1, :] + norms[1:2, :]).astype(bf16)
    hidden[...] = h
    total = None
    for j in range(w_in.shape[1] // 512):
        cols = slice(512 * j, 512 * (j + 1))
        a = mm(h, w_in[:, cols])
        s = (a * sigmoid(a)).astype(bf16)
        before[:, cols] = a.astype(bf16)
        active[:, cols] = s
        part = mm(s, w_out[cols, :])
        total = part if total is None else total + part
    x1[...] = value + 0.5 * total


def ff_forward(me, x, norms, parts, rel):
    rows, d = x.shape
    er, sr = d // len(rel), 4 * d // len(rel)
    ff = sr * len(rel)
    return run(
        functools.partial(ff_forward_body, rel=rel, er=er, sr=sr),
        "ff_forward",
        (me,),
        (x, norms, *parts),
        [row_spec(d), whole(*norms.shape)] + anywhere(len(rel)),
        [row_spec(d), row_spec(d), row_spec(ff), row_spec(ff)],
        [
            out_shape(rows, d),
            out_shape(rows, d, dtype=bf16),
            out_shape(rows, ff, dtype=bf16),
            out_shape(rows, ff, dtype=bf16),
        ],
        [pltpu.VMEM((d, ff), bf16), pltpu.VMEM((ff, d), bf16), pltpu.SemaphoreType.DMA((5 * len(rel),))],
        (rows // TILE,),
        4 * rows * d * ff,
        rows * ff,
        True,
    )


def qkv_body(t, me, x1, norms, cs, sn, *refs, rel, ar):
    n = len(rel)
    parts = refs[:n]
    hidden, q, k, v, kt, w, sems = refs[n:]
    copies = []
    for j, r in enumerate(rel):
        copies += column_blocks(parts[j], me[0] ^ r, w, ar)
    load_once(t, copies, sems)
    normed, _ = normalize(x1[...])
    h = (normed * norms[2:3, :] + norms[3:4, :]).astype(bf16)
    hidden[...] = h
    c, s = cs[...], sn[...]
    for p in range(4):
        cols = slice(128 * p, 128 * (p + 1))
        a = mm(h, w[:, 128 * p : 128 * (p + 1)])
        q[:, cols] = ((a * c + partner(a) * s).astype(bf16) * 0.125).astype(bf16)
        a = mm(h, w[:, 512 + 128 * p : 512 + 128 * (p + 1)])
        turned = (a * c + partner(a) * s).astype(bf16)
        k[:, cols] = turned
        kt[cols, :] = turned.T
    v[...] = mm(h, w[:, 1024:1536]).astype(bf16)


def qkv(me, x1, norms, cs, sn, parts, rel):
    rows, d = x1.shape
    ar = parts[0].shape[0] // 4
    half = lambda: out_shape(rows, d, dtype=bf16)
    return run(
        functools.partial(qkv_body, rel=rel, ar=ar),
        "query_key_value",
        (me,),
        (x1, norms, cs, sn, *parts),
        [row_spec(d), whole(*norms.shape), row_spec(128), row_spec(128)] + anywhere(len(rel)),
        [row_spec(d)] * 4 + ["col"],
        [half(), half(), half(), half(), out_shape(d, rows, dtype=bf16)],
        [pltpu.VMEM((d, 3 * d), bf16), pltpu.SemaphoreType.DMA((3 * len(rel),))],
        (rows // TILE,),
        6 * rows * d * d,
    )


def attention_body(t, ends, me, q, k, v, x1, *refs, rel, ar, rows):
    n = len(rel)
    parts = refs[:n]
    x2, mixed, lse, w, sems = refs[n:]
    copies = []
    for j, r in enumerate(rel):
        copies += row_block(parts[j], me[0] ^ r, w, ar, 3 * ar)
    load_once(t, copies, sems)
    e = [ends[j] for j in range(4)]
    first = t * TILE
    lo, hi = key_range(first, first + TILE - 1, e, rows)
    sq = seg_of(first + lax.broadcasted_iota(jnp.int32, (1, TILE), 1), e)
    low = lax.broadcasted_iota(jnp.int32, (1, 128), 1) < 64
    zero = jnp.zeros((), bf16)

    def body(start, w_keys):
        keys = pl.ds(start, w_keys)
        same = seg_of(start + lax.broadcasted_iota(jnp.int32, (w_keys, 1), 0), e) == sq
        for p in range(4):
            cols = slice(128 * p, 128 * (p + 1))
            qp, kp, vp = q[:, cols], k[keys, cols], v[keys, cols]
            both = None
            for h in range(2):
                head = 2 * p + h
                pick = low if h == 0 else jnp.logical_not(low)
                s = jnp.where(same, mm_nt(kp, jnp.where(pick, qp, zero)), masked_score)
                top = jnp.max(s, axis=0, keepdims=True)
                expo = jnp.exp(s - top)
                total = col_sum(expo)
                lse[head : head + 1, :] = top + jnp.log(total)
                prob = (expo * (1.0 / total)).astype(bf16)
                part = mm_tn(prob, jnp.where(pick, vp, zero))
                both = part if both is None else both + part
            mixed[:, cols] = both.astype(bf16)

    in_window(lo, hi, rows, body)
    x2[...] = x1[...] + mm(mixed[...], w[...])


def attention(ends, me, q, k, v, x1, parts, rel):
    rows, d = q.shape
    ar = parts[0].shape[0] // 4
    return run(
        functools.partial(attention_body, rel=rel, ar=ar, rows=rows),
        "attention_forward",
        (ends, me),
        (q, k, v, x1, *parts),
        [row_spec(d), whole(rows, d), whole(rows, d), row_spec(d)] + anywhere(len(rel)),
        [row_spec(d), row_spec(d), "col"],
        [out_shape(rows, d), out_shape(rows, d, dtype=bf16), out_shape(HEADS, rows)],
        [pltpu.VMEM((d, d), bf16), pltpu.SemaphoreType.DMA((len(rel),))],
        (rows // TILE,),
        16 * rows * rows * d // 4,
        HEADS * rows * rows,
    )


def attention_back_body(t, ends, q, k, kt, v, do, lse, delta, cs, sn, gp, dqt, *, rows, pairs, base):
    e = [ends[j] for j in range(4)]
    first = pl.multiple_of(t * TILE, TILE)
    lo, hi = key_range(first, first + TILE - 1, e, rows)
    sk = seg_of(first + lax.broadcasted_iota(jnp.int32, (TILE, 1), 0), e)
    low = lax.broadcasted_iota(jnp.int32, (1, 128), 1) < 64
    here = pl.ds(first, TILE)
    zero = jnp.zeros((), bf16)

    @pl.when(t == 0)
    def _():
        dqt[...] = jnp.zeros_like(dqt)

    def body(start, w):
        qs = pl.ds(start, w)
        same = sk == seg_of(start + lax.broadcasted_iota(jnp.int32, (1, w), 1), e)
        for p in range(pairs):
            cols = slice(128 * p, 128 * (p + 1))
            held = slice(128 * (base + p), 128 * (base + p + 1))
            qp, dop = q[qs, held], do[qs, held]
            kp, vp = k[here, held], v[here, held]
            gk, gv = None, None
            for h in range(2):
                head = 2 * p + h
                full = 2 * base + head
                pick = low if h == 0 else jnp.logical_not(low)
                qm, dom = jnp.where(pick, qp, zero), jnp.where(pick, dop, zero)
                hr = slice(64 * head, 64 * (head + 1))
                hk = slice(64 * full, 64 * (full + 1))
                expo = jnp.exp(mm_nt(kp, qm) - lse[full : full + 1, qs])
                prob = jnp.where(same, expo, 0.0)
                ds = (prob * (mm_nt(vp, dom) - delta[full : full + 1, qs])).astype(bf16)
                v_part = mm(prob.astype(bf16), dom)
                k_part = mm(ds, qm)
                dqt[hr, qs] += mm(kt[hk, here], ds)
                gv = v_part if gv is None else gv + v_part
                gk = k_part if gk is None else gk + k_part
            c, s = cs[here, :], sn[here, :]
            gp[here, 128 * (2 * pairs + p) : 128 * (2 * pairs + p + 1)] = gv.astype(bf16)
            turned = gk * c - partner(gk) * s
            gp[here, 128 * (pairs + p) : 128 * (pairs + p + 1)] = turned.astype(bf16)

    in_window(lo, hi, rows, body)

    @pl.when(t == rows // TILE - 1)
    def _():
        c, s = cs[...] * 0.125, sn[...] * 0.125
        for p in range(pairs):
            cols = slice(128 * p, 128 * (p + 1))
            g = dqt[cols, :].T
            gp[:, cols] = (g * c - partner(g) * s).astype(bf16)


def attention_back(ends, q, k, kt, v, do, lse, delta, cs, sn, base, pairs):
    rows, d = q.shape
    wide = 128 * pairs
    return run(
        functools.partial(attention_back_body, rows=rows, pairs=pairs, base=base),
        "attention_backward",
        (ends,),
        (q, k, kt, v, do, lse, delta, cs, sn),
        [whole(rows, d)] * 5
        + [whole(HEADS, rows)] * 2
        + [whole(rows, 128)] * 2,
        [whole(rows, 3 * wide)],
        [out_shape(rows, 3 * wide, dtype=bf16)],
        [pltpu.VMEM((wide, rows), f32)],
        (rows // TILE,),
        10 * rows * rows * d * pairs // 4,
        HEADS * rows * rows * pairs // 4,
    )[0]


def spaced_rows(rows):
    return rows + 6 * GAP


def group_segments(row, ends):
    return seg_of(row + lax.broadcasted_iota(jnp.int32, (8, 128), 0), ends)


def spread_all(groups, first, spans, ends, read, buf):
    def put(s, row, seg, values):
        at = pl.ds(pl.multiple_of(GAP + GAP * s + row, 8), 8)
        keep = seg == s
        for c in range(4):
            buf[c, at, :] = jnp.where(keep, values[c], 0.0)

    def one(g, carry):
        row = 8 * (first + g)
        seg = group_segments(row, ends)
        values = read(g)
        put(spans[0, first + g], row, seg, values)
        put(spans[1, first + g], row, seg, values)
        return carry

    lax.fori_loop(0, groups, one, 0, unroll=4)

    @pl.when(spans[2, 0] > 1)
    def _():
        def rest(g, carry):
            row = 8 * (first + g)
            seg = group_segments(row, ends)
            values = read(g)

            def fix(s, inner):
                put(s, row, seg, values)
                return inner

            return lax.fori_loop(spans[0, first + g] + 1, spans[1, first + g], fix, carry)

        lax.fori_loop(0, groups, rest, 0)


def collect_all(groups, first, spans, ends, buf, out):
    def one(g, carry):
        row = 8 * (first + g)
        seg = group_segments(row, ends)
        lo, hi = spans[0, first + g], spans[1, first + g]
        keep = seg == lo
        a = pl.ds(pl.multiple_of(GAP + GAP * lo + row, 8), 8)
        b = pl.ds(pl.multiple_of(GAP + GAP * hi + row, 8), 8)
        to = pl.ds(pl.multiple_of(8 * g, 8), 8)
        for c in range(4):
            out[to, 128 * c : 128 * (c + 1)] = jnp.where(keep, buf[c, a, :], buf[c, b, :])
        return carry

    lax.fori_loop(0, groups, one, 0, unroll=4)

    @pl.when(spans[2, 0] > 1)
    def _():
        def rest(g, carry):
            row = 8 * (first + g)
            seg = group_segments(row, ends)
            to = pl.ds(pl.multiple_of(8 * g, 8), 8)

            def fix(s, inner):
                a = pl.ds(pl.multiple_of(GAP + GAP * s + row, 8), 8)
                for c in range(4):
                    cols = slice(128 * c, 128 * (c + 1))
                    out[to, cols] = jnp.where(seg == s, buf[c, a, :], out[to, cols])
                return inner

            return lax.fori_loop(spans[0, first + g] + 1, spans[1, first + g], fix, carry)

        lax.fori_loop(0, groups, rest, 0)


CHUNK = 8


def slide(src, taps, dst, rows, shift, reverse):
    span = 8 * CHUNK

    def step(i, carry):
        c = i // ((rows + 4 * GAP) // span)
        base = pl.multiple_of((i - c * ((rows + 4 * GAP) // span)) * span, 8)
        acc = [jnp.zeros((8, 128), f32) for _ in range(CHUNK)]
        for b in range(8):
            loads = [
                src[c, pl.ds(base + (shift + b + 8 * m), 8), :] for m in range(CHUNK + 3)
            ]
            for a in range(4):
                j = 8 * a + b
                j = TAPS - 1 - j if reverse else j
                w = jnp.broadcast_to(taps[c, j : j + 1, :], (8, 128))
                for m in range(CHUNK):
                    acc[m] = acc[m] + w * loads[m + a]
        for m in range(CHUNK):
            dst[c, pl.ds(base + GAP + 8 * m, 8), :] = acc[m]
        return carry

    lax.fori_loop(0, 4 * ((rows + 4 * GAP) // span), step, 0)


def tap_sums(grad, src, out, rows):
    span = 8 * CHUNK

    def lanes(c, carry):
        def step(i, acc):
            acc = list(acc)
            base = pl.multiple_of(i * span, 8)
            g = [grad[c, pl.ds(base + GAP + 8 * m, 8), :] for m in range(CHUNK)]
            for b in range(8):
                loads = [src[c, pl.ds(base + (b + 8 * m), 8), :] for m in range(CHUNK + 3)]
                for a in range(4):
                    j = 8 * a + b
                    for m in range(CHUNK):
                        acc[j] = acc[j] + g[m] * loads[m + a]
            return tuple(acc)

        zeros = tuple(jnp.zeros((8, 128), f32) for _ in range(TAPS))
        acc = lax.fori_loop(0, (rows + 4 * GAP) // span, step, zeros)
        for j in range(TAPS):
            out[c, j : j + 1, :] = col_sum(acc[j])
        return carry

    lax.fori_loop(0, 4, lanes, 0)


def conv_front_body(t, ends, me, spans, x2, norms, taps, *refs, rel, ar, rows):
    n = len(rel)
    parts = refs[:n]
    hidden, gates_out, conv, spaced, stats, glu, answer, w, sems = refs[n:]
    copies = []
    for j, r in enumerate(rel):
        copies += column_blocks(parts[j], me[0] ^ r, w, ar)
    load_once(t, copies, sems)
    e = [ends[j] for j in range(4)]

    @pl.when(t == 0)
    def _():
        spaced[...] = jnp.zeros_like(spaced)

    normed, _ = normalize(x2[...])
    h = (normed * norms[4:5, :] + norms[5:6, :]).astype(bf16)
    hidden[...] = h
    half = mm(h, w[:, :512])
    gate = mm(h, w[:, 512:])
    gates_out[:, :512] = half.astype(bf16)
    gates_out[:, 512:] = gate.astype(bf16)
    glu[...] = half * sigmoid(gate)

    def read(g):
        at = pl.ds(pl.multiple_of(8 * g, 8), 8)
        return [glu[at, 128 * c : 128 * (c + 1)] for c in range(4)]

    spread_all(TILE // 8, t * (TILE // 8), spans, e, read, spaced)

    @pl.when(t == rows // TILE - 1)
    def _():
        slide(spaced, taps, answer, rows, 0, False)
        collect_all(rows // 8, 0, spans, e, answer, conv)
        keep = lax.broadcasted_iota(jnp.int32, (rows, 1), 0) < e[3]
        kept = jnp.where(keep, conv[...], 0.0)
        stats[0:1, :] = col_sum(kept)
        stats[1:2, :] = col_sum(kept * kept)
        stats[2:3, :] = jnp.full((1, 512), e[3], jnp.int32).astype(f32)


def conv_front(ends, me, spans, x2, norms, taps, parts, rel):
    rows, d = x2.shape
    ar = parts[0].shape[0] // 3
    far = spaced_rows(rows)
    return run(
        functools.partial(conv_front_body, rel=rel, ar=ar, rows=rows),
        "gated_convolution",
        (ends, me, spans),
        (x2, norms, taps, *parts),
        [row_spec(d), whole(*norms.shape), whole(4, TAPS, 128)] + anywhere(len(rel)),
        [row_spec(d), row_spec(2 * d), whole(rows, d), whole(4, far, 128), whole(3, d)],
        [
            out_shape(rows, d, dtype=bf16),
            out_shape(rows, 2 * d, dtype=bf16),
            out_shape(rows, d),
            out_shape(4, far, 128),
            out_shape(3, d),
        ],
        [
            pltpu.VMEM((TILE, d), f32),
            pltpu.VMEM((4, far, 128), f32),
            pltpu.VMEM((d, 2 * d), bf16),
            pltpu.SemaphoreType.DMA((2 * len(rel),)),
        ],
        (rows // TILE,),
        8 * rows * d * d,
        rows * d,
    )


def conv_back_body(t, ends, spans, gz, conv, batch, totals, norms, taps, spaced, g_glu, tap_grad, grad, *, rows):
    e = [ends[j] for j in range(4)]
    grad[...] = jnp.zeros_like(grad)
    mean, scale, count = batch[0:1, :], batch[1:2, :], batch[2:3, :]
    bias_all = jnp.sum(totals[:, 0, :], axis=0, keepdims=True) / count
    gain_all = jnp.sum(totals[:, 1, :], axis=0, keepdims=True) / count
    factor = scale * norms[6:7, :]
    per = []
    for c in range(4):
        cols = slice(128 * c, 128 * (c + 1))
        per.append(
            [
                jnp.broadcast_to(v[:, cols], (8, 128))
                for v in (mean, scale, bias_all, gain_all, factor)
            ]
        )

    def read(g):
        row = pl.multiple_of(8 * g, 8)
        keep = row + lax.broadcasted_iota(jnp.int32, (8, 128), 0) < e[3]
        values = []
        for c in range(4):
            cols = slice(128 * c, 128 * (c + 1))
            m, s, b, k, f = per[c]
            zhat = (conv[pl.ds(row, 8), cols] - m) * s
            away = jnp.where(keep, b + zhat * k, 0.0)
            values.append(f * (gz[pl.ds(row, 8), cols] - away))
        return values

    spread_all(rows // 8, 0, spans, e, read, grad)
    slide(grad, taps, g_glu, rows, 1, True)
    tap_sums(grad, spaced, tap_grad, rows)


def conv_back(ends, spans, gz, conv, batch, totals, norms, taps, spaced):
    rows, d = conv.shape
    far = spaced_rows(rows)
    return run(
        functools.partial(conv_back_body, rows=rows),
        "convolution_backward",
        (ends, spans),
        (gz, conv, batch, totals, norms, taps, spaced),
        [whole(rows, d), whole(rows, d), whole(3, d), whole(*totals.shape), whole(*norms.shape)]
        + [whole(4, TAPS, 128), whole(4, far, 128)],
        [whole(4, far, 128), whole(4, TAPS, 128)],
        [out_shape(4, far, 128), out_shape(4, TAPS, 128)],
        [pltpu.VMEM((4, far, 128), f32)],
        (1,),
        12 * rows * d * TAPS * 40,
        rows * d,
    )


def gates_back_body(t, ends, me, spans, g_glu, norms, gates, x2, g3, mixed, *refs, rel, ar, rows):
    n = len(rel)
    parts, heads = refs[:n], refs[n : 2 * n]
    (g_gates, g2, g_attn, g_mixed, delta, sums) = refs[2 * n : 2 * n + 6]
    glu_rows, w, w_heads, sems = refs[2 * n + 6 :]
    copies = []
    for j, r in enumerate(rel):
        copies += column_blocks(parts[j], me[0] ^ r, w, ar)
        copies += row_block(heads[j], me[0] ^ r, w_heads, ar, 3 * ar)
    load_once(t, copies, sems)
    e = [ends[j] for j in range(4)]

    @pl.when(t == 0)
    def _():
        sums[...] = jnp.zeros_like(sums)

    collect_all(TILE // 8, t * (TILE // 8), spans, e, g_glu, glu_rows)
    gg = glu_rows[...]
    sigma = sigmoid(gates[:, 512:].astype(f32))
    first = (gg * sigma).astype(bf16)
    second = (gg * gates[:, :512].astype(f32) * sigma * (1.0 - sigma)).astype(bf16)
    g_gates[:, :512] = first
    g_gates[:, 512:] = second
    g_hidden = mm_nt(first, w[:, :512]) + mm_nt(second, w[:, 512:])
    normed, scale = normalize(x2[...])
    sums[0:1, :] += col_sum(g_hidden * normed)
    sums[1:2, :] += col_sum(g_hidden)
    out = g3[...] + norm_back(g_hidden, norms[4:5, :], normed, scale)
    g2[...] = out
    branch = out.astype(bf16)
    g_attn[...] = branch
    gm = mm_nt(branch, w_heads[...]).astype(bf16)
    g_mixed[...] = gm
    dots = gm.astype(f32) * mixed[...].astype(f32)
    upper = dots.astype(bf16)
    lower = (dots - upper.astype(f32)).astype(bf16)
    head = lax.broadcasted_iota(jnp.int32, (HEADS, 512), 0)
    ones = (lax.broadcasted_iota(jnp.int32, (HEADS, 512), 1) // 64 == head).astype(bf16)
    delta[...] = mm_nt(ones, upper) + mm_nt(ones, lower)


def gates_back(ends, me, spans, g_glu, norms, gates, x2, g3, mixed, parts, heads, rel):
    rows, d = x2.shape
    ar = parts[0].shape[0] // 3
    return run(
        functools.partial(gates_back_body, rel=rel, ar=ar, rows=rows),
        "gates_backward",
        (ends, me, spans),
        (g_glu, norms, gates, x2, g3, mixed, *parts, *heads),
        [whole(*g_glu.shape), whole(*norms.shape), row_spec(2 * d)]
        + [row_spec(d)] * 3
        + anywhere(2 * len(rel)),
        [row_spec(2 * d), row_spec(d), row_spec(d), row_spec(d)]
        + ["col", whole(2, d)],
        [
            out_shape(rows, 2 * d, dtype=bf16),
            out_shape(rows, d),
            out_shape(rows, d, dtype=bf16),
            out_shape(rows, d, dtype=bf16),
            out_shape(HEADS, rows),
            out_shape(2, d),
        ],
        [
            pltpu.VMEM((TILE, d), f32),
            pltpu.VMEM((d, 2 * d), bf16),
            pltpu.VMEM((d, d), bf16),
            pltpu.SemaphoreType.DMA((3 * len(rel),)),
        ],
        (rows // TILE,),
        6 * rows * d * d,
        rows * d,
    )


def rear_body(t, ends, me, conv, totals, x2, cot, norms, *refs, rel, ar, er, sr):
    n = len(rel)
    points, ffs = refs[:n], refs[n : 2 * n]
    (y, g_third, g_zed, wact, branch_out, hidden, active, g_before, g_out, sums, batch) = refs[2 * n : 2 * n + 11]
    w_point, w_in, w_out, slope, sems = refs[2 * n + 11 :]
    copies = []
    for j, r in enumerate(rel):
        copies += row_block(points[j], me[0] ^ r, w_point, ar, 2 * ar)
        copies += column_blocks(ffs[j], me[0] ^ r, w_in, er)
        copies += row_block(ffs[j], me[0] ^ r, w_out, sr, 4 * er)
    load_once(t, copies, sems)

    @pl.when(t == 0)
    def _():
        sums[...] = jnp.zeros_like(sums)
        total = jnp.sum(totals[...], axis=0)
        count = total[2:3, :]
        mean = total[0:1, :] / count
        batch[0:1, :] = mean
        batch[1:2, :] = lax.rsqrt(total[1:2, :] / count - mean * mean + batch_epsilon)
        batch[2:3, :] = count

    zhat = (conv[...] - batch[0:1, :]) * batch[1:2, :]
    zed = zhat * norms[6:7, :] + norms[7:8, :]
    sigma = sigmoid(zed)
    wa = (zed * sigma).astype(bf16)
    wact[...] = wa
    zed_slope = slope_of(zed, sigma)
    third = x2[...] + mm(wa, w_point[...])
    normed, scale = normalize(third)
    h = (normed * norms[8:9, :] + norms[9:10, :]).astype(bf16)
    hidden[...] = h
    total = None
    for j in range(w_in.shape[1] // 512):
        cols = slice(512 * j, 512 * (j + 1))
        a = mm(h, w_in[:, cols])
        sg = sigmoid(a)
        s = (a * sg).astype(bf16)
        active[:, cols] = s
        slope[:, cols] = slope_of(a, sg)
        part = mm(s, w_out[cols, :])
        total = part if total is None else total + part
    fourth = third + 0.5 * total
    last, last_scale = normalize(fourth)
    keep = t * TILE + lax.broadcasted_iota(jnp.int32, (TILE, 1), 0) < ends[3]
    y[...] = jnp.where(keep, last * norms[10:11, :] + norms[11:12, :], 0.0).astype(bf16)
    g_y = jnp.where(keep, cot[...].astype(f32), 0.0)
    sums[0:1, :] += col_sum(g_y * last)
    sums[1:2, :] += col_sum(g_y)
    g_fourth = norm_back(g_y, norms[10:11, :], last, last_scale)
    go = (0.5 * g_fourth).astype(bf16)
    g_out[...] = go
    g_hidden = None
    for j in range(w_in.shape[1] // 512):
        cols = slice(512 * j, 512 * (j + 1))
        gb = (mm_nt(go, w_out[cols, :]) * slope[:, cols]).astype(bf16)
        g_before[:, cols] = gb
        part = mm_nt(gb, w_in[:, cols])
        g_hidden = part if g_hidden is None else g_hidden + part
    sums[2:3, :] += col_sum(g_hidden * normed)
    sums[3:4, :] += col_sum(g_hidden)
    g3 = g_fourth + norm_back(g_hidden, norms[8:9, :], normed, scale)
    g_third[...] = g3
    branch = g3.astype(bf16)
    branch_out[...] = branch
    gz = mm_nt(branch, w_point[...]) * zed_slope
    g_zed[...] = gz
    sums[4:5, :] += col_sum(gz)
    sums[5:6, :] += col_sum(gz * zhat)


def rear(ends, me, conv, totals, x2, cot, norms, points, ffs, rel):
    rows, d = x2.shape
    ar = points[0].shape[0] // 3
    ff = 4 * d
    er, sr = d // len(rel), ff // len(rel)
    return run(
        functools.partial(rear_body, rel=rel, ar=ar, er=er, sr=sr),
        "norm_feed_forward_and_back",
        (ends, me),
        (conv, totals, x2, cot, norms, *points, *ffs),
        [row_spec(d), whole(*totals.shape), row_spec(d), row_spec(d), whole(*norms.shape)]
        + anywhere(2 * len(rel)),
        [row_spec(d)] * 6 + [row_spec(ff), row_spec(ff), row_spec(d), whole(6, d), whole(3, d)],
        [
            out_shape(rows, d, dtype=bf16),
            out_shape(rows, d),
            out_shape(rows, d),
            out_shape(rows, d, dtype=bf16),
            out_shape(rows, d, dtype=bf16),
            out_shape(rows, d, dtype=bf16),
            out_shape(rows, ff, dtype=bf16),
            out_shape(rows, ff, dtype=bf16),
            out_shape(rows, d, dtype=bf16),
            out_shape(6, d),
            out_shape(3, d),
        ],
        [
            pltpu.VMEM((d, d), bf16),
            pltpu.VMEM((d, ff), bf16),
            pltpu.VMEM((ff, d), bf16),
            pltpu.VMEM((TILE, ff), f32),
            pltpu.SemaphoreType.DMA((6 * len(rel),)),
        ],
        (rows // TILE,),
        rows * d * (8 * ff + 4 * d),
        rows * ff,
        True,
    )


def qkv_back_body(t, me, ga, gb, x1, g2, norms, *refs, rel, ar):
    n = len(rel)
    attn = refs[:n]
    g1, g_out, sums, w, sems = refs[n:]
    copies = []
    for j, r in enumerate(rel):
        copies += column_blocks(attn[j], me[0] ^ r, w, ar)
    load_once(t, copies, sems)

    @pl.when(t == 0)
    def _():
        sums[...] = jnp.zeros_like(sums)

    g_hidden = None
    for z in range(3):
        for half, g in enumerate((ga, gb)):
            cols = slice(512 * z + 256 * half, 512 * z + 256 * (half + 1))
            part = mm_nt(g[:, 256 * z : 256 * (z + 1)], w[:, cols])
            g_hidden = part if g_hidden is None else g_hidden + part
    normed, scale = normalize(x1[...])
    sums[0:1, :] += col_sum(g_hidden * normed)
    sums[1:2, :] += col_sum(g_hidden)
    out = g2[...] + norm_back(g_hidden, norms[2:3, :], normed, scale)
    g1[...] = out
    g_out[...] = (0.5 * out).astype(bf16)


def qkv_back(me, ga, gb, x1, g2, norms, attn, rel):
    rows, d = x1.shape
    ar = d // len(rel)
    return run(
        functools.partial(qkv_back_body, rel=rel, ar=ar),
        "query_key_value_backward",
        (me,),
        (ga, gb, x1, g2, norms, *attn),
        [row_spec(3 * d // 2)] * 2 + [row_spec(d)] * 2 + [whole(*norms.shape)] + anywhere(len(rel)),
        [row_spec(d), row_spec(d), whole(2, d)],
        [out_shape(rows, d), out_shape(rows, d, dtype=bf16), out_shape(2, d)],
        [pltpu.VMEM((d, 3 * d), bf16), pltpu.SemaphoreType.DMA((3 * len(rel),))],
        (rows // TILE,),
        6 * rows * d * d,
    )


def ff_back_body(t, me, g1, go, x, before, norms, *refs, rel, er, sr):
    n = len(rel)
    parts = refs[:n]
    g_frames, g_before, sums, w_in, w_out, sems = refs[n:]
    copies = []
    for j, r in enumerate(rel):
        copies += column_blocks(parts[j], me[0] ^ r, w_in, er)
        copies += row_block(parts[j], me[0] ^ r, w_out, sr, 4 * er)
    load_once(t, copies, sems)

    @pl.when(t == 0)
    def _():
        sums[...] = jnp.zeros_like(sums)

    out = go[...]
    g_hidden = None
    for j in range(w_in.shape[1] // 512):
        cols = slice(512 * j, 512 * (j + 1))
        a = before[:, cols].astype(f32)
        gb = (mm_nt(out, w_out[cols, :]) * slope_of(a, sigmoid(a))).astype(bf16)
        g_before[:, cols] = gb
        part = mm_nt(gb, w_in[:, cols])
        g_hidden = part if g_hidden is None else g_hidden + part
    normed, scale = normalize(x[...].astype(f32))
    sums[0:1, :] += col_sum(g_hidden * normed)
    sums[1:2, :] += col_sum(g_hidden)
    g_frames[...] = g1[...] + norm_back(g_hidden, norms[0:1, :], normed, scale)


def ff_back(me, g1, go, x, before, norms, parts, rel):
    rows, d = x.shape
    ff = 4 * d
    er, sr = d // len(rel), ff // len(rel)
    return run(
        functools.partial(ff_back_body, rel=rel, er=er, sr=sr),
        "feed_forward_backward",
        (me,),
        (g1, go, x, before, norms, *parts),
        [row_spec(d), row_spec(d), row_spec(d), row_spec(ff), whole(*norms.shape)] + anywhere(len(rel)),
        [row_spec(d), row_spec(ff), whole(2, d)],
        [out_shape(rows, d), out_shape(rows, ff, dtype=bf16), out_shape(2, d)],
        [
            pltpu.VMEM((d, ff), bf16),
            pltpu.VMEM((ff, d), bf16),
            pltpu.SemaphoreType.DMA((5 * len(rel),)),
        ],
        (rows // TILE,),
        4 * rows * d * ff,
        rows * ff,
        True,
    )


def place_owners(me, tile, keep, send, base, height, owners, first):
    for k in range(owners):
        owner = first + k
        rows = tile[k * height : (k + 1) * height, :]
        mine = ((owner ^ me[0]) & 1) == 0

        @pl.when(mine)
        def _(rows=rows, owner=owner):
            keep[owner >> 1, pl.ds(base, height), :] = rows

        @pl.when(jnp.logical_not(mine))
        def _(rows=rows, owner=owner):
            send[owner >> 1, pl.ds(base, height), :] = rows


def weight_grad_body(t, me, *refs, fs, parts, n1, n2):
    refs = list(refs)
    first = [refs.pop(0) for _ in range(1 + parts)] if n1 else None
    second = [refs.pop(0) for _ in range(2)] if n2 else None
    keep, send = refs.pop(0), refs.pop(0)
    er = 512 // fs
    if n1:
        base = pl.multiple_of(t * er, er)
        tiles = [mm_tn(first[0][...], ref[...]).astype(bf16) for ref in first[1:]]
        tile = tiles[0] if parts == 1 else jnp.concatenate(tiles, axis=1)
        place_owners(me, tile, keep, send, base, er, fs, 0)
    if n2:
        sr = 512 * n2 // fs
        per = max(1, 512 // sr)

        def one(block):
            tile = mm_tn(second[0][...], second[1][...]).astype(bf16)
            place_owners(me, tile, keep, send, n1 * er, sr, per, block * per)

        if n1 in (0, n2):
            one(t)
        else:
            pl.when(t == 0)(lambda: one(0))


def weight_grad(name, me, fs, first=None, second=None):
    inputs, specs = [], []
    n1 = n2 = parts = 0
    if first:
        h, gs = first
        rows, parts = h.shape[0], len(gs)
        wide = 512 // parts
        n1 = gs[0].shape[1] // wide
        inputs += [h, *gs]
        specs += [whole(rows, 512)] + [("lane", wide)] * parts
    if second:
        s, o = second
        rows = s.shape[0]
        n2 = s.shape[1] // 512
        inputs += [s, o]
        stepped = n1 in (0, n2)
        specs += [("lane", 512) if stepped else "whole", whole(rows, 512)]
    height = (n1 + n2) * 512 // fs
    return run(
        functools.partial(weight_grad_body, fs=fs, parts=parts, n1=n1, n2=n2),
        name,
        (me,),
        inputs,
        specs,
        [whole(fs // 2, height, 512)] * 2,
        [out_shape(fs // 2, height, 512, dtype=bf16)] * 2,
        [],
        (n1 or n2,),
        2 * rows * 512 * 512 * (n1 + n2),
        0,
        n1 == n2,
    )


def join(*pairs):
    return tuple(jnp.concatenate(list(side), axis=1) for side in zip(*pairs))


def bits_of(size):
    return int(size).bit_length() - 1


def swap(value, axis, size, mask):
    return lax.ppermute(value, axis, [(k, k ^ mask) for k in range(size)])


def relative(fs):
    rel = [0]
    for bit in reversed(range(bits_of(fs))):
        rel = rel + [r ^ (1 << bit) for r in rel]
    return tuple(rel)


def first_part(own, fs):
    parts = [own]
    for bit in reversed(range(1, bits_of(fs))):
        parts = parts + [swap(part, "fsdp", fs, 1 << bit) for part in parts]
    return parts


def second_part(parts, fs):
    return parts + [swap(part, "fsdp", fs, 1) for part in parts]


def sum_of(parts):
    total = parts[0].astype(f32)
    for part in parts[1:]:
        total = total + part.astype(f32)
    return total.astype(bf16)


class Chain:
    def __init__(self, pair, fs, dp):
        keep, send = pair
        self.fs, self.dp = fs, dp
        self.me, self.pack = lax.axis_index("fsdp"), lax.axis_index("dp")
        zero = jnp.int32(0)
        self.at, self.size = [zero, zero], list(keep.shape[:2])
        self.parts = [(keep, zero, zero)]
        self.stages = [("fsdp", bit, "halve") for bit in reversed(range(1, bits_of(fs)))]
        self.stages += [("dp", bit, "add" if bit else "halve") for bit in range(bits_of(dp))]
        self.stages.append(("dp", 0, "join"))
        self.flight = swap(send, "fsdp", fs, 1)
        self.whole = None

    def take(self, y, r):
        shape = (self.size[0], self.size[1], 512)
        return sum_of(
            [lax.dynamic_slice(part, (y - y0, r - r0, 0), shape) for part, y0, r0 in self.parts]
        )

    def hold(self, *tokens):
        self.flight = after(self.flight, *tokens)

    def advance(self):
        if not self.stages:
            return None
        self.parts.append((self.flight, *self.at))
        axis, bit, kind = self.stages.pop(0)
        size, index = (self.fs, self.me) if axis == "fsdp" else (self.dp, self.pack)
        side = (index >> bit) & 1
        if kind == "halve":
            dim = 0 if axis == "fsdp" else 1
            base = self.at[dim]
            self.size[dim] //= 2
            self.at[dim] = base + (1 - side) * self.size[dim]
            send = self.take(*self.at)
            self.at[dim] = base + side * self.size[dim]
        else:
            send = self.take(*self.at)
            self.parts = [(send, *self.at)]
        self.flight = swap(send, axis, size, 1 << bit)
        return send

    def result(self):
        while self.stages:
            self.advance()
        mine, other = self.parts[0][0].reshape(-1, 512), self.flight.reshape(-1, 512)
        pair = [jnp.concatenate([mine, other], axis=0), jnp.concatenate([other, mine], axis=0)]
        return jnp.where((self.pack & 1) == 0, *pair)


def after(value, *tokens):
    tokens = [token for token in tokens if token is not None]
    return lax.optimization_barrier((value, *tokens))[0]


def from_everyone(rows):
    axes = ("dp", "fsdp")
    count = lax.axis_size(axes)
    spread = jnp.broadcast_to(rows[None], (count,) + rows.shape)
    return lax.all_to_all(spread, axes, 0, 0, tiled=True)


def to_rows(block):
    r, c = block.shape
    k = c // 512
    return block.reshape(r, k, 512).swapaxes(0, 1).reshape(k * r, 512)


def from_rows(rows, r, c):
    k = c // 512
    return rows.reshape(k, r, 512).swapaxes(0, 1).reshape(r, c)


def pack_body(t, a, b, out, *, n, er):
    for j in range(n):
        out[er * j : er * (j + 1), :] = a[:, 512 * j : 512 * (j + 1)].astype(bf16)
    out[er * n :, :] = b[...].astype(bf16)


def pack(name, a, b, index=None):
    er, n = a.shape[-2], a.shape[-1] // 512
    sr = b.shape[-2]
    return run(
        functools.partial(pack_body, n=n, er=er),
        name,
        (),
        (a, b),
        ["whole" if index is None else ("stack", index)] * 2,
        ["whole"],
        [out_shape(n * er + sr, 512, dtype=bf16)],
        [],
        (1,),
        er * n * 1024,
        0,
        True,
    )[0]


def adam_body(*refs):
    ga, gb = refs[0][...], refs[1][...]
    outs = refs[-6:]
    for ref, grad, to in ((refs[2:5], ga, outs[:3]), (refs[5:8], gb, outs[3:])):
        new = adam_update(ref[0][...], ref[1][...], ref[2][...], grad.astype(f32), decay_rate)
        for place, value in zip(to, new):
            place[...] = value


def adam_single_body(*refs):
    outs = refs[-3:]
    new = adam_update(refs[1][...], refs[2][...], refs[3][...], refs[0][...].astype(f32), decay_rate)
    for place, value in zip(outs, new):
        place[...] = value


def adam_single(name, grad, state, by_row, index, into):
    height, width = state[0].shape[-2:]
    n = 4
    block = (height // n, width) if by_row else (height, width // n)
    spec = pl.BlockSpec((None,) + block, lambda i: (index, i, 0) if by_row else (index, 0, i))
    return pl.pallas_call(
        adam_single_body,
        grid=(n,),
        in_specs=[pl.BlockSpec(block, lambda i: (i, 0))] + [spec] * 3 + [pl.BlockSpec(memory_space=pl.ANY)] * 3,
        out_specs=[spec] * 3,
        out_shape=[out_shape(*v.shape) for v in state],
        input_output_aliases={4 + j: j for j in range(3)},
        cost_estimate=pl.CostEstimate(
            flops=20 * height * width, bytes_accessed=26 * height * width, transcendentals=height * width
        ),
        name=name,
    )(grad, *state, *into)


def adam_pair(name, grad, first, second, steps, index=None, into=None):
    er, n = first[0].shape[-2], first[0].shape[-1] // 512
    sr = second[0].shape[-2]
    part = sr // n if steps else sr
    lead = () if index is None else (None,)
    at = () if index is None else (index,)
    spec_a = pl.BlockSpec(lead + (er, 512), lambda i: at + (0, i))
    spec_b = pl.BlockSpec(lead + (part, 512), lambda i: at + ((i, 0) if steps else (0, 0)))
    grad_a = pl.BlockSpec((er, 512), lambda i: (i, 0))
    grad_b = pl.BlockSpec((part, 512), lambda i: (n * er // part + (i if steps else 0), 0))
    inputs = [grad, grad, *first, *second]
    specs = [grad_a, grad_b] + [spec_a] * 3 + [spec_b] * 3
    alias = {}
    if into is not None:
        alias = {len(inputs) + j: j for j in range(6)}
        inputs += list(into)
        specs += [pl.BlockSpec(memory_space=pl.ANY)] * 6
    return pl.pallas_call(
        adam_body,
        grid=(n,),
        in_specs=specs,
        out_specs=[spec_a] * 3 + [spec_b] * 3,
        out_shape=[out_shape(*v.shape) for v in (*first, *second)],
        input_output_aliases=alias,
        cost_estimate=pl.CostEstimate(
            flops=20 * er * 512 * n, bytes_accessed=26 * (er * n + sr) * 512, transcendentals=er * 512 * n
        ),
        name=name,
    )(*inputs)


def adam_update(master, first, second_block, grad, decay):
    first_new = beta_first * first + (1.0 - beta_first) * grad
    second_new = beta_second * second_block + (1.0 - beta_second) * grad * grad
    first_hat = first_new / (1.0 - beta_first**STEP)
    second_hat = second_new / (1.0 - beta_second**STEP)
    master_new = master - learn_rate * (
        first_hat / (jnp.sqrt(second_hat) + adam_epsilon) + decay * master
    )
    return (master_new, first_new, second_new)


def moments_only(first, second_block, grad):
    first_new = beta_first * first + (1.0 - beta_first) * grad
    second_new = beta_second * second_block + (1.0 - beta_second) * grad * grad
    return (first_new, second_new)


def rotary_tables(position, half):
    freq = jnp.exp(jnp.arange(half, dtype=f32) * (-math.log(10000.0) / half))
    angle = position.astype(f32)[:, None] * freq[None, :]
    cosine, sine = jnp.cos(angle), jnp.sin(angle)
    return (
        jnp.concatenate([cosine] * 4, axis=1),
        jnp.concatenate([-sine, sine, -sine, sine], axis=1),
    )


def per_device(
    frames,
    cotangent,
    lengths,
    expand,
    expand_first,
    expand_second,
    shrink,
    shrink_first,
    shrink_second,
    attend,
    attend_first,
    attend_second,
    heads_out,
    heads_out_first,
    heads_out_second,
    pointwise,
    pointwise_first,
    pointwise_second,
    pointwise_out,
    pointwise_out_first,
    pointwise_out_second,
    depthwise,
    depthwise_first,
    depthwise_second,
    norm_table,
    norm_table_first,
    norm_table_second,
):
    fs, dp = (lax.axis_size("fsdp"), lax.axis_size("dp"))
    rel = relative(fs)
    er, sr, ar = expand.shape[1], shrink.shape[1], attend.shape[0]
    dr = depthwise.shape[1]
    device = lax.axis_index("fsdp")
    me = device.astype(jnp.int32).reshape(1)
    ends = jnp.cumsum(lengths[0, :4]).astype(jnp.int32)
    rows, width = frames.shape

    early_own = pack("pack_early", expand, shrink, 0)
    ff_zero = first_part(early_own, fs)
    small = jnp.concatenate([after(depthwise, early_own), norm_table], axis=0).astype(bf16)
    tiny_rows = small.shape[0]
    small_parts = second_part(first_part(small, fs), fs)
    places = jnp.arange(rows, dtype=jnp.int32)
    segment = jnp.sum((places[:, None] >= ends[None, :]).astype(jnp.int32), axis=1)
    starts = jnp.concatenate([jnp.zeros((1,), jnp.int32), ends])
    pick = (segment[:, None] == jnp.arange(5, dtype=jnp.int32)[None, :]).astype(jnp.int32)
    position = places - jnp.sum(pick * starts[None, :], axis=1)
    lo, hi = segment[::8], segment[7::8]
    spans = jnp.stack([lo, hi, jnp.broadcast_to(jnp.max(hi - lo), lo.shape)])
    cs, sn = rotary_tables(position, width // HEADS // 2)

    attn_own = pack("pack_attn", attend, heads_out)
    conv_own = pack("pack_conv", pointwise, pointwise_out)
    late_own = pack("pack_late", expand, shrink, 1)
    small_full = jnp.zeros((fs, tiny_rows, dr), bf16)
    for k, r in enumerate(rel):
        small_full = lax.dynamic_update_slice_in_dim(small_full, small_parts[k][None], device ^ r, 0)
    small_full = small_full.swapaxes(0, 1).reshape(tiny_rows, fs * dr).astype(f32)
    norms = small_full[TAPS:]
    taps = small_full[:TAPS].reshape(TAPS, width // 128, 128).swapaxes(0, 1)
    ff_zero = [ff_zero[0]] + [after(part, attn_own, conv_own, late_own, cs, sn, norms, taps) for part in ff_zero[1:]]
    attn_parts = first_part(after(attn_own, *ff_zero), fs)
    ff_zero = second_part(ff_zero, fs)


    x1, hidden_zero, before_zero, active_zero = ff_forward(
        me, frames, norms, ff_zero, rel
    )
    attn_parts = [after(part, x1) for part in attn_parts]
    conv_parts = first_part(after(conv_own, *attn_parts), fs)
    attn_parts = second_part(attn_parts, fs)
    hidden_attn, q, k, v, kt = qkv(me, x1, norms, cs, sn, attn_parts, rel)
    conv_parts = [after(part, q) for part in conv_parts]
    ff_one = first_part(after(late_own, *conv_parts), fs)
    conv_parts = second_part(conv_parts, fs)
    x2, mixed, lse = attention(ends, me, after(q, *conv_parts), k, v, x1, attn_parts, rel)
    hidden_conv, gates, conv, spaced, stats = conv_front(ends, me, spans, x2, norms, taps, conv_parts, rel)
    ff_one = second_part([after(part, stats) for part in ff_one], fs)
    totals = from_everyone(stats)
    (
        layer_output,
        g_third,
        g_zed,
        wact,
        g_branch,
        hidden_one,
        active_one,
        g_before_one,
        g_out_one,
        rear_sums,
        batch,
    ) = rear(ends, me, conv, totals, x2, cotangent, norms, conv_parts, ff_one, rel)
    back_totals = from_everyone(rear_sums[4:6])
    late_pair = weight_grad(
        "weight_grad_late", me, fs, (hidden_one, (g_before_one,)), (active_one, g_out_one)
    )
    late = Chain((late_pair[0], after(late_pair[1], back_totals)), fs, dp)
    g_glu, tap_grad = conv_back(ends, spans, after(g_zed, late_pair[1]), conv, batch, back_totals, norms, taps, spaced)
    g_glu = after(g_glu, late.advance())
    g_gates, g_second, g_attn, g_mixed, delta, conv_sums = gates_back(
        ends, me, spans, g_glu, norms, gates, x2, g_third, mixed, conv_parts, attn_parts, rel
    )
    conv_pair = weight_grad("weight_grad_conv", me, fs, (hidden_conv, (g_gates,)), (wact, g_branch))
    middle = Chain(conv_pair, fs, dp)
    first_half = attention_back(
        ends, q, k, kt, v, after(g_mixed, conv_pair[1]), lse, delta, cs, sn, 0, 2
    )
    late.hold(first_half)
    middle.hold(first_half)
    tokens = (late.advance(), middle.advance(), first_half)
    second_half = attention_back(ends, q, k, kt, v, after(g_mixed, *tokens), lse, delta, cs, sn, 2, 2)
    late.hold(second_half)
    middle.hold(second_half)
    first_half = after(first_half, late.advance(), middle.advance())
    attn_pair = weight_grad(
        "weight_grad_attn", me, fs, (hidden_attn, (first_half, second_half)), (mixed, g_attn)
    )
    attn = Chain(attn_pair, fs, dp)
    g_first, g_out_zero, qkv_sums = qkv_back(
        me, after(first_half, attn_pair[1]), second_half, x1, g_second, norms, attn_parts, rel
    )
    for chain in (late, middle, attn):
        chain.hold(g_first)
    tokens = (late.advance(), middle.advance(), attn.advance())
    out_pair = weight_grad(
        "weight_grad_shrink", me, fs, None, (active_zero, after(g_out_zero, *tokens))
    )
    early_out = Chain(out_pair, fs, dp)
    middle.hold(out_pair[1])
    frames_grad, g_before_zero, ff_sums = ff_back(
        me, g_first, after(g_out_zero, out_pair[1], middle.advance()), frames, before_zero, norms, ff_zero, rel
    )
    for chain in (late, middle, attn, early_out):
        chain.hold(g_before_zero)
    tokens = (late.advance(), attn.advance(), early_out.advance(), middle.advance())
    early_in = weight_grad(
        "weight_grad_expand", me, fs, (hidden_zero, (after(g_before_zero, *tokens),))
    )
    grad_norms = jnp.concatenate(
        [
            ff_sums,
            qkv_sums,
            conv_sums,
            rear_sums[5:6],
            rear_sums[4:5],
            rear_sums[2:4],
            rear_sums[0:2],
        ]
    )
    grad_kernel = tap_grad.swapaxes(0, 1).reshape(TAPS, width)
    small_grad = jnp.concatenate([grad_kernel, grad_norms], axis=0).astype(bf16)
    small_grad = small_grad.reshape(tiny_rows, fs, dr).swapaxes(0, 1)
    small_size = tiny_rows * dr
    small_pad = -small_size % (512 * dp)
    small_grad = jnp.pad(small_grad.reshape(fs, small_size), ((0, 0), (0, small_pad)))
    small_grad = small_grad.reshape(fs // 2, 2, -1, 512).swapaxes(0, 1)
    core = device & 1
    small_pair = (
        lax.dynamic_index_in_dim(small_grad, core, 0, False),
        lax.dynamic_index_in_dim(small_grad, 1 - core, 0, False),
    )
    tail_pair = join(early_in, small_pair)
    tail = Chain(tail_pair, fs, dp)
    for chain in (late, middle, attn, early_out):
        chain.hold(tail_pair[1])
    sent = tail.advance()
    for chain in (late, middle, attn, early_out):
        chain.hold(sent)
    attn.advance()
    early_out.advance()
    red_late, red_conv = late.result(), middle.result()
    expands = (expand, expand_first, expand_second)
    shrinks = (shrink, shrink_first, shrink_second)
    new_late = adam_pair("adam_late", red_late, expands, shrinks, True, 1)
    new_conv = adam_pair(
        "adam_conv",
        red_conv,
        (pointwise, pointwise_first, pointwise_second),
        (pointwise_out, pointwise_out_first, pointwise_out_second),
        False,
    )
    tail.hold(new_late[0])
    sent = tail.advance()
    attn.hold(sent)
    early_out.hold(sent)
    tail.hold(attn.advance(), early_out.advance(), new_conv[0])
    sent = tail.advance()
    attn.hold(sent)
    early_out.hold(sent)
    tail.hold(attn.advance(), early_out.advance())
    sent = tail.advance()
    early_out.hold(sent)
    tail.hold(early_out.advance())
    new_attn = adam_pair(
        "adam_attn",
        after(attn.result(), sent),
        (attend, attend_first, attend_second),
        (heads_out, heads_out_first, heads_out_second),
        False,
    )
    tail.hold(new_attn[0])
    sent = tail.advance()
    red_out = after(early_out.result(), sent)
    new_shrink = adam_single("adam_shrink", red_out, shrinks, True, 0, new_late[3:])
    tail.hold(new_shrink[0])
    red_in = tail.result()
    new_expand = adam_single("adam_expand", red_in, expands, False, 0, new_late[:3])
    red_small = red_in[4 * er :].reshape(-1)[:small_size].reshape(tiny_rows, dr).astype(f32)
    new_taps = adam_update(depthwise, depthwise_first, depthwise_second, red_small[:TAPS], decay_rate)
    red_norms = red_small[TAPS:]
    new_norms = moments_only(norm_table_first, norm_table_second, red_norms)
    return (
        layer_output,
        frames_grad,
        *new_expand,
        *new_shrink,
        *new_attn,
        *new_conv,
        *new_taps,
        red_norms,
        *new_norms,
    )


def solution(mesh):
    return jax.shard_map(
        per_device,
        mesh=mesh,
        in_specs=(
            P(("dp", "fsdp"), None),
            P(("dp", "fsdp"), None),
            P(("dp", "fsdp"), None),
            P(None, "fsdp", None),
            P(None, "fsdp", None),
            P(None, "fsdp", None),
            P(None, "fsdp", None),
            P(None, "fsdp", None),
            P(None, "fsdp", None),
            P("fsdp", None),
            P("fsdp", None),
            P("fsdp", None),
            P("fsdp", None),
            P("fsdp", None),
            P("fsdp", None),
            P("fsdp", None),
            P("fsdp", None),
            P("fsdp", None),
            P("fsdp", None),
            P("fsdp", None),
            P("fsdp", None),
            P(None, "fsdp"),
            P(None, "fsdp"),
            P(None, "fsdp"),
            P(None, "fsdp"),
            P(None, "fsdp"),
            P(None, "fsdp"),
        ),
        out_specs=(
            P(("dp", "fsdp"), None),
            P(("dp", "fsdp"), None),
            P(None, "fsdp", None),
            P(None, "fsdp", None),
            P(None, "fsdp", None),
            P(None, "fsdp", None),
            P(None, "fsdp", None),
            P(None, "fsdp", None),
            P("fsdp", None),
            P("fsdp", None),
            P("fsdp", None),
            P("fsdp", None),
            P("fsdp", None),
            P("fsdp", None),
            P("fsdp", None),
            P("fsdp", None),
            P("fsdp", None),
            P("fsdp", None),
            P("fsdp", None),
            P("fsdp", None),
            P(None, "fsdp"),
            P(None, "fsdp"),
            P(None, "fsdp"),
            P(None, "fsdp"),
            P(None, "fsdp"),
            P(None, "fsdp"),
        ),
        check_vma=False,
    )
```

time: 941 us -> 437 us (0.46)
  waiting for transfers between devices: 338 us -> 77.4 us
  Pallas kernels: 0 us -> 226 us
  matrix products: 175 us -> 0 us
  other arithmetic: 186 us -> 42 us
  blocking collectives: 152 us -> 16.4 us
  local copies, waits for them, and re-layouts: 68.8 us -> 29.8 us
  starting transfers between devices: 0.54 us -> 35.7 us
  between operations: 17.4 us -> 2.05 us
    pallas_call x0 -> x25, Pallas kernels: none -> 226 us  [the longest x12 139 us: run(): pl.pallas_call(kernel, in_specs=[pl.BlockSpec(memory_space=pltpu.SMEM)] *...]
    dot_general x30 -> x0, matrix products: 175 us -> none  [the longest x8 39.1 us: times_transposed(): lax.dot_general(left, right, (((1,), (1,)), ((), ())), preferred_element_...]
    psum x1 -> x0, waiting for transfers between devices: 174 us -> none  [per_device(): lax.psum((shards[0], shards[1], shards[2], shards[3], shards[4], shards[5...]
    reduce_scatter x8 -> x0, waiting for transfers between devices: 143 us -> none  [the longest x1 74.3 us: per_device(): lax.psum_scatter(gradients[0], 'fsdp', scatter_dimension=1, tiled=True)]
    psum x3 -> x0, blocking collectives: 121 us -> none  [the longest x1 41.2 us: per_device(): totals = lax.psum((local_bias, local_gain), ('dp', 'fsdp'))]
    reduce_sum x20 -> x2, other arithmetic: 80.3 us -> 0.17 us  [the longest x1 0.08 us: per_device(): jnp.sum((places[:, None] >= ends[None, :]).astype(jnp.int32), axis=1)]
    ppermute x0 -> x45, waiting for transfers between devices: none -> 77.4 us  [swap(): return lax.ppermute(value, axis, [(k, k ^ mask) for k in range(size)])]
    another operation x10 -> x5, other arithmetic: 36.8 us -> 0.26 us
  transfers between devices with their start and end apart: 13 -> 46, of which waited for: 7 -> 16; matrix products, arithmetic and copies ran while one was open for 34% -> 10% of each run, Pallas kernels for 0% -> 44%
where the time goes in v2:
time: 437 us; the launch traced here: 430 us
  Pallas kernels  226 us (52%)
  waiting for transfers between devices  77.4 us (18%)
  other arithmetic  42 us (10%)
  starting transfers between devices  35.7 us (8%)
  local copies, waits for them, and re-layouts  29.8 us (7%)
  blocking collectives  16.4 us (4%)
    pallas_call x12, Pallas kernels, run(): pl.pallas_call(kernel, in_specs=[pl.BlockSpec(memory_space=pltpu.SMEM)] *...  139 us
    ppermute x45, waiting for transfers between devices, swap(): return lax.ppermute(value, axis, [(k, k ^ mask) for k in range(size)])  77.4 us
    pallas_call x8, Pallas kernels, run(): pl.pallas_call(lambda *refs: body(pl.program_id(0), *refs), grid_spec=plt...  63.3 us
    ppermute x45, starting transfers between devices, swap(): return lax.ppermute(value, axis, [(k, k ^ mask) for k in range(size)])  33.1 us
    convert_element_type x25, other arithmetic, sum_of(): return total.astype(bf16)  27 us
    unnamed x118, local copies, waits for them, and re-layouts  21.9 us
    all_to_all x1, blocking collectives, from_everyone(): return lax.all_to_all(spread, axes, 0, 0, tiled=True)  16.4 us
    pallas_call x3, Pallas kernels, adam_pair(): pl.pallas_call(adam_body, grid=(n,), in_specs=specs, out_specs=[spec_a] *...  15 us
  transfers between devices with their start and end apart: 46, of which 16 were waited for; matrix products, arithmetic and copies ran while one was open for 10% of the time, Pallas kernels for 44%

profile of v2, /device:TPU:0, one launch (start us, length us, event | category | flops | bytes accessed | tf_op | source)
XLA Modules:
  0.0 429.5 jit_solution(13745209364245483906)
XLA Ops:
  2.3 2.4 pack_early.1.refs_3_.refs_6_
  4.7 3.0 collective-permute-start
  8.7 1.9 fusion.3
  13.5 2.4 pack_late.1.refs_11_
  17.1 16.4 %collective-permute-done.3.refs_4_.refs_7_ = bf16[1024,512]{1,0:T(8,128)(2,1)} collective-permute-done((bf16[1024,512]{1,0:T(8,128)(2,1)}, bf16[1024,512]{1,0:T(8,128)(2,1)}, u32[]{:S(2)}, u32[]{:S(2)}) %collective-permute-start.3) | collective-permute-done | bytes 1048608 | tf_op jit(solution)/shard_map/ppermute | solution.py:1063
  34.0 2.5 collective-permute-done.5.refs_6_.refs_9_
  37.4 11.3 %ff_forward.1 = (f32[1024,512]{1,0:T(8,128)}, bf16[1024,512]{1,0:T(8,128)(2,1)S(1)}, bf16[1024,2048]{1,0:T(8,128)(2,1)}, bf16[1024,2048]{1,0:T(8,128)(2,1)}) custom-call(s32[1]{0:T(128)} %bitcast.2.refs_0_.refs_1_, bf16[1024,512]{1,0:T(8,128)(2,1)S(1)} %copy-done.17, f32[12,512]{1,0:T(8,128)S(1)} %bitcast.62, bf16[1024,512]{1,0:T(8,128)(2,1)} %pack_early.1.refs_3_.refs_6_, ...), custom_call_target="tpu_custom_call" | custom-call | flops 4294967296 | bytes 16801792 | tf_op jit(solution)/shard_map/ff_forward/pallas_call | solution.py:183
  52.4 9.0 %query_key_value.1 = (bf16[1024,512]{1,0:T(8,128)(2,1)}, bf16[1024,512]{1,0:T(8,128)(2,1)}, bf16[1024,512]{1,0:T(8,128)(2,1)}, bf16[1024,512]{1,0:T(8,128)(2,1)}, bf16[512,1024]{1,0:T(8,128)(2,1)}) custom-call(s32[1]{0:T(128)} %bitcast.2.refs_0_.refs_1_, f32[1024,512]{1,0:T(8,128)} %get-tuple-element.159.refs_1_.refs_5_.refs_3_, f32[12,512]{1,0:T(8,128)S(1)} %bitcast.63, ...), custom_call_target="tpu_custom_call" | custom-call | flops 1610612736 | bytes 10510336 | tf_op jit(solution)/shard_map/query_key_value/pallas_call | solution.py:215
  64.3 21.2 %attention_forward.1 = (f32[1024,512]{1,0:T(8,128)}, bf16[1024,512]{1,0:T(8,128)(2,1)S(1)}, f32[8,1024]{1,0:T(8,128)S(1)}) custom-call(s32[4]{0:T(128)S(1)} %bitcast.72, s32[1]{0:T(128)} %bitcast.2.refs_0_.refs_1_, bf16[1024,512]{1,0:T(8,128)(2,1)} %get-tuple-element.167.refs_2_.refs_1_, bf16[1024,512]{1,0:T(8,128)(2,1)} %get-tuple-element.168.refs_3_.refs_2_, ...), custom_call_target="tpu_custom_call" | custom-call | flops 2147483648 | bytes 10518528 | tf_op jit(solution)/shard_map/attention_forward/pallas_call | solution.py:215
  86.6 17.6 %gated_convolution.1 = (bf16[1024,512]{1,0:T(8,128)(2,1)S(1)}, bf16[1024,1024]{1,0:T(8,128)(2,1)}, f32[1024,512]{1,0:T(8,128)}, f32[4,1120,128]{2,1,0:T(8,128)}, f32[3,512]{1,0:T(4,128)S(1)}) custom-call(s32[4]{0:T(128)S(1)} %bitcast.73, s32[1]{0:T(128)} %bitcast.2.refs_0_.refs_1_, s32[3,128]{1,0:T(4,128)S(1)} %add_add_fusion.refs_2_.refs_1_, ...), custom_call_target="tpu_custom_call" | custom-call | flops 2147483648 | bytes 11302912 | tf_op jit(solution)/shard_map/gated_convolution/pallas_call | solution.py:215
  105.7 16.4 %all_to_all.10.refs_3_ = f32[32,3,512]{2,1,0:T(4,128)S(1)} all-to-all(f32[32,3,512]{2,1,0:T(4,128)S(1)} %broadcast_in_dim.16), channel_id=1, replica_groups=mesh['dp'=8,'fsdp'=4] {'dp','fsdp'}, dimensions={0} | all-to-all | bytes 393216 | tf_op jit(solution)/shard_map/all_to_all | solution.py:1151
  123.5 24.1 %norm_feed_forward_and_back.1 = (bf16[1024,512]{1,0:T(8,128)(2,1)}, f32[1024,512]{1,0:T(8,128)}, f32[1024,512]{1,0:T(8,128)}, bf16[1024,512]{1,0:T(8,128)(2,1)S(...) custom-call(s32[4]{0:T(128)S(1)} %bitcast.74, ...), custom_call_target="tpu_custom_call" | custom-call | flops 9663676416 | bytes 29075456 | tf_op jit(solution)/shard_map/norm_feed_forward_and_back/pallas_call | solution.py:183
  150.3 2.6 all-to-all-start.1
  155.3 10.1 %weight_grad_late.1 = (bf16[2,1024,512]{2,1,0:T(8,128)(2,1)}, bf16[2,1024,512]{2,1,0:T(8,128)(2,1)}) custom-call(s32[1]{0:T(128)} %bitcast.2.refs_0_.refs_1_, bf16[1024,512]{1,0:T(8,128)(2,1)S(1)} %copy-done.31, bf16[1024,2048]{1,0:T(8,128)(2,1)} %get-tuple-element.180.refs_2_, bf16[1024,2048]{1,0:T(8,128)(2,1)} %get-tuple-element.181.refs_3_, ...), custom_call_target="tpu_custom_call" | custom-call | flops 4294967296 | bytes 14680064 | tf_op jit(solution)/shard_map/weight_grad_late/pallas_call | solution.py:183
  167.9 17.6 %convolution_backward.1 = (f32[4,1120,128]{2,1,0:T(8,128)}, f32[4,32,128]{2,1,0:T(8,128)S(1)}) custom-call(s32[4]{0:T(128)S(1)} %bitcast.75, s32[3,128]{1,0:T(4,128)S(1)} %add_add_fusion.refs_2_.refs_1_, f32[1024,512]{1,0:T(8,128)S(1)} %copy-done.35, f32[1024,512]{1,0:T(8,128)} %get-tuple-element.171.refs_2_.refs_3_, ...), custom_call_target="tpu_custom_call" | custom-call | flops 8053063680 | bytes 9074688 | tf_op jit(solution)/shard_map/convolution_backward/pallas_call | solution.py:215
  185.5 2.5 add_convert_fusion
  189.7 13.3 %gates_backward.1 = (bf16[1024,1024]{1,0:T(8,128)(2,1)}, f32[1024,512]{1,0:T(8,128)}, bf16[1024,512]{1,0:T(8,128)(2,1)}, bf16[1024,512]{1,0:T(8,128)(2,1)}, f32[8,1024]{1,0:T(8,128)S(1)}, /*index=5*/f32[2,512]{1,0:T(2,128)S(1)}) custom-call(s32[4]{0:T(128)S(1)} %bitcast.76, s32[1]{0:T(128)} %bitcast.2.refs_0_.refs_1_, ...), custom_call_target="tpu_custom_call" | custom-call | flops 1610612736 | bytes 19656704 | tf_op jit(solution)/shard_map/gates_backward/pallas_call | solution.py:215
  203.6 5.3 %weight_grad_conv.1 = (bf16[2,384,512]{2,1,0:T(8,128)(2,1)S(1)}, bf16[2,384,512]{2,1,0:T(8,128)(2,1)}) custom-call(s32[1]{0:T(128)} %bitcast.2.refs_0_.refs_1_, bf16[1024,512]{1,0:T(8,128)(2,1)S(1)} %copy-done.25, bf16[1024,1024]{1,0:T(8,128)(2,1)} %get-tuple-element.197.refs_2_, bf16[1024,512]{1,0:T(8,128)(2,1)S(1)} %copy-done.27, bf16[1024,512]{1,0:T(8,128)(2,1)} %copy-done.28), custom_call_target="tpu_custom_call" | custom-call | flops 1610612736 | bytes 6815744 | tf_op jit(solution)/shard_map/weight_grad_conv/pallas_call | solution.py:215
  215.2 14.8 %attention_backward.2.refs_2_.refs_1_ = bf16[1024,768]{1,0:T(8,128)(2,1)} custom-call(s32[4]{0:T(128)S(1)} %bitcast.77, bf16[1024,512]{1,0:T(8,128)(2,1)S(1)} %copy-done.22, bf16[1024,512]{1,0:T(8,128)(2,1)S(1)} %copy-done.23, bf16[512,1024]{1,0:T(8,128)(2,1)} %get-tuple-element.177.refs_3_, bf16[1024,512]{1,0:T(8,128)(2,1)} %get-tuple-element.169.refs_4_, ...), custom_call_target="tpu_custom_call" | custom-call | flops 2684354560 | bytes 7929856 | tf_op jit(solution)/shard_map/attention_backward/pallas_call | solution.py:215
  232.6 3.4 collective-permute-start.17
  236.6 14.8 %attention_backward.3.refs_3_.refs_2_ = bf16[1024,768]{1,0:T(8,128)(2,1)} custom-call(s32[4]{0:T(128)S(1)} %bitcast.78, bf16[1024,512]{1,0:T(8,128)(2,1)S(1)} %copy-done.22, bf16[1024,512]{1,0:T(8,128)(2,1)S(1)} %copy-done.23, bf16[512,1024]{1,0:T(8,128)(2,1)} %get-tuple-element.177.refs_3_, bf16[1024,512]{1,0:T(8,128)(2,1)} %get-tuple-element.169.refs_4_, ...), custom_call_target="tpu_custom_call" | custom-call | flops 2684354560 | bytes 7929856 | tf_op jit(solution)/shard_map/attention_backward/pallas_call | solution.py:215
  254.2 5.8 %weight_grad_attn.1 = (bf16[2,512,512]{2,1,0:T(8,128)(2,1)S(1)}, bf16[2,512,512]{2,1,0:T(8,128)(2,1)S(1)}) custom-call(s32[1]{0:T(128)} %bitcast.2.refs_0_.refs_1_, bf16[1024,512]{1,0:T(8,128)(2,1)S(1)} %copy-done.21, bf16[1024,768]{1,0:T(8,128)(2,1)} %attention_backward.2.refs_2_.refs_1_, bf16[1024,768]{1,0:T(8,128)(2,1)} %attention_backward.3.refs_3_.refs_2_, ...), custom_call_target="tpu_custom_call" | custom-call | flops 2147483648 | bytes 8388608 | tf_op jit(solution)/shard_map/weight_grad_attn/pallas_call | solution.py:215
  260.2 8.1 %query_key_value_backward.1 = (f32[1024,512]{1,0:T(8,128)}, bf16[1024,512]{1,0:T(8,128)(2,1)S(1)}, f32[2,512]{1,0:T(2,128)S(1)}) custom-call(s32[1]{0:T(128)} %bitcast.2.refs_0_.refs_1_, bf16[1024,768]{1,0:T(8,128)(2,1)} %attention_backward.2.refs_2_.refs_1_, bf16[1024,768]{1,0:T(8,128)(2,1)} %attention_backward.3.refs_3_.refs_2_, ...), custom_call_target="tpu_custom_call" | custom-call | flops 1610612736 | bytes 12611584 | tf_op jit(solution)/shard_map/query_key_value_backward/pallas_call | solution.py:215
  269.3 1.9 collective-permute-start.23
  271.2 3.7 collective-permute-done.20
  278.0 5.8 %weight_grad_shrink.1 = (bf16[2,512,512]{2,1,0:T(8,128)(2,1)S(1)}, bf16[2,512,512]{2,1,0:T(8,128)(2,1)S(1)}) custom-call(s32[1]{0:T(128)} %bitcast.2.refs_0_.refs_1_, bf16[1024,2048]{1,0:T(8,128)(2,1)} %get-tuple-element.218.refs_1_, bf16[1024,512]{1,0:T(8,128)(2,1)S(1)} %get-tuple-element.226.refs_2_), custom_call_target="tpu_custom_call" | custom-call | flops 2147483648 | bytes 7340032 | tf_op jit(solution)/shard_map/weight_grad_shrink/pallas_call | solution.py:215
  286.7 13.0 %feed_forward_backward.1 = (f32[1024,512]{1,0:T(8,128)}, bf16[1024,2048]{1,0:T(8,128)(2,1)}, f32[2,512]{1,0:T(2,128)S(1)}) custom-call(s32[1]{0:T(128)} %bitcast.2.refs_0_.refs_1_, f32[1024,512]{1,0:T(8,128)} %get-tuple-element.216.refs_1_, bf16[1024,512]{1,0:T(8,128)(2,1)S(1)} %get-tuple-element.226.refs_2_, bf16[1024,512]{1,0:T(8,128)(2,1)S(1)} %copy-done.18, ...), custom_call_target="tpu_custom_call" | custom-call | flops 4294967296 | bytes 18903040 | tf_op jit(solution)/shard_map/feed_forward_backward/pallas_call | solution.py:183
  299.8 4.1 concatenate.96
  306.1 2.2 add_convert_fusion.3
  310.7 1.9 add_convert_fusion.20
  312.6 2.0 add_convert_fusion.2
  314.6 5.6 %weight_grad_expand.1 = (bf16[2,512,512]{2,1,0:T(8,128)(2,1)S(1)}, bf16[2,512,512]{2,1,0:T(8,128)(2,1)S(1)}) custom-call(s32[1]{0:T(128)} %bitcast.2.refs_0_.refs_1_, bf16[1024,512]{1,0:T(8,128)(2,1)S(1)} %copy-done.30, bf16[1024,2048]{1,0:T(8,128)(2,1)} %get-tuple-element.236.refs_2_), custom_call_target="tpu_custom_call" | custom-call | flops 2147483648 | bytes 7340032 | tf_op jit(solution)/shard_map/weight_grad_expand/pallas_call | solution.py:215
  321.2 2.0 collective-permute-start.30
  325.2 20.7 %collective-permute-done.36 = bf16[1,192,512]{2,1,0:T(8,128)(2,1)} collective-permute-done((bf16[1,192,512]{2,1,0:T(8,128)(2,1)S(1)}, bf16[1,192,512]{2,1,0:T(8,128)(2,1)}, u32[]{:S(2)}, u32[]{:S(2)}) %collective-permute-start.36) | collective-permute-done | bytes 196640 | tf_op jit(solution)/shard_map/ppermute | solution.py:1063
  346.0 2.0 add_convert_fusion.1
  352.9 1.9 maximum_select_fusion.4.refs_0_.refs_1_
  354.8 3.5 adam_conv.1
  358.4 2.8 maximum_select_fusion.refs_0_.refs_1_
  361.2 6.5 %adam_late.1 = (f32[2,128,2048]{2,1,0:T(8,128)}, f32[2,128,2048]{2,1,0:T(8,128)}, f32[2,128,2048]{2,1,0:T(8,128)}, f32[2,512,512]{2,1,0:T(8,128)}, f32[2,512,512]{2,1,0:T(8,128)}, /*index=5*/f32[2,512,512]{2,1,0:T(8,128)}) custom-call(bf16[1024,512]{1,0:T(8,128)(2,1)} %maximum_select_fusion.refs_0_.refs_1_, ...), custom_call_target="tpu_custom_call" | custom-call | flops 5242880 | bytes 13631488 | tf_op jit(solution)/shard_map/adam_late/pallas_call | solution.py:1242
  369.9 3.6 collective-permute-start.38
  374.8 2.1 collective-permute-done.31
  380.0 4.3 collective-permute-done.38
  384.3 5.2 %collective-permute-done.39 = bf16[1,256,512]{2,1,0:T(8,128)(2,1)S(1)} collective-permute-done((bf16[1,256,512]{2,1,0:T(8,128)(2,1)S(1)}, bf16[1,256,512]{2,1,0:T(8,128)(2,1)S(1)}, u32[]{:S(2)}, u32[]{:S(2)}) %collective-permute-start.39) | collective-permute-done | bytes 262176 | tf_op jit(solution)/shard_map/ppermute | solution.py:1063
  390.6 4.2 collective-permute-done.37
  396.9 10.7 %collective-permute-done.41 = bf16[1,256,512]{2,1,0:T(8,128)(2,1)S(1)} collective-permute-done((bf16[1,256,512]{2,1,0:T(8,128)(2,1)S(1)}, bf16[1,256,512]{2,1,0:T(8,128)(2,1)S(1)}, u32[]{:S(2)}, u32[]{:S(2)}) %collective-permute-start.41) | collective-permute-done | bytes 262176 | tf_op jit(solution)/shard_map/ppermute | solution.py:1063
  409.3 4.9 %adam_attn.1 = (f32[128,1536]{1,0:T(8,128)}, f32[128,1536]{1,0:T(8,128)}, f32[128,1536]{1,0:T(8,128)}, f32[128,512]{1,0:T(8,128)}, f32[128,512]{1,0:T(8,128)}, /*index=5*/f32[128,512]{1,0:T(8,128)}) custom-call(bf16[512,512]{1,0:T(8,128)(2,1)} %maximum_select_fusion.2.refs_0_.refs_1_, bf16[512,512]{1,0:T(8,128)(2,1)} %maximum_select_fusion.2.refs_0_.refs_1_, ...), custom_call_target="tpu_custom_call" | custom-call | flops 3932160 | bytes 6815744 | tf_op jit(solution)/shard_map/adam_attn/pallas_call | solution.py:1242
  417.6 4.5 %adam_shrink.1 = (f32[2,512,512]{2,1,0:T(8,128)}, f32[2,512,512]{2,1,0:T(8,128)}, f32[2,512,512]{2,1,0:T(8,128)}) custom-call(bf16[512,512]{1,0:T(8,128)(2,1)} %maximum_select_fusion.3.refs_0_, f32[2,512,512]{2,1,0:T(8,128)} %refs_1_.12, f32[2,512,512]{2,1,0:T(8,128)} %refs_2_.8, ...), custom_call_target="tpu_custom_call", output_to_operand_aliasing={{0}: (4, {}), {1}: (5, {}), {2}: (6, {})} | custom-call | flops 5242880 | bytes 6815744 | tf_op jit(solution)/shard_map/adam_shrink/pallas_call | solution.py:1211
  423.2 4.6 %adam_expand.1 = (f32[2,128,2048]{2,1,0:T(8,128)}, f32[2,128,2048]{2,1,0:T(8,128)}, f32[2,128,2048]{2,1,0:T(8,128)}) custom-call(bf16[528,512]{1,0:T(8,128)(2,1)} %copy-done.36, f32[2,128,2048]{2,1,0:T(8,128)} %refs_1_.13, f32[2,128,2048]{2,1,0:T(8,128)} %refs_2_.9, ...), custom_call_target="tpu_custom_call", output_to_operand_aliasing={{0}: (4, {}), {1}: (5, {}), {2}: (6, {})} | custom-call | flops 5242880 | bytes 6815744 | tf_op jit(solution)/shard_map/adam_expand/pallas_call | solution.py:1211
  (267 shorter events, 77.3 us)
Async XLA Ops:
  4.7 11.2 %collective-permute-start = (bf16[44,128]{1,0:T(8,128)(2,1)S(1)}, bf16[44,128]{1,0:T(8,128)(2,1)S(1)}, u32[]{:S(2)}, u32[]{:S(2)}) collective-permute-start(bf16[44,128]{1,0:T(8,128)(2,1)S(1)} %pad_maximum_fusion.3), channel_id=1, source_target_pairs={{0,2},{1,3},{2,0},{3,1},{4,6},{5,7},{6,4},{7,5},{8,10},{9,11},{10,... | collective-permute-start | bytes 33800 | tf_op jit(solution)/shard_map/ppermute | solution.py:1063
  7.7 8.3 %collective-permute-start.1 = (bf16[44,128]{1,0:T(8,128)(2,1)S(1)}, bf16[44,128]{1,0:T(8,128)(2,1)S(1)}, u32[]{:S(2)}, u32[]{:S(2)}) collective-permute-start(bf16[44,128]{1,0:T(8,128)(2,1)S(1)} %pad_maximum_fusion.3), channel_id=1, source_target_pairs={{0,1},{1,0},{2,3},{3,2},{4,5},{5,4},{6,7},{7,6},{8,9},{9,8},{10,11... | collective-permute-start | bytes 33800 | tf_op jit(solution)/shard_map/ppermute | solution.py:1063
  7.7 25.9 %collective-permute-start.3 = (bf16[1024,512]{1,0:T(8,128)(2,1)}, bf16[1024,512]{1,0:T(8,128)(2,1)}, u32[]{:S(2)}, u32[]{:S(2)}) collective-permute-start(bf16[1024,512]{1,0:T(8,128)(2,1)} %pack_early.1.refs_3_.refs_6_), channel_id=1, source_target_pairs={{0,2},{1,3},{2,0},{3,1},{4,6},{5,7},{6,4},{7,5},{8,10},{9,11},{10,... | collective-permute-start | bytes 3145736 | tf_op jit(solution)/shard_map/ppermute | solution.py:1063
  7.8 26.1 %collective-permute-start.4 = (bf16[1024,512]{1,0:T(8,128)(2,1)}, bf16[1024,512]{1,0:T(8,128)(2,1)}, u32[]{:S(2)}, u32[]{:S(2)}) collective-permute-start(bf16[1024,512]{1,0:T(8,128)(2,1)} %pack_early.1.refs_3_.refs_6_), channel_id=1, source_target_pairs={{0,1},{1,0},{2,3},{3,2},{4,5},{5,4},{6,7},{7,6},{8,9},{9,8},{10,11... | collective-permute-start | bytes 3145736 | tf_op jit(solution)/shard_map/ppermute | solution.py:1063
  15.8 1.2 collective-permute-start.2
  17.1 69.4 %copy-start.15 = (f32[4,32,128]{2,1,0:T(8,128)}, f32[4,32,128]{2,1,0:T(8,128)S(1)}, u32[]{:S(2)}) copy-start(f32[4,32,128]{2,1,0:T(8,128)S(1)} %slice_bitcast_fusion.refs_5_.refs_7_) | copy-start | bytes 196612
  33.6 2.9 collective-permute-start.5
  33.6 16.2 %collective-permute-start.6 = (bf16[512,512]{1,0:T(8,128)(2,1)S(1)}, bf16[512,512]{1,0:T(8,128)(2,1)S(1)}, u32[]{:S(2)}, u32[]{:S(2)}) collective-permute-start(bf16[512,512]{1,0:T(8,128)(2,1)S(1)} %pack_attn.1.refs_5_.refs_6_.refs_13_), channel_id=1, source_target_pairs={{0,2},{1,3},{2,0},{3,1},{4,6},{5,7},{6,4},{7,5},{8,10},{9,11},{10,... | collective-permute-start | bytes 1572872 | tf_op jit(solution)/shard_map/ppermute | solution.py:1063
  49.8 1.9 collective-permute-start.8
  49.9 2.5 collective-permute-start.7
  50.3 11.2 %collective-permute-start.9 = (bf16[384,512]{1,0:T(8,128)(2,1)S(1)}, bf16[384,512]{1,0:T(8,128)(2,1)S(1)}, u32[]{:S(2)}, u32[]{:S(2)}) collective-permute-start(bf16[384,512]{1,0:T(8,128)(2,1)S(1)} %copy-done.5), channel_id=1, source_target_pairs={{0,2},{1,3},{2,0},{3,1},{4,6},{5,7},{6,4},{7,5},{8,10},{9,11},{10,... | collective-permute-start | bytes 1179656 | tf_op jit(solution)/shard_map/ppermute | solution.py:1063
  61.4 43.7 %collective-permute-start.12 = (bf16[1024,512]{1,0:T(8,128)(2,1)}, bf16[1024,512]{1,0:T(8,128)(2,1)}, u32[]{:S(2)}, u32[]{:S(2)}) collective-permute-start(bf16[1024,512]{1,0:T(8,128)(2,1)} %pack_late.1.refs_11_), channel_id=1, source_target_pairs={{0,2},{1,3},{2,0},{3,1},{4,6},{5,7},{6,4},{7,5},{8,10},{9,11},{10,... | collective-permute-start | bytes 3145736 | tf_op jit(solution)/shard_map/ppermute | solution.py:1063
  61.9 2.4 collective-permute-start.11
  61.9 2.4 collective-permute-start.10
  105.2 16.9 %collective-permute-start.13 = (bf16[1024,512]{1,0:T(8,128)(2,1)}, bf16[1024,512]{1,0:T(8,128)(2,1)S(1)}, u32[]{:S(2)}, u32[]{:S(2)}) collective-permute-start(bf16[1024,512]{1,0:T(8,128)(2,1)} %pack_late.1.refs_11_), channel_id=1, source_target_pairs={{0,1},{1,0},{2,3},{3,2},{4,5},{5,4},{6,7},{7,6},{8,9},{9,8},{10,11... | collective-permute-start | bytes 3145736 | tf_op jit(solution)/shard_map/ppermute | solution.py:1063
  105.2 16.9 %collective-permute-start.14 = (bf16[1024,512]{1,0:T(8,128)(2,1)}, bf16[1024,512]{1,0:T(8,128)(2,1)S(1)}, u32[]{:S(2)}, u32[]{:S(2)}) collective-permute-start(bf16[1024,512]{1,0:T(8,128)(2,1)} %collective-permute-done.12.refs_12_), channel_id=1, source_target_pairs={{0,1},{1,0},{2,3},{3,2},{4,5},{5,4},{6,7},{7,6},{8,9},{9,8},{10,11... | collective-permute-start | bytes 3145736 | tf_op jit(solution)/shard_map/ppermute | solution.py:1063
  150.3 15.1 %all-to-all-start.1 = ((f32[32,2,512]{2,1,0:T(2,128)}), f32[32,2,512]{2,1,0:T(2,128)S(1)}, u32[]{:S(2)}, u32[]{:S(2)}) async-start(f32[32,2,512]{2,1,0:T(2,128)} %broadcast_in_dim.17), calls=%async_computation.1 | async-start | bytes 262144 | tf_op jit(solution)/shard_map/all_to_all | solution.py:1151
  165.4 20.1 %collective-permute-start.15 = (bf16[2,1024,512]{2,1,0:T(8,128)(2,1)}, bf16[2,1024,512]{2,1,0:T(8,128)(2,1)}, u32[]{:S(2)}, u32[]{:S(2)}) collective-permute-start(bf16[2,1024,512]{2,1,0:T(8,128)(2,1)} %get-tuple-element.190), channel_id=1, source_target_pairs={{0,1},{1,0},{2,3},{3,2},{4,5},{5,4},{6,7},{7,6},{8,9},{9,8},{10,11... | collective-permute-start | bytes 6291464 | tf_op jit(solution)/shard_map/ppermute | solution.py:1063
  188.0 43.1 %collective-permute-start.16 = (bf16[1,1024,512]{2,1,0:T(8,128)(2,1)}, bf16[1,1024,512]{2,1,0:T(8,128)(2,1)}, u32[]{:S(2)}, u32[]{:S(2)}) collective-permute-start(bf16[1,1024,512]{2,1,0:T(8,128)(2,1)} %add_convert_fusion), channel_id=1, source_target_pairs={{0,2},{1,3},{2,0},{3,1},{4,6},{5,7},{6,4},{7,5},{8,10},{9,11},{10,... | collective-permute-start | bytes 3145736 | tf_op jit(solution)/shard_map/ppermute | solution.py:1063
  209.0 21.0 %collective-permute-start.18 = (bf16[2,384,512]{2,1,0:T(8,128)(2,1)}, bf16[2,384,512]{2,1,0:T(8,128)(2,1)}, u32[]{:S(2)}, u32[]{:S(2)}) collective-permute-start(bf16[2,384,512]{2,1,0:T(8,128)(2,1)} %get-tuple-element.200), channel_id=1, source_target_pairs={{0,1},{1,0},{2,3},{3,2},{4,5},{5,4},{6,7},{7,6},{8,9},{9,8},{10,11... | collective-permute-start | bytes 2359304 | tf_op jit(solution)/shard_map/ppermute | solution.py:1063
  231.1 20.4 %collective-permute-start.19 = (bf16[1,384,512]{2,1,0:T(8,128)(2,1)S(1)}, bf16[1,384,512]{2,1,0:T(8,128)(2,1)S(1)}, u32[]{:S(2)}, u32[]{:S(2)}) collective-permute-start(bf16[1,384,512]{2,1,0:T(8,128)(2,1)S(1)} %add_convert_fusion.8), channel_id=1, source_target_pairs={{0,2},{1,3},{2,0},{3,1},{4,6},{5,7},{6,4},{7,5},{8,10},{9,11},{10,... | collective-permute-start | bytes 1179656 | tf_op jit(solution)/shard_map/ppermute | solution.py:1063
  232.6 20.1 %collective-permute-start.17 = (bf16[1,512,512]{2,1,0:T(8,128)(2,1)S(1)}, bf16[1,512,512]{2,1,0:T(8,128)(2,1)S(1)}, u32[]{:S(2)}, u32[]{:S(2)}) collective-permute-start(bf16[1,512,512]{2,1,0:T(8,128)(2,1)S(1)} %add_convert_fusion.7), channel_id=1, source_target_pairs={{0,4},{4,0},{8,12},{12,8},{16,20},{20,16},{24,28},{28,24},{1,5},{5... | collective-permute-start | bytes 1572872 | tf_op jit(solution)/shard_map/ppermute | solution.py:1063
  252.6 15.7 %collective-permute-start.21 = (bf16[1,192,512]{2,1,0:T(8,128)(2,1)S(1)}, bf16[1,192,512]{2,1,0:T(8,128)(2,1)S(1)}, u32[]{:S(2)}, u32[]{:S(2)}) collective-permute-start(bf16[1,192,512]{2,1,0:T(8,128)(2,1)S(1)} %add_convert_fusion.24), channel_id=1, source_target_pairs={{0,4},{4,0},{8,12},{12,8},{16,20},{20,16},{24,28},{28,24},{1,5},{5... | collective-permute-start | bytes 589832 | tf_op jit(solution)/shard_map/ppermute | solution.py:1063
  260.0 16.9 %collective-permute-start.22 = (bf16[2,512,512]{2,1,0:T(8,128)(2,1)S(1)}, bf16[2,512,512]{2,1,0:T(8,128)(2,1)S(1)}, u32[]{:S(2)}, u32[]{:S(2)}) collective-permute-start(bf16[2,512,512]{2,1,0:T(8,128)(2,1)S(1)} %get-tuple-element.213), channel_id=1, source_target_pairs={{0,1},{1,0},{2,3},{3,2},{4,5},{5,4},{6,7},{7,6},{8,9},{9,8},{10,11... | collective-permute-start | bytes 3145736 | tf_op jit(solution)/shard_map/ppermute | solution.py:1063
  260.1 14.8 %collective-permute-start.20 = (bf16[1,512,512]{2,1,0:T(8,128)(2,1)S(1)}, bf16[1,512,512]{2,1,0:T(8,128)(2,1)S(1)}, u32[]{:S(2)}, u32[]{:S(2)}) collective-permute-start(bf16[1,512,512]{2,1,0:T(8,128)(2,1)S(1)} %add_convert_fusion.6), channel_id=1, source_target_pairs={{0,8},{4,12},{8,0},{12,4},{16,24},{20,28},{24,16},{28,20},{1,9},{5... | collective-permute-start | bytes 1572872 | tf_op jit(solution)/shard_map/ppermute | solution.py:1063
  269.3 14.6 %collective-permute-start.23 = (bf16[1,192,512]{2,1,0:T(8,128)(2,1)S(1)}, bf16[1,192,512]{2,1,0:T(8,128)(2,1)S(1)}, u32[]{:S(2)}, u32[]{:S(2)}) collective-permute-start(bf16[1,192,512]{2,1,0:T(8,128)(2,1)S(1)} %add_convert_fusion.23), channel_id=1, source_target_pairs={{0,8},{4,12},{8,0},{12,4},{16,24},{20,28},{24,16},{28,20},{1,9},{5... | collective-permute-start | bytes 589832 | tf_op jit(solution)/shard_map/ppermute | solution.py:1063
  275.8 30.3 %collective-permute-start.24 = (bf16[1,512,512]{2,1,0:T(8,128)(2,1)}, bf16[1,512,512]{2,1,0:T(8,128)(2,1)}, u32[]{:S(2)}, u32[]{:S(2)}) collective-permute-start(bf16[1,512,512]{2,1,0:T(8,128)(2,1)} %add_convert_fusion.5), channel_id=1, source_target_pairs={{0,16},{4,20},{8,24},{12,28},{16,0},{20,4},{24,8},{28,12},{1,17},{... | collective-permute-start | bytes 1572872 | tf_op jit(solution)/shard_map/ppermute | solution.py:1063
  283.9 25.8 %collective-permute-start.27 = (bf16[1,192,512]{2,1,0:T(8,128)(2,1)S(1)}, bf16[1,192,512]{2,1,0:T(8,128)(2,1)}, u32[]{:S(2)}, u32[]{:S(2)}) collective-permute-start(bf16[1,192,512]{2,1,0:T(8,128)(2,1)S(1)} %add_convert_fusion.22), channel_id=1, source_target_pairs={{0,16},{4,20},{8,24},{12,28},{16,0},{20,4},{24,8},{28,12},{1,17},{... | collective-permute-start | bytes 589832 | tf_op jit(solution)/shard_map/ppermute | solution.py:1063
  285.8 26.8 %collective-permute-start.26 = (bf16[2,512,512]{2,1,0:T(8,128)(2,1)S(1)}, bf16[2,512,512]{2,1,0:T(8,128)(2,1)}, u32[]{:S(2)}, u32[]{:S(2)}) collective-permute-start(bf16[2,512,512]{2,1,0:T(8,128)(2,1)S(1)} %get-tuple-element.224), channel_id=1, source_target_pairs={{0,1},{1,0},{2,3},{3,2},{4,5},{5,4},{6,7},{7,6},{8,9},{9,8},{10,11... | collective-permute-start | bytes 3145736 | tf_op jit(solution)/shard_map/ppermute | solution.py:1063
  285.8 24.9 %collective-permute-start.25 = (bf16[1,512,512]{2,1,0:T(8,128)(2,1)}, bf16[1,512,512]{2,1,0:T(8,128)(2,1)}, u32[]{:S(2)}, u32[]{:S(2)}) collective-permute-start(bf16[1,512,512]{2,1,0:T(8,128)(2,1)} %add_convert_fusion.4), channel_id=1, source_target_pairs={{0,2},{1,3},{2,0},{3,1},{4,6},{5,7},{6,4},{7,5},{8,10},{9,11},{10,... | collective-permute-start | bytes 1572872 | tf_op jit(solution)/shard_map/ppermute | solution.py:1063
  320.2 25.8 %copy-start.44 = (bf16[2,16,512]{2,1,0:T(8,128)(2,1)S(1)}, bf16[2,16,512]{2,1,0:T(8,128)(2,1)}, u32[]{:S(2)}) copy-start(bf16[2,16,512]{2,1,0:T(8,128)(2,1)} %get-tuple-element.292) | copy-start | bytes 98308
  321.2 24.8 %collective-permute-start.28 = (bf16[2,528,512]{2,1,0:T(8,128)(2,1)}, bf16[2,528,512]{2,1,0:T(8,128)(2,1)}, u32[]{:S(2)}, u32[]{:S(2)}) collective-permute-start(bf16[2,528,512]{2,1,0:T(8,128)(2,1)} %pad_maximum_fusion), channel_id=1, source_target_pairs={{0,1},{1,0},{2,3},{3,2},{4,5},{5,4},{6,7},{7,6},{8,9},{9,8},{10,11... | collective-permute-start | bytes 3244040 | tf_op jit(solution)/shard_map/ppermute | solution.py:1063
  321.2 24.7 %collective-permute-start.30 = (bf16[1,512,512]{2,1,0:T(8,128)(2,1)}, bf16[1,512,512]{2,1,0:T(8,128)(2,1)}, u32[]{:S(2)}, u32[]{:S(2)}) collective-permute-start(bf16[1,512,512]{2,1,0:T(8,128)(2,1)} %add_convert_fusion.3), channel_id=1, source_target_pairs={{0,4},{4,0},{8,12},{12,8},{16,20},{20,16},{24,28},{28,24},{1,5},{5... | collective-permute-start | bytes 1572872 | tf_op jit(solution)/shard_map/ppermute | solution.py:1063
  323.2 22.7 %collective-permute-start.34 = (bf16[1,512,512]{2,1,0:T(8,128)(2,1)}, bf16[1,512,512]{2,1,0:T(8,128)(2,1)}, u32[]{:S(2)}, u32[]{:S(2)}) collective-permute-start(bf16[1,512,512]{2,1,0:T(8,128)(2,1)} %add_convert_fusion.2), channel_id=1, source_target_pairs={{0,2},{1,3},{2,0},{3,1},{4,6},{5,7},{6,4},{7,5},{8,10},{9,11},{10,... | collective-permute-start | bytes 1572872 | tf_op jit(solution)/shard_map/ppermute | solution.py:1063
  323.2 22.7 %collective-permute-start.32 = (bf16[1,256,512]{2,1,0:T(8,128)(2,1)}, bf16[1,256,512]{2,1,0:T(8,128)(2,1)}, u32[]{:S(2)}, u32[]{:S(2)}) collective-permute-start(bf16[1,256,512]{2,1,0:T(8,128)(2,1)} %add_convert_fusion.20), channel_id=1, source_target_pairs={{0,4},{4,0},{8,12},{12,8},{16,20},{20,16},{24,28},{28,24},{1,5},{5... | collective-permute-start | bytes 786440 | tf_op jit(solution)/shard_map/ppermute | solution.py:1063
  323.8 22.2 %collective-permute-start.36 = (bf16[1,192,512]{2,1,0:T(8,128)(2,1)S(1)}, bf16[1,192,512]{2,1,0:T(8,128)(2,1)}, u32[]{:S(2)}, u32[]{:S(2)}) collective-permute-start(bf16[1,192,512]{2,1,0:T(8,128)(2,1)S(1)} %add_convert_fusion.21), channel_id=1, source_target_pairs={{0,4},{4,0},{8,12},{12,8},{16,20},{20,16},{24,28},{28,24},{1,5},{5... | collective-permute-start | bytes 589832 | tf_op jit(solution)/shard_map/ppermute | solution.py:1063
  348.0 19.7 %collective-permute-start.29 = (bf16[1,528,512]{2,1,0:T(8,128)(2,1)}, bf16[1,528,512]{2,1,0:T(8,128)(2,1)}, u32[]{:S(2)}, u32[]{:S(2)}) collective-permute-start(bf16[1,528,512]{2,1,0:T(8,128)(2,1)} %add_convert_fusion.1), channel_id=1, source_target_pairs={{0,2},{1,3},{2,0},{3,1},{4,6},{5,7},{6,4},{7,5},{8,10},{9,11},{10,... | collective-permute-start | bytes 1622024 | tf_op jit(solution)/shard_map/ppermute | solution.py:1063
  350.1 19.8 %collective-permute-start.35 = (bf16[1,256,512]{2,1,0:T(8,128)(2,1)}, bf16[1,256,512]{2,1,0:T(8,128)(2,1)}, u32[]{:S(2)}, u32[]{:S(2)}) collective-permute-start(bf16[1,256,512]{2,1,0:T(8,128)(2,1)} %add_convert_fusion.17), channel_id=1, source_target_pairs={{0,4},{4,0},{8,12},{12,8},{16,20},{20,16},{24,28},{28,24},{1,5},{5... | collective-permute-start | bytes 786440 | tf_op jit(solution)/shard_map/ppermute | solution.py:1063
  352.9 17.0 %collective-permute-start.33 = (bf16[1,256,512]{2,1,0:T(8,128)(2,1)S(1)}, bf16[1,256,512]{2,1,0:T(8,128)(2,1)S(1)}, u32[]{:S(2)}, u32[]{:S(2)}) collective-permute-start(bf16[1,256,512]{2,1,0:T(8,128)(2,1)S(1)} %add_convert_fusion.19), channel_id=1, source_target_pairs={{0,8},{4,12},{8,0},{12,4},{16,24},{20,28},{24,16},{28,20},{1,9},{5... | collective-permute-start | bytes 786440 | tf_op jit(solution)/shard_map/ppermute | solution.py:1063
  369.0 7.9 %collective-permute-start.31 = (bf16[1,264,512]{2,1,0:T(8,128)(2,1)S(1)}, bf16[1,264,512]{2,1,0:T(8,128)(2,1)S(1)}, u32[]{:S(2)}, u32[]{:S(2)}) collective-permute-start(bf16[1,264,512]{2,1,0:T(8,128)(2,1)S(1)} %add_convert_fusion.12), channel_id=1, source_target_pairs={{0,4},{4,0},{8,12},{12,8},{16,20},{20,16},{24,28},{28,24},{1,5},{5... | collective-permute-start | bytes 811016 | tf_op jit(solution)/shard_map/ppermute | solution.py:1063
  369.9 14.4 %collective-permute-start.38 = (bf16[1,256,512]{2,1,0:T(8,128)(2,1)S(1)}, bf16[1,256,512]{2,1,0:T(8,128)(2,1)S(1)}, u32[]{:S(2)}, u32[]{:S(2)}) collective-permute-start(bf16[1,256,512]{2,1,0:T(8,128)(2,1)S(1)} %add_convert_fusion.18), channel_id=1, source_target_pairs={{0,16},{4,20},{8,24},{12,28},{16,0},{20,4},{24,8},{28,12},{1,17},{... | collective-permute-start | bytes 786440 | tf_op jit(solution)/shard_map/ppermute | solution.py:1063
  374.7 14.8 %collective-permute-start.39 = (bf16[1,256,512]{2,1,0:T(8,128)(2,1)S(1)}, bf16[1,256,512]{2,1,0:T(8,128)(2,1)S(1)}, u32[]{:S(2)}, u32[]{:S(2)}) collective-permute-start(bf16[1,256,512]{2,1,0:T(8,128)(2,1)S(1)} %add_convert_fusion.16), channel_id=1, source_target_pairs={{0,8},{4,12},{8,0},{12,4},{16,24},{20,28},{24,16},{28,20},{1,9},{5... | collective-permute-start | bytes 786440 | tf_op jit(solution)/shard_map/ppermute | solution.py:1063
  378.2 16.6 %collective-permute-start.37 = (bf16[1,264,512]{2,1,0:T(8,128)(2,1)S(1)}, bf16[1,264,512]{2,1,0:T(8,128)(2,1)S(1)}, u32[]{:S(2)}, u32[]{:S(2)}) collective-permute-start(bf16[1,264,512]{2,1,0:T(8,128)(2,1)S(1)} %add_convert_fusion.11), channel_id=1, source_target_pairs={{0,8},{4,12},{8,0},{12,4},{16,24},{20,28},{24,16},{28,20},{1,9},{5... | collective-permute-start | bytes 811016 | tf_op jit(solution)/shard_map/ppermute | solution.py:1063
  389.5 6.4 %collective-permute-start.42 = (bf16[1,256,512]{2,1,0:T(8,128)(2,1)S(1)}, bf16[1,256,512]{2,1,0:T(8,128)(2,1)S(1)}, u32[]{:S(2)}, u32[]{:S(2)}) collective-permute-start(bf16[1,256,512]{2,1,0:T(8,128)(2,1)S(1)} %add_convert_fusion.15), channel_id=1, source_target_pairs={{0,4},{4,0},{8,12},{12,8},{16,20},{20,16},{24,28},{28,24},{1,5},{5... | collective-permute-start | bytes 786440 | tf_op jit(solution)/shard_map/ppermute | solution.py:1063
  390.5 17.1 %collective-permute-start.41 = (bf16[1,256,512]{2,1,0:T(8,128)(2,1)S(1)}, bf16[1,256,512]{2,1,0:T(8,128)(2,1)S(1)}, u32[]{:S(2)}, u32[]{:S(2)}) collective-permute-start(bf16[1,256,512]{2,1,0:T(8,128)(2,1)S(1)} %add_convert_fusion.14), channel_id=1, source_target_pairs={{0,16},{4,20},{8,24},{12,28},{16,0},{20,4},{24,8},{28,12},{1,17},{... | collective-permute-start | bytes 786440 | tf_op jit(solution)/shard_map/ppermute | solution.py:1063
  394.9 19.4 %collective-permute-start.40 = (bf16[1,264,512]{2,1,0:T(8,128)(2,1)S(1)}, bf16[1,264,512]{2,1,0:T(8,128)(2,1)S(1)}, u32[]{:S(2)}, u32[]{:S(2)}) collective-permute-start(bf16[1,264,512]{2,1,0:T(8,128)(2,1)S(1)} %add_convert_fusion.10), channel_id=1, source_target_pairs={{0,16},{4,20},{8,24},{12,28},{16,0},{20,4},{24,8},{28,12},{1,17},{... | collective-permute-start | bytes 811016 | tf_op jit(solution)/shard_map/ppermute | solution.py:1063
  407.7 8.9 %collective-permute-start.44 = (bf16[1,256,512]{2,1,0:T(8,128)(2,1)S(1)}, bf16[1,256,512]{2,1,0:T(8,128)(2,1)S(1)}, u32[]{:S(2)}, u32[]{:S(2)}) collective-permute-start(bf16[1,256,512]{2,1,0:T(8,128)(2,1)S(1)} %add_convert_fusion.13), channel_id=1, source_target_pairs={{0,4},{4,0},{8,12},{12,8},{16,20},{20,16},{24,28},{28,24},{1,5},{5... | collective-permute-start | bytes 786440 | tf_op jit(solution)/shard_map/ppermute | solution.py:1063
  414.3 7.8 %collective-permute-start.43 = (bf16[1,264,512]{2,1,0:T(8,128)(2,1)S(1)}, bf16[1,264,512]{2,1,0:T(8,128)(2,1)S(1)}, u32[]{:S(2)}, u32[]{:S(2)}) collective-permute-start(bf16[1,264,512]{2,1,0:T(8,128)(2,1)S(1)} %add_convert_fusion.9), channel_id=1, source_target_pairs={{0,4},{4,0},{8,12},{12,8},{16,20},{20,16},{24,28},{28,24},{1,5},{5... | collective-permute-start | bytes 811016 | tf_op jit(solution)/shard_map/ppermute | solution.py:1063
  (55 other events, 332.1 us)

commit v3 on v2

--- a/solution.py
+++ b/solution.py
@@ -12,9 +12,11 @@
 STEP = 10
 TAPS = 32
 GAP = 16
-LIMIT = 50 * 1024 * 1024
+LIMIT = 48 * 1024 * 1024
 TILE = 256
 WINDOWS = (512, 768)
+BIG_TILE = 512
+BIG = ("ff_forward", "norm_feed_forward_and_back")
 
 norm_epsilon = 1e-05
 batch_epsilon = 1e-05
@@ -157,15 +159,19 @@
     return ref
 
 
-def block_of(kind, shape, index=None):
+def block_of(kind, shape, tile):
     if kind == "any":
         return pl.BlockSpec(memory_space=pl.ANY)
     if kind == "row":
-        return pl.BlockSpec((TILE, shape[1]), lambda i, *_: (i, 0))
+        return pl.BlockSpec((tile, shape[1]), lambda i, *_: (i, 0))
     if kind == "col":
-        return pl.BlockSpec((shape[0], TILE), lambda i, *_: (0, i))
+        return pl.BlockSpec((shape[0], tile), lambda i, *_: (0, i))
     if isinstance(kind, tuple) and kind[0] == "lane":
         return pl.BlockSpec((shape[0], kind[1]), lambda i, *_: (0, i))
+    if isinstance(kind, tuple) and kind[0] == "cut":
+        _, dim, width, at = kind
+        block = (shape[0], width) if dim else (width, shape[1])
+        return pl.BlockSpec(block, lambda i, *_: (0, at) if dim else (at, 0))
     if isinstance(kind, tuple):
         return pl.BlockSpec((None,) + shape[1:], lambda i, *_: (kind[1],) + (0,) * (len(shape) - 1))
     return pl.BlockSpec(shape, lambda i, *_: (0,) * len(shape))
@@ -174,19 +180,22 @@
 def run(
     body, name, scalars, inputs, in_specs, out_specs, outs, scratch, grid, flops, count=0, piped=False
 ):
+    tile = BIG_TILE if name in BIG else TILE
     size = sum(math.prod(o.shape) * o.dtype.itemsize for o in outs)
     size += sum(math.prod(o.shape) * o.dtype.itemsize for o in inputs)
     lead = len(scalars)
     cost = pl.CostEstimate(flops=int(flops), bytes_accessed=int(size), transcendentals=int(count))
     params = pltpu.CompilerParams(vmem_limit_bytes=LIMIT)
-    if piped:
+    if piped or grid[0] > 1:
+        inputs = [pltpu.with_memory_space_constraint(v, pltpu.HBM) for v in inputs]
+        outs = [pltpu.HBM(v.shape, v.dtype) for v in outs]
         return pl.pallas_call(
             lambda *refs: body(pl.program_id(0), *refs),
             grid_spec=pltpu.PrefetchScalarGridSpec(
                 num_scalar_prefetch=lead,
                 grid=grid,
-                in_specs=[block_of(k, v.shape) for k, v in zip(in_specs, inputs)],
-                out_specs=[block_of(k, v.shape) for k, v in zip(out_specs, outs)],
+                in_specs=[block_of(k, v.shape, tile) for k, v in zip(in_specs, inputs)],
+                out_specs=[block_of(k, v.shape, tile) for k, v in zip(out_specs, outs)],
                 scratch_shapes=scratch,
             ),
             out_shape=outs,
@@ -267,7 +276,7 @@
             out_shape(rows, ff, dtype=bf16),
         ],
         [pltpu.VMEM((d, ff), bf16), pltpu.VMEM((ff, d), bf16), pltpu.SemaphoreType.DMA((5 * len(rel),))],
-        (rows // TILE,),
+        (rows // BIG_TILE,),
         4 * rows * d * ff,
         rows * ff,
         True,
@@ -333,8 +342,9 @@
     def body(start, w_keys):
         keys = pl.ds(start, w_keys)
         same = seg_of(start + lax.broadcasted_iota(jnp.int32, (w_keys, 1), 0), e) == sq
-        for p in range(4):
-            cols = slice(128 * p, 128 * (p + 1))
+
+        def pair(p, carry):
+            cols = pl.ds(pl.multiple_of(128 * p, 128), 128)
             qp, kp, vp = q[:, cols], k[keys, cols], v[keys, cols]
             both = None
             for h in range(2):
@@ -344,11 +354,14 @@
                 top = jnp.max(s, axis=0, keepdims=True)
                 expo = jnp.exp(s - top)
                 total = col_sum(expo)
-                lse[head : head + 1, :] = top + jnp.log(total)
+                lse[pl.ds(head, 1), :] = top + jnp.log(total)
                 prob = (expo * (1.0 / total)).astype(bf16)
                 part = mm_tn(prob, jnp.where(pick, vp, zero))
                 both = part if both is None else both + part
             mixed[:, cols] = both.astype(bf16)
+            return carry
+
+        lax.fori_loop(0, 4, pair, 0, unroll=2)
 
     in_window(lo, hi, rows, body)
     x2[...] = x1[...] + mm(mixed[...], w[...])
@@ -388,9 +401,9 @@
     def body(start, w):
         qs = pl.ds(start, w)
         same = sk == seg_of(start + lax.broadcasted_iota(jnp.int32, (1, w), 1), e)
-        for p in range(pairs):
-            cols = slice(128 * p, 128 * (p + 1))
-            held = slice(128 * (base + p), 128 * (base + p + 1))
+
+        def pair(p, carry):
+            held = pl.ds(pl.multiple_of(128 * p, 128), 128)
             qp, dop = q[qs, held], do[qs, held]
             kp, vp = k[here, held], v[here, held]
             gk, gv = None, None
@@ -399,20 +412,22 @@
                 full = 2 * base + head
                 pick = low if h == 0 else jnp.logical_not(low)
                 qm, dom = jnp.where(pick, qp, zero), jnp.where(pick, dop, zero)
-                hr = slice(64 * head, 64 * (head + 1))
-                hk = slice(64 * full, 64 * (full + 1))
-                expo = jnp.exp(mm_nt(kp, qm) - lse[full : full + 1, qs])
+                hr = pl.ds(pl.multiple_of(64 * head, 64), 64)
+                expo = jnp.exp(mm_nt(kp, qm) - lse[pl.ds(full, 1), qs])
                 prob = jnp.where(same, expo, 0.0)
-                ds = (prob * (mm_nt(vp, dom) - delta[full : full + 1, qs])).astype(bf16)
+                ds = (prob * (mm_nt(vp, dom) - delta[pl.ds(full, 1), qs])).astype(bf16)
                 v_part = mm(prob.astype(bf16), dom)
                 k_part = mm(ds, qm)
-                dqt[hr, qs] += mm(kt[hk, here], ds)
+                dqt[hr, qs] += mm(kt[hr, here], ds)
                 gv = v_part if gv is None else gv + v_part
                 gk = k_part if gk is None else gk + k_part
             c, s = cs[here, :], sn[here, :]
-            gp[here, 128 * (2 * pairs + p) : 128 * (2 * pairs + p + 1)] = gv.astype(bf16)
+            gp[here, pl.ds(pl.multiple_of(128 * (2 * pairs + p), 128), 128)] = gv.astype(bf16)
             turned = gk * c - partner(gk) * s
-            gp[here, 128 * (pairs + p) : 128 * (pairs + p + 1)] = turned.astype(bf16)
+            gp[here, pl.ds(pl.multiple_of(128 * (pairs + p), 128), 128)] = turned.astype(bf16)
+            return carry
+
+        lax.fori_loop(0, pairs, pair, 0)
 
     in_window(lo, hi, rows, body)
 
@@ -427,13 +442,15 @@
 
 def attention_back(ends, q, k, kt, v, do, lse, delta, cs, sn, base, pairs):
     rows, d = q.shape
-    wide = 128 * pairs
+    wide, at = 128 * pairs, base // pairs
     return run(
         functools.partial(attention_back_body, rows=rows, pairs=pairs, base=base),
         "attention_backward",
         (ends,),
         (q, k, kt, v, do, lse, delta, cs, sn),
-        [whole(rows, d)] * 5
+        [("cut", 1, wide, at)] * 2
+        + [("cut", 0, wide, at)]
+        + [("cut", 1, wide, at)] * 2
         + [whole(HEADS, rows)] * 2
         + [whole(rows, 128)] * 2,
         [whole(rows, 3 * wide)],
@@ -642,7 +659,9 @@
     )
 
 
-def conv_back_body(t, ends, spans, gz, conv, batch, totals, norms, taps, spaced, g_glu, tap_grad, grad, *, rows):
+def conv_back_body(t, ends, spans, gz, conv, batch, totals, norms, taps, far, g_glu, tap_grad, grad, spaced, sem, *, rows):
+    arriving = pltpu.make_async_copy(far, spaced, sem.at[0])
+    arriving.start()
     e = [ends[j] for j in range(4)]
     grad[...] = jnp.zeros_like(grad)
     mean, scale, count = batch[0:1, :], batch[1:2, :], batch[2:3, :]
@@ -673,6 +692,7 @@
 
     spread_all(rows // 8, 0, spans, e, read, grad)
     slide(grad, taps, g_glu, rows, 1, True)
+    arriving.wait()
     tap_sums(grad, spaced, tap_grad, rows)
 
 
@@ -685,10 +705,14 @@
         (ends, spans),
         (gz, conv, batch, totals, norms, taps, spaced),
         [whole(rows, d), whole(rows, d), whole(3, d), whole(*totals.shape), whole(*norms.shape)]
-        + [whole(4, TAPS, 128), whole(4, far, 128)],
+        + [whole(4, TAPS, 128), "any"],
         [whole(4, far, 128), whole(4, TAPS, 128)],
         [out_shape(4, far, 128), out_shape(4, TAPS, 128)],
-        [pltpu.VMEM((4, far, 128), f32)],
+        [
+            pltpu.VMEM((4, far, 128), f32),
+            pltpu.VMEM((4, far, 128), f32),
+            pltpu.SemaphoreType.DMA((1,)),
+        ],
         (1,),
         12 * rows * d * TAPS * 40,
         rows * d,
@@ -813,7 +837,7 @@
         total = part if total is None else total + part
     fourth = third + 0.5 * total
     last, last_scale = normalize(fourth)
-    keep = t * TILE + lax.broadcasted_iota(jnp.int32, (TILE, 1), 0) < ends[3]
+    keep = t * BIG_TILE + lax.broadcasted_iota(jnp.int32, (BIG_TILE, 1), 0) < ends[3]
     y[...] = jnp.where(keep, last * norms[10:11, :] + norms[11:12, :], 0.0).astype(bf16)
     g_y = jnp.where(keep, cot[...].astype(f32), 0.0)
     sums[0:1, :] += col_sum(g_y * last)
@@ -870,10 +894,10 @@
             pltpu.VMEM((d, d), bf16),
             pltpu.VMEM((d, ff), bf16),
             pltpu.VMEM((ff, d), bf16),
-            pltpu.VMEM((TILE, ff), f32),
+            pltpu.VMEM((BIG_TILE, ff), f32),
             pltpu.SemaphoreType.DMA((6 * len(rel),)),
         ],
-        (rows // TILE,),
+        (rows // BIG_TILE,),
         rows * d * (8 * ff + 4 * d),
         rows * ff,
         True,
@@ -924,10 +948,10 @@
     )
 
 
-def ff_back_body(t, me, g1, go, x, before, norms, *refs, rel, er, sr):
+def ff_back_body(t, me, g1, go, x, before, norms, qkv_sums, conv_sums, rear_sums, tap_grad, *refs, rel, er, sr, steps):
     n = len(rel)
     parts = refs[:n]
-    g_frames, g_before, sums, w_in, w_out, sems = refs[n:]
+    g_frames, g_before, small, sums, w_in, w_out, sems = refs[n:]
     copies = []
     for j, r in enumerate(rel):
         copies += column_blocks(parts[j], me[0] ^ r, w_in, er)
@@ -952,20 +976,34 @@
     sums[1:2, :] += col_sum(g_hidden)
     g_frames[...] = g1[...] + norm_back(g_hidden, norms[0:1, :], normed, scale)
 
-
-def ff_back(me, g1, go, x, before, norms, parts, rel):
+    @pl.when(t == steps - 1)
+    def _():
+        for c in range(tap_grad.shape[0]):
+            small[:TAPS, 128 * c : 128 * (c + 1)] = tap_grad[c, :, :]
+        rows = [sums[0:1, :], sums[1:2, :], qkv_sums[...], conv_sums[...], rear_sums[5:6, :]]
+        rows += [rear_sums[4:5, :], rear_sums[2:4, :], rear_sums[0:2, :]]
+        at = TAPS
+        for row in rows:
+            small[at : at + row.shape[0], :] = row
+            at += row.shape[0]
+
+
+def ff_back(me, g1, go, x, before, norms, sums, parts, rel):
     rows, d = x.shape
     ff = 4 * d
     er, sr = d // len(rel), ff // len(rel)
     return run(
-        functools.partial(ff_back_body, rel=rel, er=er, sr=sr),
+        functools.partial(ff_back_body, rel=rel, er=er, sr=sr, steps=rows // TILE),
         "feed_forward_backward",
         (me,),
-        (g1, go, x, before, norms, *parts),
-        [row_spec(d), row_spec(d), row_spec(d), row_spec(ff), whole(*norms.shape)] + anywhere(len(rel)),
-        [row_spec(d), row_spec(ff), whole(2, d)],
-        [out_shape(rows, d), out_shape(rows, ff, dtype=bf16), out_shape(2, d)],
+        (g1, go, x, before, norms, *sums, *parts),
+        [row_spec(d), row_spec(d), row_spec(d), row_spec(ff), whole(*norms.shape)]
+        + ["whole"] * len(sums)
+        + anywhere(len(rel)),
+        [row_spec(d), row_spec(ff), whole(TAPS + 12, d)],
+        [out_shape(rows, d), out_shape(rows, ff, dtype=bf16), out_shape(TAPS + 12, d)],
         [
+            pltpu.VMEM((2, d), f32),
             pltpu.VMEM((d, ff), bf16),
             pltpu.VMEM((ff, d), bf16),
             pltpu.SemaphoreType.DMA((5 * len(rel),)),
@@ -992,10 +1030,11 @@
             send[owner >> 1, pl.ds(base, height), :] = rows
 
 
-def weight_grad_body(t, me, *refs, fs, parts, n1, n2):
+def weight_grad_body(t, me, *refs, fs, parts, n1, n2, extra):
     refs = list(refs)
     first = [refs.pop(0) for _ in range(1 + parts)] if n1 else None
     second = [refs.pop(0) for _ in range(2)] if n2 else None
+    more = refs.pop(0) if extra else None
     keep, send = refs.pop(0), refs.pop(0)
     er = 512 // fs
     if n1:
@@ -1015,9 +1054,15 @@
             one(t)
         else:
             pl.when(t == 0)(lambda: one(0))
-
-
-def weight_grad(name, me, fs, first=None, second=None):
+    if extra:
+
+        @pl.when(t == 0)
+        def _():
+            tile = more[...].reshape(fs * extra, 512)
+            place_owners(me, tile, keep, send, (n1 + n2) * er, extra, fs, 0)
+
+
+def weight_grad(name, me, fs, first=None, second=None, more=None):
     inputs, specs = [], []
     n1 = n2 = parts = 0
     if first:
@@ -1034,9 +1079,14 @@
         inputs += [s, o]
         stepped = n1 in (0, n2)
         specs += [("lane", 512) if stepped else "whole", whole(rows, 512)]
-    height = (n1 + n2) * 512 // fs
+    extra = 0
+    if more is not None:
+        extra = more.shape[1]
+        inputs.append(more)
+        specs.append("whole")
+    height = (n1 + n2) * 512 // fs + extra
     return run(
-        functools.partial(weight_grad_body, fs=fs, parts=parts, n1=n1, n2=n2),
+        functools.partial(weight_grad_body, fs=fs, parts=parts, n1=n1, n2=n2, extra=extra),
         name,
         (me,),
         inputs,
@@ -1097,10 +1147,11 @@
         self.at, self.size = [zero, zero], list(keep.shape[:2])
         self.parts = [(keep, zero, zero)]
         self.stages = [("fsdp", bit, "halve") for bit in reversed(range(1, bits_of(fs)))]
-        self.stages += [("dp", bit, "add" if bit else "halve") for bit in range(bits_of(dp))]
-        self.stages.append(("dp", 0, "join"))
+        last = bits_of(dp) - 1
+        self.stages += [("dp", bit, "halve") for bit in range(last)] + [("dp", last, "add")]
+        self.stages += [("dp", bit, "join") for bit in reversed(range(last))]
         self.flight = swap(send, "fsdp", fs, 1)
-        self.whole = None
+        self.joining = None
 
     def take(self, y, r):
         shape = (self.size[0], self.size[1], 512)
@@ -1114,7 +1165,7 @@
     def advance(self):
         if not self.stages:
             return None
-        self.parts.append((self.flight, *self.at))
+        self.settle()
         axis, bit, kind = self.stages.pop(0)
         size, index = (self.fs, self.me) if axis == "fsdp" else (self.dp, self.pack)
         side = (index >> bit) & 1
@@ -1126,17 +1177,32 @@
             send = self.take(*self.at)
             self.at[dim] = base + side * self.size[dim]
         else:
-            send = self.take(*self.at)
-            self.parts = [(send, *self.at)]
+            if self.joining is None:
+                send = self.take(*self.at)
+            else:
+                send = self.whole
+            if kind == "join":
+                send = send.reshape(-1, 512)
+                self.whole, self.joining = send, side
+            else:
+                self.parts = [(send, *self.at)]
         self.flight = swap(send, axis, size, 1 << bit)
         return send
+
+    def settle(self):
+        if self.joining is None:
+            self.parts.append((self.flight, *self.at))
+        else:
+            pair = [self.whole, self.flight]
+            self.whole = jnp.where(
+                self.joining == 0, jnp.concatenate(pair, axis=0), jnp.concatenate(pair[::-1], axis=0)
+            )
 
     def result(self):
         while self.stages:
             self.advance()
-        mine, other = self.parts[0][0].reshape(-1, 512), self.flight.reshape(-1, 512)
-        pair = [jnp.concatenate([mine, other], axis=0), jnp.concatenate([other, mine], axis=0)]
-        return jnp.where((self.pack & 1) == 0, *pair)
+        self.settle()
+        return self.whole
 
 
 def after(value, *tokens):
@@ -1218,6 +1284,7 @@
         cost_estimate=pl.CostEstimate(
             flops=20 * height * width, bytes_accessed=26 * height * width, transcendentals=height * width
         ),
+        compiler_params=pltpu.CompilerParams(vmem_limit_bytes=(8 if by_row else 48) * 1024 * 1024),
         name=name,
     )(grad, *state, *into)
 
@@ -1249,6 +1316,7 @@
         cost_estimate=pl.CostEstimate(
             flops=20 * er * 512 * n, bytes_accessed=26 * (er * n + sr) * 512, transcendentals=er * 512 * n
         ),
+        compiler_params=pltpu.CompilerParams(vmem_limit_bytes=8 * 1024 * 1024),
         name=name,
     )(*inputs)
 
@@ -1410,50 +1478,47 @@
     )
     early_out = Chain(out_pair, fs, dp)
     middle.hold(out_pair[1])
-    frames_grad, g_before_zero, ff_sums = ff_back(
-        me, g_first, after(g_out_zero, out_pair[1], middle.advance()), frames, before_zero, norms, ff_zero, rel
+    sums = (qkv_sums, conv_sums, rear_sums, tap_grad)
+    frames_grad, g_before_zero, small_grad = ff_back(
+        me,
+        g_first,
+        after(g_out_zero, out_pair[1], early_out.advance()),
+        frames,
+        before_zero,
+        norms,
+        sums,
+        ff_zero,
+        rel,
     )
     for chain in (late, middle, attn, early_out):
         chain.hold(g_before_zero)
-    tokens = (late.advance(), attn.advance(), early_out.advance(), middle.advance())
-    early_in = weight_grad(
-        "weight_grad_expand", me, fs, (hidden_zero, (after(g_before_zero, *tokens),))
-    )
-    grad_norms = jnp.concatenate(
-        [
-            ff_sums,
-            qkv_sums,
-            conv_sums,
-            rear_sums[5:6],
-            rear_sums[4:5],
-            rear_sums[2:4],
-            rear_sums[0:2],
-        ]
-    )
-    grad_kernel = tap_grad.swapaxes(0, 1).reshape(TAPS, width)
-    small_grad = jnp.concatenate([grad_kernel, grad_norms], axis=0).astype(bf16)
-    small_grad = small_grad.reshape(tiny_rows, fs, dr).swapaxes(0, 1)
+    tokens = (attn.flight, early_out.flight, late.flight, middle.flight)
+    small_grad = small_grad.astype(bf16).reshape(tiny_rows, fs, dr).swapaxes(0, 1)
     small_size = tiny_rows * dr
-    small_pad = -small_size % (512 * dp)
+    small_pad = -small_size % (512 * 16)
     small_grad = jnp.pad(small_grad.reshape(fs, small_size), ((0, 0), (0, small_pad)))
-    small_grad = small_grad.reshape(fs // 2, 2, -1, 512).swapaxes(0, 1)
-    core = device & 1
-    small_pair = (
-        lax.dynamic_index_in_dim(small_grad, core, 0, False),
-        lax.dynamic_index_in_dim(small_grad, 1 - core, 0, False),
-    )
-    tail_pair = join(early_in, small_pair)
+    small_grad = small_grad.reshape(fs, -1, 512)
+    tail_pair = weight_grad(
+        "weight_grad_expand",
+        me,
+        fs,
+        (hidden_zero, (after(g_before_zero, *tokens),)),
+        None,
+        small_grad,
+    )
     tail = Chain(tail_pair, fs, dp)
-    for chain in (late, middle, attn, early_out):
-        chain.hold(tail_pair[1])
-    sent = tail.advance()
-    for chain in (late, middle, attn, early_out):
-        chain.hold(sent)
-    attn.advance()
-    early_out.advance()
-    red_late, red_conv = late.result(), middle.result()
+    attn.hold(tail_pair[1])
+    early_out.hold(tail_pair[1])
+    tail_sent = tail.advance()
     expands = (expand, expand_first, expand_second)
     shrinks = (shrink, shrink_first, shrink_second)
+
+    def hold(*chains):
+        for chain in chains:
+            chain.hold(tail_sent)
+
+    hold(late, middle, attn, early_out)
+    red_late, red_conv = late.result(), middle.result()
     new_late = adam_pair("adam_late", red_late, expands, shrinks, True, 1)
     new_conv = adam_pair(
         "adam_conv",
@@ -1462,30 +1527,14 @@
         (pointwise_out, pointwise_out_first, pointwise_out_second),
         False,
     )
-    tail.hold(new_late[0])
-    sent = tail.advance()
-    attn.hold(sent)
-    early_out.hold(sent)
-    tail.hold(attn.advance(), early_out.advance(), new_conv[0])
-    sent = tail.advance()
-    attn.hold(sent)
-    early_out.hold(sent)
-    tail.hold(attn.advance(), early_out.advance())
-    sent = tail.advance()
-    early_out.hold(sent)
-    tail.hold(early_out.advance())
     new_attn = adam_pair(
         "adam_attn",
-        after(attn.result(), sent),
+        attn.result(),
         (attend, attend_first, attend_second),
         (heads_out, heads_out_first, heads_out_second),
         False,
     )
-    tail.hold(new_attn[0])
-    sent = tail.advance()
-    red_out = after(early_out.result(), sent)
-    new_shrink = adam_single("adam_shrink", red_out, shrinks, True, 0, new_late[3:])
-    tail.hold(new_shrink[0])
+    new_shrink = adam_single("adam_shrink", early_out.result(), shrinks, True, 0, new_late[3:])
     red_in = tail.result()
     new_expand = adam_single("adam_expand", red_in, expands, False, 0, new_late[:3])
     red_small = red_in[4 * er :].reshape(-1)[:small_size].reshape(tiny_rows, dr).astype(f32)

time: 437 us -> 392 us (0.90)
  waiting for transfers between devices: 77.4 us -> 54.2 us
  local copies, waits for them, and re-layouts: 29.8 us -> 13.2 us
  other arithmetic: 42 us -> 29.3 us
  starting transfers between devices: 35.7 us -> 43.7 us
    pallas_call x8 -> x19, Pallas kernels: 63.3 us -> 197 us  [run(): pl.pallas_call(lambda *refs: body(pl.program_id(0), *refs), grid_spec=plt...]
    pallas_call x12 -> x1, Pallas kernels: 139 us -> 15.7 us  [run(): pl.pallas_call(kernel, in_specs=[pl.BlockSpec(memory_space=pltpu.SMEM)] *...]
    ppermute x45 -> x50, waiting for transfers between devices: 77.4 us -> 54.2 us  [swap(): return lax.ppermute(value, axis, [(k, k ^ mask) for k in range(size)])]
    unnamed x118 -> x125, local copies, waits for them, and re-layouts: 21.9 us -> 9.19 us
    ppermute x45 -> x50, starting transfers between devices: 33.1 us -> 41.1 us  [swap(): return lax.ppermute(value, axis, [(k, k ^ mask) for k in range(size)])]
    convert_element_type x25 -> x20, other arithmetic: 27 us -> 20.3 us  [sum_of(): return total.astype(bf16)]
    pallas_call x3, Pallas kernels: 15 us -> 8.73 us  [adam_pair(): pl.pallas_call(adam_body, grid=(n,), in_specs=specs, out_specs=[spec_a] *...]
    select_n x5 -> x10, other arithmetic: 7.04 us -> 1.7 us  [settle(): jnp.where(self.joining == 0, jnp.concatenate(pair, axis=0), jnp.concatena...]
  transfers between devices with their start and end apart: 46 -> 51, of which waited for: 16 -> 14; matrix products, arithmetic and copies ran while one was open for 10% -> 6% of each run, Pallas kernels for 44% -> 46%
where the time goes in v3:
time: 392 us; the launch traced here: 388 us
  Pallas kernels  228 us (58%)
  waiting for transfers between devices  54.2 us (14%)
  starting transfers between devices  43.7 us (11%)
  other arithmetic  29.3 us (7%)
  blocking collectives  17.4 us (4%)
  local copies, waits for them, and re-layouts  13.2 us (3%)
    pallas_call x19, Pallas kernels, run(): pl.pallas_call(lambda *refs: body(pl.program_id(0), *refs), grid_spec=plt...  197 us
    ppermute x50, waiting for transfers between devices, swap(): return lax.ppermute(value, axis, [(k, k ^ mask) for k in range(size)])  54.2 us
    ppermute x50, starting transfers between devices, swap(): return lax.ppermute(value, axis, [(k, k ^ mask) for k in range(size)])  41.1 us
    convert_element_type x20, other arithmetic, sum_of(): return total.astype(bf16)  20.3 us
    all_to_all x1, blocking collectives, from_everyone(): return lax.all_to_all(spread, axes, 0, 0, tiled=True)  17.4 us
    pallas_call x1, Pallas kernels, run(): pl.pallas_call(kernel, in_specs=[pl.BlockSpec(memory_space=pltpu.SMEM)] *...  15.7 us
    unnamed x125, local copies, waits for them, and re-layouts  9.19 us
    pallas_call x3, Pallas kernels, adam_pair(): pl.pallas_call(adam_body, grid=(n,), in_specs=specs, out_specs=[spec_a] *...  8.73 us
  transfers between devices with their start and end apart: 51, of which 14 were waited for; matrix products, arithmetic and copies ran while one was open for 6% of the time, Pallas kernels for 46%

profile of v3, /device:TPU:0, one launch (start us, length us, event | category | flops | bytes accessed | tf_op | source)
XLA Modules:
  0.0 387.9 jit_solution(14093354231703499882)
XLA Ops:
  0.7 2.7 pack_early.1.refs_3_.refs_10_
  3.4 3.0 collective-permute-start
  7.4 1.9 fusion.1
  9.3 1.8 pad_maximum_fusion
  11.2 1.9 pack_conv.1.refs_6_.refs_7_.refs_9_
  13.1 2.0 pack_attn.1.refs_5_.refs_6_.refs_13_
  15.1 2.7 pack_late.1.refs_11_
  20.3 11.9 %collective-permute-done.3.refs_4_.refs_11_ = bf16[1024,512]{1,0:T(8,128)(2,1)S(1)} collective-permute-done((bf16[1024,512]{1,0:T(8,128)(2,1)}, bf16[1024,512]{1,0:T(8,128)(2,1)S(1)}, u32[]{:S(2)}, u32[]{:S(2)}) %collective-permute-start.3) | collective-permute-done | bytes 1048608 | tf_op jit(solution)/shard_map/ppermute | solution.py:1113
  32.7 2.2 collective-permute-done.5.refs_6_.refs_13_
  35.8 11.3 %ff_forward.1 = (f32[1024,512]{1,0:T(8,128)}, bf16[1024,512]{1,0:T(8,128)(2,1)}, bf16[1024,2048]{1,0:T(8,128)(2,1)}, bf16[1024,2048]{1,0:T(8,128)(2,1)}) custom-call(s32[1]{0:T(128)} %bitcast.2.refs_0_.refs_1_, bf16[1024,512]{1,0:T(8,128)(2,1)} %refs_3_.6, f32[12,512]{1,0:T(8,128)} %bitcast.41, bf16[1024,512]{1,0:T(8,128)(2,1)} %pack_early.1.refs_3_.refs_10_, ...), custom_call_target="tpu_custom_call" | custom-call | flops 4294967296 | bytes 16801792 | tf_op jit(solution)/shard_map/ff_forward/pallas_call | solution.py:192
  50.7 8.8 %query_key_value.1 = (bf16[1024,512]{1,0:T(8,128)(2,1)}, bf16[1024,512]{1,0:T(8,128)(2,1)}, bf16[1024,512]{1,0:T(8,128)(2,1)}, bf16[1024,512]{1,0:T(8,128)(2,1)}, bf16[512,1024]{1,0:T(8,128)(2,1)}) custom-call(s32[1]{0:T(128)} %bitcast.2.refs_0_.refs_1_, f32[1024,512]{1,0:T(8,128)} %get-tuple-element.144.refs_1_.refs_5_.refs_3_, f32[12,512]{1,0:T(8,128)} %bitcast.42, ...), custom_call_target="tpu_custom_call" | custom-call | flops 1610612736 | bytes 10510336 | tf_op jit(solution)/shard_map/query_key_value/pallas_call | solution.py:192
  62.7 22.7 %attention_forward.1 = (f32[1024,512]{1,0:T(8,128)}, bf16[1024,512]{1,0:T(8,128)(2,1)}, f32[8,1024]{1,0:T(8,128)}) custom-call(s32[4]{0:T(128)S(1)} %bitcast.51, s32[1]{0:T(128)} %bitcast.2.refs_0_.refs_1_, bf16[1024,512]{1,0:T(8,128)(2,1)} %get-tuple-element.152.refs_2_.refs_1_, bf16[1024,512]{1,0:T(8,128)(2,1)} %get-tuple-element.153.refs_3_.refs_2_, ...), custom_call_target="tpu_custom_call" | custom-call | flops 2147483648 | bytes 10518528 | tf_op jit(solution)/shard_map/attention_forward/pallas_call | solution.py:192
  85.4 18.2 %gated_convolution.1 = (bf16[1024,512]{1,0:T(8,128)(2,1)}, bf16[1024,1024]{1,0:T(8,128)(2,1)}, f32[1024,512]{1,0:T(8,128)}, f32[4,1120,128]{2,1,0:T(8,128)}, f32[3,512]{1,0:T(4,128)}) custom-call(s32[4]{0:T(128)S(1)} %bitcast.52, s32[1]{0:T(128)} %bitcast.2.refs_0_.refs_1_, s32[3,128]{1,0:T(4,128)S(1)} %add_add_fusion.refs_2_.refs_1_, ...), custom_call_target="tpu_custom_call" | custom-call | flops 2147483648 | bytes 11302912 | tf_op jit(solution)/shard_map/gated_convolution/pallas_call | solution.py:192
  104.9 17.4 %all_to_all.10.refs_3_ = f32[32,3,512]{2,1,0:T(4,128)} all-to-all(f32[32,3,512]{2,1,0:T(4,128)S(1)} %broadcast_in_dim.16), channel_id=1, replica_groups=mesh['dp'=8,'fsdp'=4] {'dp','fsdp'}, dimensions={0} | all-to-all | bytes 393216 | tf_op jit(solution)/shard_map/all_to_all | solution.py:1217
  123.7 22.4 %norm_feed_forward_and_back.1 = (bf16[1024,512]{1,0:T(8,128)(2,1)}, f32[1024,512]{1,0:T(8,128)}, f32[1024,512]{1,0:T(8,128)}, bf16[1024,512]{1,0:T(8,128)(2,1)},...) custom-call(s32[4]{0:T(128)S(1)} %bitcast.53, ...), custom_call_target="tpu_custom_call" | custom-call | flops 9663676416 | bytes 29075456 | tf_op jit(solution)/shard_map/norm_feed_forward_and_back/pallas_call | solution.py:192
  147.5 2.6 all-to-all-start.1
  150.1 10.8 %weight_grad_late.1 = (bf16[2,1024,512]{2,1,0:T(8,128)(2,1)}, bf16[2,1024,512]{2,1,0:T(8,128)(2,1)}) custom-call(s32[1]{0:T(128)} %bitcast.2.refs_0_.refs_1_, bf16[1024,512]{1,0:T(8,128)(2,1)} %get-tuple-element.164.refs_1_, bf16[1024,2048]{1,0:T(8,128)(2,1)} %get-tuple-element.165.refs_2_, bf16[1024,2048]{1,0:T(8,128)(2,1)} %get-tuple-element.166.refs_3_, ...), custom_call_target="tpu_custom_call" | custom-call | flops 4294967296 | bytes 14680064 | tf_op jit(solution)/shard_map/weight_grad_late/pallas_call | solution.py:192
  162.7 15.7 %convolution_backward.1 = (f32[4,1120,128]{2,1,0:T(8,128)}, f32[4,32,128]{2,1,0:T(8,128)S(1)}) custom-call(s32[4]{0:T(128)S(1)} %bitcast.54, s32[3,128]{1,0:T(4,128)S(1)} %add_add_fusion.refs_2_.refs_1_, f32[1024,512]{1,0:T(8,128)S(1)} %copy-done.23, f32[1024,512]{1,0:T(8,128)S(1)} %copy-done.21, f32[3,512]{1,0:T(4,128)S(1)} %copy-done.24, ...), custom_call_target="tpu_custom_call" | custom-call | flops 8053063680 | bytes 9074688 | tf_op jit(solution)/shard_map/convolution_backward/pallas_call | solution.py:224
  182.3 11.5 %gates_backward.1 = (bf16[1024,1024]{1,0:T(8,128)(2,1)}, f32[1024,512]{1,0:T(8,128)}, bf16[1024,512]{1,0:T(8,128)(2,1)}, bf16[1024,512]{1,0:T(8,128)(2,1)}, f32[8,1024]{1,0:T(8,128)}, /*index=5*/f32[2,512]{1,0:T(2,128)}) custom-call(s32[4]{0:T(128)S(1)} %bitcast.55, s32[1]{0:T(128)} %bitcast.2.refs_0_.refs_1_, s32[3,128]{1,0:T(4,128)S(1)} %add_add_fusion.refs_2_.refs_1_, ...), custom_call_target="tpu_custom_call" | custom-call | flops 1610612736 | bytes 19656704 | tf_op jit(solution)/shard_map/gates_backward/pallas_call | solution.py:192
  193.9 5.8 %weight_grad_conv.1 = (bf16[2,384,512]{2,1,0:T(8,128)(2,1)}, bf16[2,384,512]{2,1,0:T(8,128)(2,1)}) custom-call(s32[1]{0:T(128)} %bitcast.2.refs_0_.refs_1_, bf16[1024,512]{1,0:T(8,128)(2,1)} %get-tuple-element.181.refs_1_, bf16[1024,1024]{1,0:T(8,128)(2,1)} %get-tuple-element.182.refs_2_, bf16[1024,512]{1,0:T(8,128)(2,1)} %get-tuple-element.183.refs_3_, ...), custom_call_target="tpu_custom_call" | custom-call | flops 1610612736 | bytes 6815744 | tf_op jit(solution)/shard_map/weight_grad_conv/pallas_call | solution.py:192
  199.8 16.5 %attention_backward.2.refs_2_.refs_1_ = bf16[1024,768]{1,0:T(8,128)(2,1)} custom-call(s32[4]{0:T(128)S(1)} %bitcast.56, bf16[1024,512]{1,0:T(8,128)(2,1)} %get-tuple-element.152.refs_2_.refs_1_, bf16[1024,512]{1,0:T(8,128)(2,1)} %get-tuple-element.153.refs_3_.refs_2_, bf16[512,1024]{1,0:T(8,128)(2,1)} %get-tuple-element.162.refs_3_, ...), custom_call_target="tpu_custom_call" | custom-call | flops 2684354560 | bytes 7929856 | tf_op jit(solution)/shard_map/attention_backward/pallas_call | solution.py:192
  221.2 16.7 %attention_backward.3.refs_3_.refs_2_ = bf16[1024,768]{1,0:T(8,128)(2,1)} custom-call(s32[4]{0:T(128)S(1)} %bitcast.57, bf16[1024,512]{1,0:T(8,128)(2,1)} %get-tuple-element.152.refs_2_.refs_1_, bf16[1024,512]{1,0:T(8,128)(2,1)} %get-tuple-element.153.refs_3_.refs_2_, bf16[512,1024]{1,0:T(8,128)(2,1)} %get-tuple-element.162.refs_3_, ...), custom_call_target="tpu_custom_call" | custom-call | flops 2684354560 | bytes 7929856 | tf_op jit(solution)/shard_map/attention_backward/pallas_call | solution.py:192
  237.9 1.9 add_convert_fusion.12
  240.9 7.2 %weight_grad_attn.1 = (bf16[2,512,512]{2,1,0:T(8,128)(2,1)}, bf16[2,512,512]{2,1,0:T(8,128)(2,1)}) custom-call(s32[1]{0:T(128)} %bitcast.2.refs_0_.refs_1_, bf16[1024,512]{1,0:T(8,128)(2,1)} %get-tuple-element.196.refs_1_, bf16[1024,768]{1,0:T(8,128)(2,1)} %attention_backward.2.refs_2_.refs_1_, bf16[1024,768]{1,0:T(8,128)(2,1)} %attention_backward.3.refs_3_.refs_2_, ...), custom_call_target="tpu_custom_call" | custom-call | flops 2147483648 | bytes 8388608 | tf_op jit(solution)/shard_map/weight_grad_attn/pallas_call | solution.py:192
  248.7 2.0 collective-permute-start.20
  250.7 8.2 %query_key_value_backward.1 = (f32[1024,512]{1,0:T(8,128)}, bf16[1024,512]{1,0:T(8,128)(2,1)}, f32[2,512]{1,0:T(2,128)}) custom-call(s32[1]{0:T(128)} %bitcast.2.refs_0_.refs_1_, bf16[1024,768]{1,0:T(8,128)(2,1)} %attention_backward.2.refs_2_.refs_1_, bf16[1024,768]{1,0:T(8,128)(2,1)} %attention_backward.3.refs_3_.refs_2_, ...), custom_call_target="tpu_custom_call" | custom-call | flops 1610612736 | bytes 12611584 | tf_op jit(solution)/shard_map/query_key_value_backward/pallas_call | solution.py:192
  262.5 6.6 %weight_grad_shrink.1 = (bf16[2,512,512]{2,1,0:T(8,128)(2,1)}, bf16[2,512,512]{2,1,0:T(8,128)(2,1)}) custom-call(s32[1]{0:T(128)} %bitcast.2.refs_0_.refs_1_, bf16[1024,2048]{1,0:T(8,128)(2,1)} %get-tuple-element.203.refs_1_, bf16[1024,512]{1,0:T(8,128)(2,1)} %get-tuple-element.211.refs_2_), custom_call_target="tpu_custom_call" | custom-call | flops 2147483648 | bytes 7340032 | tf_op jit(solution)/shard_map/weight_grad_shrink/pallas_call | solution.py:192
  274.5 5.7 %collective-permute-start.26 = (bf16[1,256,512]{2,1,0:T(8,128)(2,1)S(1)}, bf16[1,256,512]{2,1,0:T(8,128)(2,1)S(1)}, u32[]{:S(2)}, u32[]{:S(2)}) collective-permute-start(bf16[1,256,512]{2,1,0:T(8,128)(2,1)S(1)} %add_convert_fusion.10), channel_id=1, source_target_pairs={{0,16},{4,20},{8,24},{12,28},{16,0},{20,4},{24,8},{28,12},{1,17},{... | collective-permute-start | bytes 786440 | tf_op jit(solution)/shard_map/ppermute | solution.py:1113
  280.3 13.6 %feed_forward_backward.1 = (f32[1024,512]{1,0:T(8,128)}, bf16[1024,2048]{1,0:T(8,128)(2,1)}, f32[44,512]{1,0:T(8,128)}) custom-call(s32[1]{0:T(128)} %bitcast.2.refs_0_.refs_1_, f32[1024,512]{1,0:T(8,128)} %get-tuple-element.201.refs_1_, bf16[1024,512]{1,0:T(8,128)(2,1)} %get-tuple-element.211.refs_2_, bf16[1024,512]{1,0:T(8,128)(2,1)} %refs_3_.6, ...), custom_call_target="tpu_custom_call" | custom-call | flops 4294967296 | bytes 19075072 | tf_op jit(solution)/shard_map/feed_forward_backward/pallas_call | solution.py:192
  296.2 7.2 %weight_grad_expand.1 = (bf16[2,528,512]{2,1,0:T(8,128)(2,1)}, bf16[2,528,512]{2,1,0:T(8,128)(2,1)}) custom-call(s32[1]{0:T(128)} %bitcast.2.refs_0_.refs_1_, bf16[1024,512]{1,0:T(8,128)(2,1)} %get-tuple-element.217.refs_1_, bf16[1024,2048]{1,0:T(8,128)(2,1)} %get-tuple-element.224.refs_2_, bf16[4,16,512]{2,1,0:T(8,128)(2,1)} %bitcast.61), custom_call_target="tpu_custom_call" | custom-call | flops 2147483648 | bytes 7471104 | tf_op jit(solution)/shard_map/weight_grad_expand/pallas_call | solution.py:192
  303.6 2.9 collective-permute-done.28
  309.0 5.6 %collective-permute-start.47 = (bf16[1,96,512]{2,1,0:T(8,128)(2,1)S(1)}, bf16[1,96,512]{2,1,0:T(8,128)(2,1)S(1)}, u32[]{:S(2)}, u32[]{:S(2)}) collective-permute-start(bf16[1,96,512]{2,1,0:T(8,128)(2,1)S(1)} %add_convert_fusion.23), channel_id=1, source_target_pairs={{0,16},{4,20},{8,24},{12,28},{16,0},{20,4},{24,8},{28,12},{1,17},{... | collective-permute-start | bytes 294920 | tf_op jit(solution)/shard_map/ppermute | solution.py:1113
  319.2 2.1 collective-permute-start.35
  321.3 3.5 collective-permute-done.48
  326.7 3.9 %collective-permute-done.37 = bf16[1,256,512]{2,1,0:T(8,128)(2,1)S(1)} collective-permute-done((bf16[1,256,512]{2,1,0:T(8,128)(2,1)S(1)}, bf16[1,256,512]{2,1,0:T(8,128)(2,1)S(1)}, u32[]{:S(2)}, u32[]{:S(2)}) %collective-permute-start.37) | collective-permute-done | bytes 262176 | tf_op jit(solution)/shard_map/ppermute | solution.py:1113
  331.6 3.2 collective-permute-done.49
  335.1 2.1 adam_conv.1
  339.2 2.9 collective-permute-start.39
  342.2 8.5 %collective-permute-done.30 = bf16[1,264,512]{2,1,0:T(8,128)(2,1)S(1)} collective-permute-done((bf16[1,264,512]{2,1,0:T(8,128)(2,1)S(1)}, bf16[1,264,512]{2,1,0:T(8,128)(2,1)S(1)}, u32[]{:S(2)}, u32[]{:S(2)}) %collective-permute-start.30) | collective-permute-done | bytes 270368 | tf_op jit(solution)/shard_map/ppermute | solution.py:1113
  351.0 2.1 collective-permute-start.45
  353.1 3.8 collective-permute-done.31
  357.9 6.8 %collective-permute-done.32 = bf16[1,132,512]{2,1,0:T(8,128)(2,1)S(1)} collective-permute-done((bf16[1,132,512]{2,1,0:T(8,128)(2,1)S(1)}, bf16[1,132,512]{2,1,0:T(8,128)(2,1)S(1)}, u32[]{:S(2)}, u32[]{:S(2)}) %collective-permute-start.32) | collective-permute-done | bytes 135200 | tf_op jit(solution)/shard_map/ppermute | solution.py:1113
  365.1 2.0 collective-permute-start.41
  367.1 2.7 collective-permute-done.33
  370.7 3.8 adam_late.1
  374.7 2.8 adam_attn.1
  377.8 2.5 adam_shrink.1
  382.2 4.2 %adam_expand.1 = (f32[2,128,2048]{2,1,0:T(8,128)}, f32[2,128,2048]{2,1,0:T(8,128)}, f32[2,128,2048]{2,1,0:T(8,128)}) custom-call(bf16[528,512]{1,0:T(8,128)(2,1)S(1)} %maximum_select_fusion.1.refs_0_, f32[2,128,2048]{2,1,0:T(8,128)S(1)} %copy-done.1, f32[2,128,2048]{2,1,0:T(8,128)S(1)} %copy-done.5, ...), custom_call_target="tpu_custom_call", output_to_operand_aliasing={{0}: (4, {}), {1}: (5, {}), {2}: (6, {})} | custom-call | flops 5242880 | bytes 6815744 | tf_op jit(solution)/shard_map/adam_expand/pallas_call | solution.py:1277
  (281 shorter events, 57.3 us)
Async XLA Ops:
  3.4 14.4 %collective-permute-start = (bf16[44,128]{1,0:T(8,128)(2,1)S(1)}, bf16[44,128]{1,0:T(8,128)(2,1)S(1)}, u32[]{:S(2)}, u32[]{:S(2)}) collective-permute-start(bf16[44,128]{1,0:T(8,128)(2,1)S(1)} %pad_maximum_fusion.2), channel_id=1, source_target_pairs={{0,2},{1,3},{2,0},{3,1},{4,6},{5,7},{6,4},{7,5},{8,10},{9,11},{10,... | collective-permute-start | bytes 33800 | tf_op jit(solution)/shard_map/ppermute | solution.py:1113
  6.4 11.6 %collective-permute-start.1 = (bf16[44,128]{1,0:T(8,128)(2,1)S(1)}, bf16[44,128]{1,0:T(8,128)(2,1)S(1)}, u32[]{:S(2)}, u32[]{:S(2)}) collective-permute-start(bf16[44,128]{1,0:T(8,128)(2,1)S(1)} %pad_maximum_fusion.2), channel_id=1, source_target_pairs={{0,1},{1,0},{2,3},{3,2},{4,5},{5,4},{6,7},{7,6},{8,9},{9,8},{10,11... | collective-permute-start | bytes 33800 | tf_op jit(solution)/shard_map/ppermute | solution.py:1113
  6.4 25.8 %collective-permute-start.3 = (bf16[1024,512]{1,0:T(8,128)(2,1)}, bf16[1024,512]{1,0:T(8,128)(2,1)S(1)}, u32[]{:S(2)}, u32[]{:S(2)}) collective-permute-start(bf16[1024,512]{1,0:T(8,128)(2,1)} %pack_early.1.refs_3_.refs_10_), channel_id=1, source_target_pairs={{0,2},{1,3},{2,0},{3,1},{4,6},{5,7},{6,4},{7,5},{8,10},{9,11},{10,... | collective-permute-start | bytes 3145736 | tf_op jit(solution)/shard_map/ppermute | solution.py:1113
  6.6 26.1 %collective-permute-start.4 = (bf16[1024,512]{1,0:T(8,128)(2,1)}, bf16[1024,512]{1,0:T(8,128)(2,1)S(1)}, u32[]{:S(2)}, u32[]{:S(2)}) collective-permute-start(bf16[1024,512]{1,0:T(8,128)(2,1)} %pack_early.1.refs_3_.refs_10_), channel_id=1, source_target_pairs={{0,1},{1,0},{2,3},{3,2},{4,5},{5,4},{6,7},{7,6},{8,9},{9,8},{10,11... | collective-permute-start | bytes 3145736 | tf_op jit(solution)/shard_map/ppermute | solution.py:1113
  32.2 2.7 collective-permute-start.5
  32.2 14.9 %collective-permute-start.6 = (bf16[512,512]{1,0:T(8,128)(2,1)S(1)}, bf16[512,512]{1,0:T(8,128)(2,1)S(1)}, u32[]{:S(2)}, u32[]{:S(2)}) collective-permute-start(bf16[512,512]{1,0:T(8,128)(2,1)S(1)} %copy-done.25), channel_id=1, source_target_pairs={{0,2},{1,3},{2,0},{3,1},{4,6},{5,7},{6,4},{7,5},{8,10},{9,11},{10,... | collective-permute-start | bytes 1572872 | tf_op jit(solution)/shard_map/ppermute | solution.py:1113
  47.4 2.5 collective-permute-start.7
  47.7 11.8 %collective-permute-start.9 = (bf16[384,512]{1,0:T(8,128)(2,1)S(1)}, bf16[384,512]{1,0:T(8,128)(2,1)S(1)}, u32[]{:S(2)}, u32[]{:S(2)}) collective-permute-start(bf16[384,512]{1,0:T(8,128)(2,1)S(1)} %copy-done.31), channel_id=1, source_target_pairs={{0,2},{1,3},{2,0},{3,1},{4,6},{5,7},{6,4},{7,5},{8,10},{9,11},{10,... | collective-permute-start | bytes 1179656 | tf_op jit(solution)/shard_map/ppermute | solution.py:1113
  59.6 44.1 %collective-permute-start.12 = (bf16[1024,512]{1,0:T(8,128)(2,1)}, bf16[1024,512]{1,0:T(8,128)(2,1)S(1)}, u32[]{:S(2)}, u32[]{:S(2)}) collective-permute-start(bf16[1024,512]{1,0:T(8,128)(2,1)} %pack_late.1.refs_11_), channel_id=1, source_target_pairs={{0,2},{1,3},{2,0},{3,1},{4,6},{5,7},{6,4},{7,5},{8,10},{9,11},{10,... | collective-permute-start | bytes 3145736 | tf_op jit(solution)/shard_map/ppermute | solution.py:1113
  60.3 2.4 collective-permute-start.10
  103.6 18.7 %collective-permute-start.13 = (bf16[1024,512]{1,0:T(8,128)(2,1)}, bf16[1024,512]{1,0:T(8,128)(2,1)S(1)}, u32[]{:S(2)}, u32[]{:S(2)}) collective-permute-start(bf16[1024,512]{1,0:T(8,128)(2,1)} %pack_late.1.refs_11_), channel_id=1, source_target_pairs={{0,1},{1,0},{2,3},{3,2},{4,5},{5,4},{6,7},{7,6},{8,9},{9,8},{10,11... | collective-permute-start | bytes 3145736 | tf_op jit(solution)/shard_map/ppermute | solution.py:1113
  103.7 18.6 %collective-permute-start.14 = (bf16[1024,512]{1,0:T(8,128)(2,1)S(1)}, bf16[1024,512]{1,0:T(8,128)(2,1)S(1)}, u32[]{:S(2)}, u32[]{:S(2)}) collective-permute-start(bf16[1024,512]{1,0:T(8,128)(2,1)S(1)} %collective-permute-done.12.refs_12_), channel_id=1, source_target_pairs={{0,1},{1,0},{2,3},{3,2},{4,5},{5,4},{6,7},{7,6},{8,9},{9,8},{10,11... | collective-permute-start | bytes 3145736 | tf_op jit(solution)/shard_map/ppermute | solution.py:1113
  147.5 13.5 %all-to-all-start.1 = ((f32[32,2,512]{2,1,0:T(2,128)}), f32[32,2,512]{2,1,0:T(2,128)S(1)}, u32[]{:S(2)}, u32[]{:S(2)}) async-start(f32[32,2,512]{2,1,0:T(2,128)} %broadcast_in_dim.17), calls=%async_computation.1 | async-start | bytes 262144 | tf_op jit(solution)/shard_map/all_to_all | solution.py:1217
  161.0 18.1 %collective-permute-start.15 = (bf16[2,1024,512]{2,1,0:T(8,128)(2,1)}, bf16[2,1024,512]{2,1,0:T(8,128)(2,1)}, u32[]{:S(2)}, u32[]{:S(2)}) collective-permute-start(bf16[2,1024,512]{2,1,0:T(8,128)(2,1)} %get-tuple-element.175), channel_id=1, source_target_pairs={{0,1},{1,0},{2,3},{3,2},{4,5},{5,4},{6,7},{7,6},{8,9},{9,8},{10,11... | collective-permute-start | bytes 6291464 | tf_op jit(solution)/shard_map/ppermute | solution.py:1113
  180.5 35.7 %collective-permute-start.16 = (bf16[1,1024,512]{2,1,0:T(8,128)(2,1)S(1)}, bf16[1,1024,512]{2,1,0:T(8,128)(2,1)}, u32[]{:S(2)}, u32[]{:S(2)}) collective-permute-start(bf16[1,1024,512]{2,1,0:T(8,128)(2,1)S(1)} %add_convert_fusion), channel_id=1, source_target_pairs={{0,2},{1,3},{2,0},{3,1},{4,6},{5,7},{6,4},{7,5},{8,10},{9,11},{10,... | collective-permute-start | bytes 3145736 | tf_op jit(solution)/shard_map/ppermute | solution.py:1113
  199.7 16.6 %collective-permute-start.18 = (bf16[2,384,512]{2,1,0:T(8,128)(2,1)}, bf16[2,384,512]{2,1,0:T(8,128)(2,1)}, u32[]{:S(2)}, u32[]{:S(2)}) collective-permute-start(bf16[2,384,512]{2,1,0:T(8,128)(2,1)} %get-tuple-element.185), channel_id=1, source_target_pairs={{0,1},{1,0},{2,3},{3,2},{4,5},{5,4},{6,7},{7,6},{8,9},{9,8},{10,11... | collective-permute-start | bytes 2359304 | tf_op jit(solution)/shard_map/ppermute | solution.py:1113
  217.8 22.0 %collective-permute-start.17 = (bf16[1,512,512]{2,1,0:T(8,128)(2,1)S(1)}, bf16[1,512,512]{2,1,0:T(8,128)(2,1)S(1)}, u32[]{:S(2)}, u32[]{:S(2)}) collective-permute-start(bf16[1,512,512]{2,1,0:T(8,128)(2,1)S(1)} %add_convert_fusion.4), channel_id=1, source_target_pairs={{0,4},{4,0},{8,12},{12,8},{16,20},{20,16},{24,28},{28,24},{1,5},{5... | collective-permute-start | bytes 1572872 | tf_op jit(solution)/shard_map/ppermute | solution.py:1113
  221.2 16.7 %collective-permute-start.19 = (bf16[1,384,512]{2,1,0:T(8,128)(2,1)}, bf16[1,384,512]{2,1,0:T(8,128)(2,1)}, u32[]{:S(2)}, u32[]{:S(2)}) collective-permute-start(bf16[1,384,512]{2,1,0:T(8,128)(2,1)} %add_convert_fusion.5), channel_id=1, source_target_pairs={{0,2},{1,3},{2,0},{3,1},{4,6},{5,7},{6,4},{7,5},{8,10},{9,11},{10,... | collective-permute-start | bytes 1179656 | tf_op jit(solution)/shard_map/ppermute | solution.py:1113
  248.1 13.2 %collective-permute-start.22 = (bf16[2,512,512]{2,1,0:T(8,128)(2,1)}, bf16[2,512,512]{2,1,0:T(8,128)(2,1)}, u32[]{:S(2)}, u32[]{:S(2)}) collective-permute-start(bf16[2,512,512]{2,1,0:T(8,128)(2,1)} %get-tuple-element.198), channel_id=1, source_target_pairs={{0,1},{1,0},{2,3},{3,2},{4,5},{5,4},{6,7},{7,6},{8,9},{9,8},{10,11... | collective-permute-start | bytes 3145736 | tf_op jit(solution)/shard_map/ppermute | solution.py:1113
  248.1 10.8 %collective-permute-start.21 = (bf16[1,192,512]{2,1,0:T(8,128)(2,1)}, bf16[1,192,512]{2,1,0:T(8,128)(2,1)S(1)}, u32[]{:S(2)}, u32[]{:S(2)}) collective-permute-start(bf16[1,192,512]{2,1,0:T(8,128)(2,1)} %add_convert_fusion.12), channel_id=1, source_target_pairs={{0,4},{4,0},{8,12},{12,8},{16,20},{20,16},{24,28},{28,24},{1,5},{5... | collective-permute-start | bytes 589832 | tf_op jit(solution)/shard_map/ppermute | solution.py:1113
  248.7 11.4 %collective-permute-start.20 = (bf16[1,256,512]{2,1,0:T(8,128)(2,1)S(1)}, bf16[1,256,512]{2,1,0:T(8,128)(2,1)S(1)}, u32[]{:S(2)}, u32[]{:S(2)}) collective-permute-start(bf16[1,256,512]{2,1,0:T(8,128)(2,1)S(1)} %add_convert_fusion.11), channel_id=1, source_target_pairs={{0,8},{4,12},{8,0},{12,4},{16,24},{20,28},{24,16},{28,20},{1,9},{5... | collective-permute-start | bytes 786440 | tf_op jit(solution)/shard_map/ppermute | solution.py:1113
  269.1 2.9 collective-permute-start.23
  269.1 24.9 %collective-permute-start.24 = (bf16[1,512,512]{2,1,0:T(8,128)(2,1)S(1)}, bf16[1,512,512]{2,1,0:T(8,128)(2,1)}, u32[]{:S(2)}, u32[]{:S(2)}) collective-permute-start(bf16[1,512,512]{2,1,0:T(8,128)(2,1)S(1)} %add_convert_fusion.3), channel_id=1, source_target_pairs={{0,2},{1,3},{2,0},{3,1},{4,6},{5,7},{6,4},{7,5},{8,10},{9,11},{10,... | collective-permute-start | bytes 1572872 | tf_op jit(solution)/shard_map/ppermute | solution.py:1113
  273.5 22.7 %collective-permute-start.25 = (bf16[1,512,512]{2,1,0:T(8,128)(2,1)S(1)}, bf16[1,512,512]{2,1,0:T(8,128)(2,1)S(1)}, u32[]{:S(2)}, u32[]{:S(2)}) collective-permute-start(bf16[1,512,512]{2,1,0:T(8,128)(2,1)S(1)} %add_convert_fusion.2), channel_id=1, source_target_pairs={{0,2},{1,3},{2,0},{3,1},{4,6},{5,7},{6,4},{7,5},{8,10},{9,11},{10,... | collective-permute-start | bytes 1572872 | tf_op jit(solution)/shard_map/ppermute | solution.py:1113
  274.5 5.8 %collective-permute-start.27 = (bf16[1,96,512]{2,1,0:T(8,128)(2,1)S(1)}, bf16[1,96,512]{2,1,0:T(8,128)(2,1)S(1)}, u32[]{:S(2)}, u32[]{:S(2)}) collective-permute-start(bf16[1,96,512]{2,1,0:T(8,128)(2,1)S(1)} %add_convert_fusion.24), channel_id=1, source_target_pairs={{0,8},{4,12},{8,0},{12,4},{16,24},{20,28},{24,16},{28,20},{1,9},{5... | collective-permute-start | bytes 294920 | tf_op jit(solution)/shard_map/ppermute | solution.py:1113
  274.5 19.4 %collective-permute-start.26 = (bf16[1,256,512]{2,1,0:T(8,128)(2,1)S(1)}, bf16[1,256,512]{2,1,0:T(8,128)(2,1)S(1)}, u32[]{:S(2)}, u32[]{:S(2)}) collective-permute-start(bf16[1,256,512]{2,1,0:T(8,128)(2,1)S(1)} %add_convert_fusion.10), channel_id=1, source_target_pairs={{0,16},{4,20},{8,24},{12,28},{16,0},{20,4},{24,8},{28,12},{1,17},{... | collective-permute-start | bytes 786440 | tf_op jit(solution)/shard_map/ppermute | solution.py:1113
  303.4 3.0 collective-permute-start.28
  307.7 29.6 %collective-permute-start.29 = (bf16[1,528,512]{2,1,0:T(8,128)(2,1)S(1)}, bf16[1,528,512]{2,1,0:T(8,128)(2,1)S(1)}, u32[]{:S(2)}, u32[]{:S(2)}) collective-permute-start(bf16[1,528,512]{2,1,0:T(8,128)(2,1)S(1)} %add_convert_fusion.1), channel_id=1, source_target_pairs={{0,2},{1,3},{2,0},{3,1},{4,6},{5,7},{6,4},{7,5},{8,10},{9,11},{10,... | collective-permute-start | bytes 1622024 | tf_op jit(solution)/shard_map/ppermute | solution.py:1113
  309.0 10.0 %collective-permute-start.47 = (bf16[1,96,512]{2,1,0:T(8,128)(2,1)S(1)}, bf16[1,96,512]{2,1,0:T(8,128)(2,1)S(1)}, u32[]{:S(2)}, u32[]{:S(2)}) collective-permute-start(bf16[1,96,512]{2,1,0:T(8,128)(2,1)S(1)} %add_convert_fusion.23), channel_id=1, source_target_pairs={{0,16},{4,20},{8,24},{12,28},{16,0},{20,4},{24,8},{28,12},{1,17},{... | collective-permute-start | bytes 294920 | tf_op jit(solution)/shard_map/ppermute | solution.py:1113
  315.8 9.7 %collective-permute-start.42 = (bf16[1,256,512]{2,1,0:T(8,128)(2,1)S(1)}, bf16[1,256,512]{2,1,0:T(8,128)(2,1)S(1)}, u32[]{:S(2)}, u32[]{:S(2)}) collective-permute-start(bf16[1,256,512]{2,1,0:T(8,128)(2,1)S(1)} %add_convert_fusion.7), channel_id=1, source_target_pairs={{0,4},{4,0},{8,12},{12,8},{16,20},{20,16},{24,28},{28,24},{1,5},{5... | collective-permute-start | bytes 786440 | tf_op jit(solution)/shard_map/ppermute | solution.py:1113
  317.4 13.2 %collective-permute-start.37 = (bf16[1,256,512]{2,1,0:T(8,128)(2,1)S(1)}, bf16[1,256,512]{2,1,0:T(8,128)(2,1)S(1)}, u32[]{:S(2)}, u32[]{:S(2)}) collective-permute-start(bf16[1,256,512]{2,1,0:T(8,128)(2,1)S(1)} %add_convert_fusion.8), channel_id=1, source_target_pairs={{0,4},{4,0},{8,12},{12,8},{16,20},{20,16},{24,28},{28,24},{1,5},{5... | collective-permute-start | bytes 786440 | tf_op jit(solution)/shard_map/ppermute | solution.py:1113
  319.1 5.7 %collective-permute-start.48 = (bf16[96,512]{1,0:T(8,128)(2,1)S(1)}, bf16[96,512]{1,0:T(8,128)(2,1)S(1)}, u32[]{:S(2)}, u32[]{:S(2)}) collective-permute-start(bf16[96,512]{1,0:T(8,128)(2,1)S(1)} %fusion.5), channel_id=1, source_target_pairs={{0,8},{4,12},{8,0},{12,4},{16,24},{20,28},{24,16},{28,20},{1,9},{5... | collective-permute-start | bytes 294920 | tf_op jit(solution)/shard_map/ppermute | solution.py:1113
  319.2 11.6 %collective-permute-start.35 = (bf16[256,512]{1,0:T(8,128)(2,1)S(1)}, bf16[256,512]{1,0:T(8,128)(2,1)S(1)}, u32[]{:S(2)}, u32[]{:S(2)}) collective-permute-start(bf16[256,512]{1,0:T(8,128)(2,1)S(1)} %fusion), channel_id=1, source_target_pairs={{0,8},{4,12},{8,0},{12,4},{16,24},{20,28},{24,16},{28,20},{1,9},{5... | collective-permute-start | bytes 786440 | tf_op jit(solution)/shard_map/ppermute | solution.py:1113
  324.9 10.0 %collective-permute-start.49 = (bf16[192,512]{1,0:T(8,128)(2,1)S(1)}, bf16[192,512]{1,0:T(8,128)(2,1)S(1)}, u32[]{:S(2)}, u32[]{:S(2)}) collective-permute-start(bf16[192,512]{1,0:T(8,128)(2,1)S(1)} %maximum_select_fusion.9), channel_id=1, source_target_pairs={{0,4},{4,0},{8,12},{12,8},{16,20},{20,16},{24,28},{28,24},{1,5},{5... | collective-permute-start | bytes 589832 | tf_op jit(solution)/shard_map/ppermute | solution.py:1113
  326.7 11.3 %collective-permute-start.43 = (bf16[1,128,512]{2,1,0:T(8,128)(2,1)S(1)}, bf16[1,128,512]{2,1,0:T(8,128)(2,1)S(1)}, u32[]{:S(2)}, u32[]{:S(2)}) collective-permute-start(bf16[1,128,512]{2,1,0:T(8,128)(2,1)S(1)} %add_convert_fusion.18), channel_id=1, source_target_pairs={{0,8},{4,12},{8,0},{12,4},{16,24},{20,28},{24,16},{28,20},{1,9},{5... | collective-permute-start | bytes 393224 | tf_op jit(solution)/shard_map/ppermute | solution.py:1113
  330.7 8.4 %collective-permute-start.38 = (bf16[1,128,512]{2,1,0:T(8,128)(2,1)S(1)}, bf16[1,128,512]{2,1,0:T(8,128)(2,1)S(1)}, u32[]{:S(2)}, u32[]{:S(2)}) collective-permute-start(bf16[1,128,512]{2,1,0:T(8,128)(2,1)S(1)} %add_convert_fusion.21), channel_id=1, source_target_pairs={{0,8},{4,12},{8,0},{12,4},{16,24},{20,28},{24,16},{28,20},{1,9},{5... | collective-permute-start | bytes 393224 | tf_op jit(solution)/shard_map/ppermute | solution.py:1113
  331.0 39.1 %collective-permute-start.36 = (bf16[512,512]{1,0:T(8,128)(2,1)S(1)}, bf16[512,512]{1,0:T(8,128)(2,1)S(1)}, u32[]{:S(2)}, u32[]{:S(2)}) collective-permute-start(bf16[512,512]{1,0:T(8,128)(2,1)S(1)} %maximum_select_fusion.2), channel_id=1, source_target_pairs={{0,4},{4,0},{8,12},{12,8},{16,20},{20,16},{24,28},{28,24},{1,5},{5... | collective-permute-start | bytes 1572872 | tf_op jit(solution)/shard_map/ppermute | solution.py:1113
  337.4 13.4 %collective-permute-start.30 = (bf16[1,264,512]{2,1,0:T(8,128)(2,1)S(1)}, bf16[1,264,512]{2,1,0:T(8,128)(2,1)S(1)}, u32[]{:S(2)}, u32[]{:S(2)}) collective-permute-start(bf16[1,264,512]{2,1,0:T(8,128)(2,1)S(1)} %add_convert_fusion.6), channel_id=1, source_target_pairs={{0,4},{4,0},{8,12},{12,8},{16,20},{20,16},{24,28},{28,24},{1,5},{5... | collective-permute-start | bytes 811016 | tf_op jit(solution)/shard_map/ppermute | solution.py:1113
  339.0 11.9 %collective-permute-start.44 = (bf16[1,128,512]{2,1,0:T(8,128)(2,1)S(1)}, bf16[1,128,512]{2,1,0:T(8,128)(2,1)S(1)}, u32[]{:S(2)}, u32[]{:S(2)}) collective-permute-start(bf16[1,128,512]{2,1,0:T(8,128)(2,1)S(1)} %add_convert_fusion.17), channel_id=1, source_target_pairs={{0,16},{4,20},{8,24},{12,28},{16,0},{20,4},{24,8},{28,12},{1,17},{... | collective-permute-start | bytes 393224 | tf_op jit(solution)/shard_map/ppermute | solution.py:1113
  339.2 18.0 %collective-permute-start.39 = (bf16[1,128,512]{2,1,0:T(8,128)(2,1)S(1)}, bf16[1,128,512]{2,1,0:T(8,128)(2,1)S(1)}, u32[]{:S(2)}, u32[]{:S(2)}) collective-permute-start(bf16[1,128,512]{2,1,0:T(8,128)(2,1)S(1)} %add_convert_fusion.20), channel_id=1, source_target_pairs={{0,16},{4,20},{8,24},{12,28},{16,0},{20,4},{24,8},{28,12},{1,17},{... | collective-permute-start | bytes 393224 | tf_op jit(solution)/shard_map/ppermute | solution.py:1113
  350.9 6.0 %collective-permute-start.31 = (bf16[1,132,512]{2,1,0:T(8,128)(2,1)S(1)}, bf16[1,132,512]{2,1,0:T(8,128)(2,1)S(1)}, u32[]{:S(2)}, u32[]{:S(2)}) collective-permute-start(bf16[1,132,512]{2,1,0:T(8,128)(2,1)S(1)} %add_convert_fusion.15), channel_id=1, source_target_pairs={{0,8},{4,12},{8,0},{12,4},{16,24},{20,28},{24,16},{28,20},{1,9},{5... | collective-permute-start | bytes 405512 | tf_op jit(solution)/shard_map/ppermute | solution.py:1113
  351.0 13.8 %collective-permute-start.45 = (bf16[128,512]{1,0:T(8,128)(2,1)S(1)}, bf16[128,512]{1,0:T(8,128)(2,1)S(1)}, u32[]{:S(2)}, u32[]{:S(2)}) collective-permute-start(bf16[128,512]{1,0:T(8,128)(2,1)S(1)} %fusion.4), channel_id=1, source_target_pairs={{0,8},{4,12},{8,0},{12,4},{16,24},{20,28},{24,16},{28,20},{1,9},{5... | collective-permute-start | bytes 393224 | tf_op jit(solution)/shard_map/ppermute | solution.py:1113
  357.1 7.6 %collective-permute-start.32 = (bf16[1,132,512]{2,1,0:T(8,128)(2,1)S(1)}, bf16[1,132,512]{2,1,0:T(8,128)(2,1)S(1)}, u32[]{:S(2)}, u32[]{:S(2)}) collective-permute-start(bf16[1,132,512]{2,1,0:T(8,128)(2,1)S(1)} %add_convert_fusion.14), channel_id=1, source_target_pairs={{0,16},{4,20},{8,24},{12,28},{16,0},{20,4},{24,8},{28,12},{1,17},{... | collective-permute-start | bytes 405512 | tf_op jit(solution)/shard_map/ppermute | solution.py:1113
  357.3 7.8 %collective-permute-start.40 = (bf16[128,512]{1,0:T(8,128)(2,1)S(1)}, bf16[128,512]{1,0:T(8,128)(2,1)S(1)}, u32[]{:S(2)}, u32[]{:S(2)}) collective-permute-start(bf16[128,512]{1,0:T(8,128)(2,1)S(1)} %fusion.3), channel_id=1, source_target_pairs={{0,8},{4,12},{8,0},{12,4},{16,24},{20,28},{24,16},{28,20},{1,9},{5... | collective-permute-start | bytes 393224 | tf_op jit(solution)/shard_map/ppermute | solution.py:1113
  364.8 5.1 %collective-permute-start.33 = (bf16[132,512]{1,0:T(8,128)(2,1)S(1)}, bf16[132,512]{1,0:T(8,128)(2,1)S(1)}, u32[]{:S(2)}, u32[]{:S(2)}) collective-permute-start(bf16[132,512]{1,0:T(8,128)(2,1)S(1)} %fusion.2), channel_id=1, source_target_pairs={{0,8},{4,12},{8,0},{12,4},{16,24},{20,28},{24,16},{28,20},{1,9},{5... | collective-permute-start | bytes 405512 | tf_op jit(solution)/shard_map/ppermute | solution.py:1113
  364.9 9.5 %collective-permute-start.46 = (bf16[256,512]{1,0:T(8,128)(2,1)S(1)}, bf16[256,512]{1,0:T(8,128)(2,1)S(1)}, u32[]{:S(2)}, u32[]{:S(2)}) collective-permute-start(bf16[256,512]{1,0:T(8,128)(2,1)S(1)} %maximum_select_fusion.8), channel_id=1, source_target_pairs={{0,4},{4,0},{8,12},{12,8},{16,20},{20,16},{24,28},{28,24},{1,5},{5... | collective-permute-start | bytes 786440 | tf_op jit(solution)/shard_map/ppermute | solution.py:1113
  365.1 12.5 %collective-permute-start.41 = (bf16[256,512]{1,0:T(8,128)(2,1)S(1)}, bf16[256,512]{1,0:T(8,128)(2,1)S(1)}, u32[]{:S(2)}, u32[]{:S(2)}) collective-permute-start(bf16[256,512]{1,0:T(8,128)(2,1)S(1)} %maximum_select_fusion.7), channel_id=1, source_target_pairs={{0,4},{4,0},{8,12},{12,8},{16,20},{20,16},{24,28},{28,24},{1,5},{5... | collective-permute-start | bytes 786440 | tf_op jit(solution)/shard_map/ppermute | solution.py:1113
  370.0 10.3 %collective-permute-start.34 = (bf16[264,512]{1,0:T(8,128)(2,1)S(1)}, bf16[264,512]{1,0:T(8,128)(2,1)S(1)}, u32[]{:S(2)}, u32[]{:S(2)}) collective-permute-start(bf16[264,512]{1,0:T(8,128)(2,1)S(1)} %maximum_select_fusion.6), channel_id=1, source_target_pairs={{0,4},{4,0},{8,12},{12,8},{16,20},{20,16},{24,28},{28,24},{1,5},{5... | collective-permute-start | bytes 811016 | tf_op jit(solution)/shard_map/ppermute | solution.py:1113
  (64 other events, 640.1 us)

commit v4 on v3

--- a/solution.py
+++ b/solution.py
@@ -109,13 +109,20 @@
 
 
 def load_once(t, copies, sems):
+    made = [pltpu.make_async_copy(s, d, sems.at[k]) for k, (s, d) in enumerate(copies)]
+
     @pl.when(t == 0)
     def _():
-        made = [pltpu.make_async_copy(s, d, sems.at[k]) for k, (s, d) in enumerate(copies)]
         for copy in made:
             copy.start()
-        for copy in made:
-            copy.wait()
+
+    def ready(first=0, last=None):
+        @pl.when(t == 0)
+        def _():
+            for copy in made[first:last]:
+                copy.wait()
+
+    return ready
 
 
 def column_blocks(piece, owner, dst, rows, base=0):
@@ -237,15 +244,18 @@
     n = len(rel)
     parts = refs[:n]
     x1, hidden, before, active, w_in, w_out, sems = refs[n:]
-    copies = []
+    copies, later = [], []
     for k, r in enumerate(rel):
         copies += column_blocks(parts[k], me[0] ^ r, w_in, er)
-        copies += row_block(parts[k], me[0] ^ r, w_out, sr, 4 * er)
-    load_once(t, copies, sems)
+        later += row_block(parts[k], me[0] ^ r, w_out, sr, 4 * er)
+    split = len(copies)
+    copies += later
+    ready = load_once(t, copies, sems)
     value = x[...].astype(f32)
     normed, _ = normalize(value)
     h = (normed * norms[0:1, :] + norms[1:2, :]).astype(bf16)
     hidden[...] = h
+    ready(0, split)
     total = None
     for j in range(w_in.shape[1] // 512):
         cols = slice(512 * j, 512 * (j + 1))
@@ -253,6 +263,8 @@
         s = (a * sigmoid(a)).astype(bf16)
         before[:, cols] = a.astype(bf16)
         active[:, cols] = s
+        if j == 0:
+            ready(split)
         part = mm(s, w_out[cols, :])
         total = part if total is None else total + part
     x1[...] = value + 0.5 * total
@@ -290,10 +302,11 @@
     copies = []
     for j, r in enumerate(rel):
         copies += column_blocks(parts[j], me[0] ^ r, w, ar)
-    load_once(t, copies, sems)
+    ready = load_once(t, copies, sems)
     normed, _ = normalize(x1[...])
     h = (normed * norms[2:3, :] + norms[3:4, :]).astype(bf16)
     hidden[...] = h
+    ready()
     c, s = cs[...], sn[...]
     for p in range(4):
         cols = slice(128 * p, 128 * (p + 1))
@@ -331,7 +344,7 @@
     copies = []
     for j, r in enumerate(rel):
         copies += row_block(parts[j], me[0] ^ r, w, ar, 3 * ar)
-    load_once(t, copies, sems)
+    ready = load_once(t, copies, sems)
     e = [ends[j] for j in range(4)]
     first = t * TILE
     lo, hi = key_range(first, first + TILE - 1, e, rows)
@@ -364,6 +377,7 @@
         lax.fori_loop(0, 4, pair, 0, unroll=2)
 
     in_window(lo, hi, rows, body)
+    ready()
     x2[...] = x1[...] + mm(mixed[...], w[...])
 
 
@@ -427,7 +441,7 @@
             gp[here, pl.ds(pl.multiple_of(128 * (pairs + p), 128), 128)] = turned.astype(bf16)
             return carry
 
-        lax.fori_loop(0, pairs, pair, 0)
+        lax.fori_loop(0, pairs, pair, 0, unroll=2)
 
     in_window(lo, hi, rows, body)
 
@@ -596,7 +610,7 @@
     copies = []
     for j, r in enumerate(rel):
         copies += column_blocks(parts[j], me[0] ^ r, w, ar)
-    load_once(t, copies, sems)
+    ready = load_once(t, copies, sems)
     e = [ends[j] for j in range(4)]
 
     @pl.when(t == 0)
@@ -606,6 +620,7 @@
     normed, _ = normalize(x2[...])
     h = (normed * norms[4:5, :] + norms[5:6, :]).astype(bf16)
     hidden[...] = h
+    ready()
     half = mm(h, w[:, :512])
     gate = mm(h, w[:, 512:])
     gates_out[:, :512] = half.astype(bf16)
@@ -728,7 +743,7 @@
     for j, r in enumerate(rel):
         copies += column_blocks(parts[j], me[0] ^ r, w, ar)
         copies += row_block(heads[j], me[0] ^ r, w_heads, ar, 3 * ar)
-    load_once(t, copies, sems)
+    ready = load_once(t, copies, sems)
     e = [ends[j] for j in range(4)]
 
     @pl.when(t == 0)
@@ -742,6 +757,7 @@
     second = (gg * gates[:, :512].astype(f32) * sigma * (1.0 - sigma)).astype(bf16)
     g_gates[:, :512] = first
     g_gates[:, 512:] = second
+    ready()
     g_hidden = mm_nt(first, w[:, :512]) + mm_nt(second, w[:, 512:])
     normed, scale = normalize(x2[...])
     sums[0:1, :] += col_sum(g_hidden * normed)
@@ -798,12 +814,14 @@
     points, ffs = refs[:n], refs[n : 2 * n]
     (y, g_third, g_zed, wact, branch_out, hidden, active, g_before, g_out, sums, batch) = refs[2 * n : 2 * n + 11]
     w_point, w_in, w_out, slope, sems = refs[2 * n + 11 :]
-    copies = []
+    copies, later, last_ones = [], [], []
     for j, r in enumerate(rel):
         copies += row_block(points[j], me[0] ^ r, w_point, ar, 2 * ar)
-        copies += column_blocks(ffs[j], me[0] ^ r, w_in, er)
-        copies += row_block(ffs[j], me[0] ^ r, w_out, sr, 4 * er)
-    load_once(t, copies, sems)
+        later += column_blocks(ffs[j], me[0] ^ r, w_in, er)
+        last_ones += row_block(ffs[j], me[0] ^ r, w_out, sr, 4 * er)
+    one, two = len(copies), len(copies) + len(later)
+    copies += later + last_ones
+    ready = load_once(t, copies, sems)
 
     @pl.when(t == 0)
     def _():
@@ -821,10 +839,12 @@
     wa = (zed * sigma).astype(bf16)
     wact[...] = wa
     zed_slope = slope_of(zed, sigma)
+    ready(0, one)
     third = x2[...] + mm(wa, w_point[...])
     normed, scale = normalize(third)
     h = (normed * norms[8:9, :] + norms[9:10, :]).astype(bf16)
     hidden[...] = h
+    ready(one, two)
     total = None
     for j in range(w_in.shape[1] // 512):
         cols = slice(512 * j, 512 * (j + 1))
@@ -833,6 +853,8 @@
         s = (a * sg).astype(bf16)
         active[:, cols] = s
         slope[:, cols] = slope_of(a, sg)
+        if j == 0:
+            ready(two)
         part = mm(s, w_out[cols, :])
         total = part if total is None else total + part
     fourth = third + 0.5 * total
@@ -911,19 +933,20 @@
     copies = []
     for j, r in enumerate(rel):
         copies += column_blocks(attn[j], me[0] ^ r, w, ar)
-    load_once(t, copies, sems)
+    ready = load_once(t, copies, sems)
 
     @pl.when(t == 0)
     def _():
         sums[...] = jnp.zeros_like(sums)
 
+    normed, scale = normalize(x1[...])
+    ready()
     g_hidden = None
     for z in range(3):
         for half, g in enumerate((ga, gb)):
             cols = slice(512 * z + 256 * half, 512 * z + 256 * (half + 1))
             part = mm_nt(g[:, 256 * z : 256 * (z + 1)], w[:, cols])
             g_hidden = part if g_hidden is None else g_hidden + part
-    normed, scale = normalize(x1[...])
     sums[0:1, :] += col_sum(g_hidden * normed)
     sums[1:2, :] += col_sum(g_hidden)
     out = g2[...] + norm_back(g_hidden, norms[2:3, :], normed, scale)
@@ -952,23 +975,28 @@
     n = len(rel)
     parts = refs[:n]
     g_frames, g_before, small, sums, w_in, w_out, sems = refs[n:]
-    copies = []
+    copies, later = [], []
     for j, r in enumerate(rel):
-        copies += column_blocks(parts[j], me[0] ^ r, w_in, er)
         copies += row_block(parts[j], me[0] ^ r, w_out, sr, 4 * er)
-    load_once(t, copies, sems)
+        later += column_blocks(parts[j], me[0] ^ r, w_in, er)
+    split = len(copies)
+    copies += later
+    ready = load_once(t, copies, sems)
 
     @pl.when(t == 0)
     def _():
         sums[...] = jnp.zeros_like(sums)
 
     out = go[...]
+    ready(0, split)
     g_hidden = None
     for j in range(w_in.shape[1] // 512):
         cols = slice(512 * j, 512 * (j + 1))
         a = before[:, cols].astype(f32)
         gb = (mm_nt(out, w_out[cols, :]) * slope_of(a, sigmoid(a))).astype(bf16)
         g_before[:, cols] = gb
+        if j == 0:
+            ready(split)
         part = mm_nt(gb, w_in[:, cols])
         g_hidden = part if g_hidden is None else g_hidden + part
     normed, scale = normalize(x[...].astype(f32))

time: 392 us -> 388 us (0.990)
  Pallas kernels: 228 us -> 215 us
  starting transfers between devices: 43.7 us -> 54.2 us
    pallas_call x19, Pallas kernels: 197 us -> 183 us  [run(): pl.pallas_call(lambda *refs: body(pl.program_id(0), *refs), grid_spec=plt...]
    ppermute x50, starting transfers between devices: 41.1 us -> 51.6 us  [swap(): return lax.ppermute(value, axis, [(k, k ^ mask) for k in range(size)])]
  transfers between devices with their start and end apart: 51 -> 51, of which waited for: 14 -> 17; matrix products, arithmetic and copies ran while one was open for 6% -> 7% of each run, Pallas kernels for 46% -> 43%
where the time goes in v4:
time: 388 us; the launch traced here: 381 us
  Pallas kernels  215 us (55%)
  starting transfers between devices  54.2 us (14%)
  waiting for transfers between devices  50.4 us (13%)
  other arithmetic  29.3 us (8%)
  blocking collectives  16.9 us (4%)
  local copies, waits for them, and re-layouts  13.3 us (3%)
    pallas_call x19, Pallas kernels, run(): pl.pallas_call(lambda *refs: body(pl.program_id(0), *refs), grid_spec=plt...  183 us
    ppermute x50, starting transfers between devices, swap(): return lax.ppermute(value, axis, [(k, k ^ mask) for k in range(size)])  51.6 us
    ppermute x50, waiting for transfers between devices, swap(): return lax.ppermute(value, axis, [(k, k ^ mask) for k in range(size)])  50.4 us
    convert_element_type x20, other arithmetic, sum_of(): return total.astype(bf16)  20.3 us
    all_to_all x1, blocking collectives, from_everyone(): return lax.all_to_all(spread, axes, 0, 0, tiled=True)  16.9 us
    pallas_call x1, Pallas kernels, run(): pl.pallas_call(kernel, in_specs=[pl.BlockSpec(memory_space=pltpu.SMEM)] *...  15.7 us
    unnamed x125, local copies, waits for them, and re-layouts  9.19 us
    pallas_call x3, Pallas kernels, adam_pair(): pl.pallas_call(adam_body, grid=(n,), in_specs=specs, out_specs=[spec_a] *...  8.73 us
  transfers between devices with their start and end apart: 51, of which 17 were waited for; matrix products, arithmetic and copies ran while one was open for 7% of the time, Pallas kernels for 43%

profile of v4, /device:TPU:0, one launch (start us, length us, event | category | flops | bytes accessed | tf_op | source)
XLA Modules:
  0.0 380.8 jit_solution(1863493424076036943)
XLA Ops:
  0.7 2.7 pack_early.1.refs_3_.refs_10_
  3.4 3.0 collective-permute-start
  7.4 1.9 fusion.1
  11.2 1.9 pack_conv.1.refs_6_.refs_7_.refs_9_
  13.1 2.0 pack_attn.1.refs_5_.refs_6_.refs_13_
  15.1 2.7 pack_late.1.refs_11_
  20.3 11.9 %collective-permute-done.3.refs_4_.refs_11_ = bf16[1024,512]{1,0:T(8,128)(2,1)S(1)} collective-permute-done((bf16[1024,512]{1,0:T(8,128)(2,1)}, bf16[1024,512]{1,0:T(8,128)(2,1)S(1)}, u32[]{:S(2)}, u32[]{:S(2)}) %collective-permute-start.3) | collective-permute-done | bytes 1048608 | tf_op jit(solution)/shard_map/ppermute | solution.py:1141
  32.7 2.2 collective-permute-done.5.refs_6_.refs_13_
  35.8 11.0 %ff_forward.1 = (f32[1024,512]{1,0:T(8,128)}, bf16[1024,512]{1,0:T(8,128)(2,1)}, bf16[1024,2048]{1,0:T(8,128)(2,1)}, bf16[1024,2048]{1,0:T(8,128)(2,1)}) custom-call(s32[1]{0:T(128)} %bitcast.2.refs_0_.refs_1_, bf16[1024,512]{1,0:T(8,128)(2,1)} %refs_3_.6, f32[12,512]{1,0:T(8,128)} %bitcast.41, bf16[1024,512]{1,0:T(8,128)(2,1)} %pack_early.1.refs_3_.refs_10_, ...), custom_call_target="tpu_custom_call" | custom-call | flops 4294967296 | bytes 16801792 | tf_op jit(solution)/shard_map/ff_forward/pallas_call | solution.py:199
  50.4 8.4 %query_key_value.1 = (bf16[1024,512]{1,0:T(8,128)(2,1)}, bf16[1024,512]{1,0:T(8,128)(2,1)}, bf16[1024,512]{1,0:T(8,128)(2,1)}, bf16[1024,512]{1,0:T(8,128)(2,1)}, bf16[512,1024]{1,0:T(8,128)(2,1)}) custom-call(s32[1]{0:T(128)} %bitcast.2.refs_0_.refs_1_, f32[1024,512]{1,0:T(8,128)} %get-tuple-element.144.refs_1_.refs_5_.refs_3_, f32[12,512]{1,0:T(8,128)} %bitcast.42, ...), custom_call_target="tpu_custom_call" | custom-call | flops 1610612736 | bytes 10510336 | tf_op jit(solution)/shard_map/query_key_value/pallas_call | solution.py:199
  62.0 17.1 %attention_forward.1 = (f32[1024,512]{1,0:T(8,128)}, bf16[1024,512]{1,0:T(8,128)(2,1)}, f32[8,1024]{1,0:T(8,128)}) custom-call(s32[4]{0:T(128)S(1)} %bitcast.51, s32[1]{0:T(128)} %bitcast.2.refs_0_.refs_1_, bf16[1024,512]{1,0:T(8,128)(2,1)} %get-tuple-element.152.refs_2_.refs_1_, bf16[1024,512]{1,0:T(8,128)(2,1)} %get-tuple-element.153.refs_3_.refs_2_, ...), custom_call_target="tpu_custom_call" | custom-call | flops 2147483648 | bytes 10518528 | tf_op jit(solution)/shard_map/attention_forward/pallas_call | solution.py:199
  79.2 17.8 %gated_convolution.1 = (bf16[1024,512]{1,0:T(8,128)(2,1)}, bf16[1024,1024]{1,0:T(8,128)(2,1)}, f32[1024,512]{1,0:T(8,128)}, f32[4,1120,128]{2,1,0:T(8,128)}, f32[3,512]{1,0:T(4,128)}) custom-call(s32[4]{0:T(128)S(1)} %bitcast.52, s32[1]{0:T(128)} %bitcast.2.refs_0_.refs_1_, s32[3,128]{1,0:T(4,128)S(1)} %add_add_fusion.refs_2_.refs_1_, ...), custom_call_target="tpu_custom_call" | custom-call | flops 2147483648 | bytes 11302912 | tf_op jit(solution)/shard_map/gated_convolution/pallas_call | solution.py:199
  97.0 3.4 collective-permute-start.13
  101.3 16.9 %all_to_all.10.refs_3_ = f32[32,3,512]{2,1,0:T(4,128)} all-to-all(f32[32,3,512]{2,1,0:T(4,128)S(1)} %broadcast_in_dim.16), channel_id=1, replica_groups=mesh['dp'=8,'fsdp'=4] {'dp','fsdp'}, dimensions={0} | all-to-all | bytes 393216 | tf_op jit(solution)/shard_map/all_to_all | solution.py:1245
  119.6 22.6 %norm_feed_forward_and_back.1 = (bf16[1024,512]{1,0:T(8,128)(2,1)}, f32[1024,512]{1,0:T(8,128)}, f32[1024,512]{1,0:T(8,128)}, bf16[1024,512]{1,0:T(8,128)(2,1)},...) custom-call(s32[4]{0:T(128)S(1)} %bitcast.53, ...), custom_call_target="tpu_custom_call" | custom-call | flops 9663676416 | bytes 29075456 | tf_op jit(solution)/shard_map/norm_feed_forward_and_back/pallas_call | solution.py:199
  143.6 2.6 all-to-all-start.1
  146.2 10.8 %weight_grad_late.1 = (bf16[2,1024,512]{2,1,0:T(8,128)(2,1)}, bf16[2,1024,512]{2,1,0:T(8,128)(2,1)}) custom-call(s32[1]{0:T(128)} %bitcast.2.refs_0_.refs_1_, bf16[1024,512]{1,0:T(8,128)(2,1)} %get-tuple-element.164.refs_1_, bf16[1024,2048]{1,0:T(8,128)(2,1)} %get-tuple-element.165.refs_2_, bf16[1024,2048]{1,0:T(8,128)(2,1)} %get-tuple-element.166.refs_3_, ...), custom_call_target="tpu_custom_call" | custom-call | flops 4294967296 | bytes 14680064 | tf_op jit(solution)/shard_map/weight_grad_late/pallas_call | solution.py:199
  158.8 15.7 %convolution_backward.1 = (f32[4,1120,128]{2,1,0:T(8,128)}, f32[4,32,128]{2,1,0:T(8,128)S(1)}) custom-call(s32[4]{0:T(128)S(1)} %bitcast.54, s32[3,128]{1,0:T(4,128)S(1)} %add_add_fusion.refs_2_.refs_1_, f32[1024,512]{1,0:T(8,128)S(1)} %copy-done.23, f32[1024,512]{1,0:T(8,128)S(1)} %copy-done.21, f32[3,512]{1,0:T(4,128)S(1)} %copy-done.24, ...), custom_call_target="tpu_custom_call" | custom-call | flops 8053063680 | bytes 9074688 | tf_op jit(solution)/shard_map/convolution_backward/pallas_call | solution.py:231
  178.4 11.5 %gates_backward.1 = (bf16[1024,1024]{1,0:T(8,128)(2,1)}, f32[1024,512]{1,0:T(8,128)}, bf16[1024,512]{1,0:T(8,128)(2,1)}, bf16[1024,512]{1,0:T(8,128)(2,1)}, f32[8,1024]{1,0:T(8,128)}, /*index=5*/f32[2,512]{1,0:T(2,128)}) custom-call(s32[4]{0:T(128)S(1)} %bitcast.55, s32[1]{0:T(128)} %bitcast.2.refs_0_.refs_1_, s32[3,128]{1,0:T(4,128)S(1)} %add_add_fusion.refs_2_.refs_1_, ...), custom_call_target="tpu_custom_call" | custom-call | flops 1610612736 | bytes 19656704 | tf_op jit(solution)/shard_map/gates_backward/pallas_call | solution.py:199
  189.9 5.8 %weight_grad_conv.1 = (bf16[2,384,512]{2,1,0:T(8,128)(2,1)}, bf16[2,384,512]{2,1,0:T(8,128)(2,1)}) custom-call(s32[1]{0:T(128)} %bitcast.2.refs_0_.refs_1_, bf16[1024,512]{1,0:T(8,128)(2,1)} %get-tuple-element.181.refs_1_, bf16[1024,1024]{1,0:T(8,128)(2,1)} %get-tuple-element.182.refs_2_, bf16[1024,512]{1,0:T(8,128)(2,1)} %get-tuple-element.183.refs_3_, ...), custom_call_target="tpu_custom_call" | custom-call | flops 1610612736 | bytes 6815744 | tf_op jit(solution)/shard_map/weight_grad_conv/pallas_call | solution.py:199
  195.8 12.6 %attention_backward.2.refs_2_.refs_1_ = bf16[1024,768]{1,0:T(8,128)(2,1)} custom-call(s32[4]{0:T(128)S(1)} %bitcast.56, bf16[1024,512]{1,0:T(8,128)(2,1)} %get-tuple-element.152.refs_2_.refs_1_, bf16[1024,512]{1,0:T(8,128)(2,1)} %get-tuple-element.153.refs_3_.refs_2_, bf16[512,1024]{1,0:T(8,128)(2,1)} %get-tuple-element.162.refs_3_, ...), custom_call_target="tpu_custom_call" | custom-call | flops 2684354560 | bytes 7929856 | tf_op jit(solution)/shard_map/attention_backward/pallas_call | solution.py:199
  213.3 3.3 collective-permute-start.19
  216.6 12.8 %attention_backward.3.refs_3_.refs_2_ = bf16[1024,768]{1,0:T(8,128)(2,1)} custom-call(s32[4]{0:T(128)S(1)} %bitcast.57, bf16[1024,512]{1,0:T(8,128)(2,1)} %get-tuple-element.152.refs_2_.refs_1_, bf16[1024,512]{1,0:T(8,128)(2,1)} %get-tuple-element.153.refs_3_.refs_2_, bf16[512,1024]{1,0:T(8,128)(2,1)} %get-tuple-element.162.refs_3_, ...), custom_call_target="tpu_custom_call" | custom-call | flops 2684354560 | bytes 7929856 | tf_op jit(solution)/shard_map/attention_backward/pallas_call | solution.py:199
  229.4 1.9 add_convert_fusion.12
  232.5 7.2 %weight_grad_attn.1 = (bf16[2,512,512]{2,1,0:T(8,128)(2,1)}, bf16[2,512,512]{2,1,0:T(8,128)(2,1)}) custom-call(s32[1]{0:T(128)} %bitcast.2.refs_0_.refs_1_, bf16[1024,512]{1,0:T(8,128)(2,1)} %get-tuple-element.196.refs_1_, bf16[1024,768]{1,0:T(8,128)(2,1)} %attention_backward.2.refs_2_.refs_1_, bf16[1024,768]{1,0:T(8,128)(2,1)} %attention_backward.3.refs_3_.refs_2_, ...), custom_call_target="tpu_custom_call" | custom-call | flops 2147483648 | bytes 8388608 | tf_op jit(solution)/shard_map/weight_grad_attn/pallas_call | solution.py:199
  239.7 2.0 collective-permute-start.22
  242.0 2.0 collective-permute-start.20
  244.0 8.7 %query_key_value_backward.1 = (f32[1024,512]{1,0:T(8,128)}, bf16[1024,512]{1,0:T(8,128)(2,1)}, f32[2,512]{1,0:T(2,128)}) custom-call(s32[1]{0:T(128)} %bitcast.2.refs_0_.refs_1_, bf16[1024,768]{1,0:T(8,128)(2,1)} %attention_backward.2.refs_2_.refs_1_, bf16[1024,768]{1,0:T(8,128)(2,1)} %attention_backward.3.refs_3_.refs_2_, ...), custom_call_target="tpu_custom_call" | custom-call | flops 1610612736 | bytes 12611584 | tf_op jit(solution)/shard_map/query_key_value_backward/pallas_call | solution.py:199
  256.4 6.8 %weight_grad_shrink.1 = (bf16[2,512,512]{2,1,0:T(8,128)(2,1)}, bf16[2,512,512]{2,1,0:T(8,128)(2,1)}) custom-call(s32[1]{0:T(128)} %bitcast.2.refs_0_.refs_1_, bf16[1024,2048]{1,0:T(8,128)(2,1)} %get-tuple-element.203.refs_1_, bf16[1024,512]{1,0:T(8,128)(2,1)} %get-tuple-element.211.refs_2_), custom_call_target="tpu_custom_call" | custom-call | flops 2147483648 | bytes 7340032 | tf_op jit(solution)/shard_map/weight_grad_shrink/pallas_call | solution.py:199
  269.4 3.0 collective-permute-start.26
  272.4 3.8 %collective-permute-done.27 = bf16[1,96,512]{2,1,0:T(8,128)(2,1)S(1)} collective-permute-done((bf16[1,96,512]{2,1,0:T(8,128)(2,1)S(1)}, bf16[1,96,512]{2,1,0:T(8,128)(2,1)S(1)}, u32[]{:S(2)}, u32[]{:S(2)}) %collective-permute-start.27) | collective-permute-done | bytes 98336 | tf_op jit(solution)/shard_map/ppermute | solution.py:1141
  276.3 14.0 %feed_forward_backward.1 = (f32[1024,512]{1,0:T(8,128)}, bf16[1024,2048]{1,0:T(8,128)(2,1)}, f32[44,512]{1,0:T(8,128)}) custom-call(s32[1]{0:T(128)} %bitcast.2.refs_0_.refs_1_, f32[1024,512]{1,0:T(8,128)} %get-tuple-element.201.refs_1_, bf16[1024,512]{1,0:T(8,128)(2,1)} %get-tuple-element.211.refs_2_, bf16[1024,512]{1,0:T(8,128)(2,1)} %refs_3_.6, ...), custom_call_target="tpu_custom_call" | custom-call | flops 4294967296 | bytes 19075072 | tf_op jit(solution)/shard_map/feed_forward_backward/pallas_call | solution.py:199
  292.6 6.9 %weight_grad_expand.1 = (bf16[2,528,512]{2,1,0:T(8,128)(2,1)}, bf16[2,528,512]{2,1,0:T(8,128)(2,1)}) custom-call(s32[1]{0:T(128)} %bitcast.2.refs_0_.refs_1_, bf16[1024,512]{1,0:T(8,128)(2,1)} %get-tuple-element.217.refs_1_, bf16[1024,2048]{1,0:T(8,128)(2,1)} %get-tuple-element.224.refs_2_, bf16[4,16,512]{2,1,0:T(8,128)(2,1)} %bitcast.61), custom_call_target="tpu_custom_call" | custom-call | flops 2147483648 | bytes 7471104 | tf_op jit(solution)/shard_map/weight_grad_expand/pallas_call | solution.py:199
  299.7 2.9 collective-permute-done.28
  312.7 2.1 collective-permute-start.35
  314.8 3.5 collective-permute-done.48
  321.2 2.1 collective-permute-done.37
  327.4 2.1 adam_conv.1
  331.8 2.6 collective-permute-start.44
  335.0 8.1 %collective-permute-done.30 = bf16[1,264,512]{2,1,0:T(8,128)(2,1)S(1)} collective-permute-done((bf16[1,264,512]{2,1,0:T(8,128)(2,1)S(1)}, bf16[1,264,512]{2,1,0:T(8,128)(2,1)S(1)}, u32[]{:S(2)}, u32[]{:S(2)}) %collective-permute-start.30) | collective-permute-done | bytes 270368 | tf_op jit(solution)/shard_map/ppermute | solution.py:1141
  343.4 2.1 collective-permute-start.45
  345.5 3.2 collective-permute-done.31
  348.9 3.0 collective-permute-start.32
  352.0 4.0 %collective-permute-done.32 = bf16[1,132,512]{2,1,0:T(8,128)(2,1)S(1)} collective-permute-done((bf16[1,132,512]{2,1,0:T(8,128)(2,1)S(1)}, bf16[1,132,512]{2,1,0:T(8,128)(2,1)S(1)}, u32[]{:S(2)}, u32[]{:S(2)}) %collective-permute-start.32) | collective-permute-done | bytes 135200 | tf_op jit(solution)/shard_map/ppermute | solution.py:1141
  363.4 3.8 adam_late.1
  367.5 2.8 adam_attn.1
  370.5 2.5 adam_shrink.1
  374.9 4.2 %adam_expand.1 = (f32[2,128,2048]{2,1,0:T(8,128)}, f32[2,128,2048]{2,1,0:T(8,128)}, f32[2,128,2048]{2,1,0:T(8,128)}) custom-call(bf16[528,512]{1,0:T(8,128)(2,1)S(1)} %maximum_select_fusion.1.refs_0_, f32[2,128,2048]{2,1,0:T(8,128)S(1)} %copy-done.1, f32[2,128,2048]{2,1,0:T(8,128)S(1)} %copy-done.5, ...), custom_call_target="tpu_custom_call", output_to_operand_aliasing={{0}: (4, {}), {1}: (5, {}), {2}: (6, {})} | custom-call | flops 5242880 | bytes 6815744 | tf_op jit(solution)/shard_map/adam_expand/pallas_call | solution.py:1305
  (281 shorter events, 72.3 us)
Async XLA Ops:
  3.4 14.4 %collective-permute-start = (bf16[44,128]{1,0:T(8,128)(2,1)S(1)}, bf16[44,128]{1,0:T(8,128)(2,1)S(1)}, u32[]{:S(2)}, u32[]{:S(2)}) collective-permute-start(bf16[44,128]{1,0:T(8,128)(2,1)S(1)} %pad_maximum_fusion.2), channel_id=1, source_target_pairs={{0,2},{1,3},{2,0},{3,1},{4,6},{5,7},{6,4},{7,5},{8,10},{9,11},{10,... | collective-permute-start | bytes 33800 | tf_op jit(solution)/shard_map/ppermute | solution.py:1141
  6.4 11.6 %collective-permute-start.1 = (bf16[44,128]{1,0:T(8,128)(2,1)S(1)}, bf16[44,128]{1,0:T(8,128)(2,1)S(1)}, u32[]{:S(2)}, u32[]{:S(2)}) collective-permute-start(bf16[44,128]{1,0:T(8,128)(2,1)S(1)} %pad_maximum_fusion.2), channel_id=1, source_target_pairs={{0,1},{1,0},{2,3},{3,2},{4,5},{5,4},{6,7},{7,6},{8,9},{9,8},{10,11... | collective-permute-start | bytes 33800 | tf_op jit(solution)/shard_map/ppermute | solution.py:1141
  6.4 25.8 %collective-permute-start.3 = (bf16[1024,512]{1,0:T(8,128)(2,1)}, bf16[1024,512]{1,0:T(8,128)(2,1)S(1)}, u32[]{:S(2)}, u32[]{:S(2)}) collective-permute-start(bf16[1024,512]{1,0:T(8,128)(2,1)} %pack_early.1.refs_3_.refs_10_), channel_id=1, source_target_pairs={{0,2},{1,3},{2,0},{3,1},{4,6},{5,7},{6,4},{7,5},{8,10},{9,11},{10,... | collective-permute-start | bytes 3145736 | tf_op jit(solution)/shard_map/ppermute | solution.py:1141
  6.6 26.1 %collective-permute-start.4 = (bf16[1024,512]{1,0:T(8,128)(2,1)}, bf16[1024,512]{1,0:T(8,128)(2,1)S(1)}, u32[]{:S(2)}, u32[]{:S(2)}) collective-permute-start(bf16[1024,512]{1,0:T(8,128)(2,1)} %pack_early.1.refs_3_.refs_10_), channel_id=1, source_target_pairs={{0,1},{1,0},{2,3},{3,2},{4,5},{5,4},{6,7},{7,6},{8,9},{9,8},{10,11... | collective-permute-start | bytes 3145736 | tf_op jit(solution)/shard_map/ppermute | solution.py:1141
  32.2 2.7 collective-permute-start.5
  32.2 14.6 %collective-permute-start.6 = (bf16[512,512]{1,0:T(8,128)(2,1)S(1)}, bf16[512,512]{1,0:T(8,128)(2,1)S(1)}, u32[]{:S(2)}, u32[]{:S(2)}) collective-permute-start(bf16[512,512]{1,0:T(8,128)(2,1)S(1)} %copy-done.25), channel_id=1, source_target_pairs={{0,2},{1,3},{2,0},{3,1},{4,6},{5,7},{6,4},{7,5},{8,10},{9,11},{10,... | collective-permute-start | bytes 1572872 | tf_op jit(solution)/shard_map/ppermute | solution.py:1141
  47.1 2.5 collective-permute-start.7
  47.4 11.5 %collective-permute-start.9 = (bf16[384,512]{1,0:T(8,128)(2,1)S(1)}, bf16[384,512]{1,0:T(8,128)(2,1)S(1)}, u32[]{:S(2)}, u32[]{:S(2)}) collective-permute-start(bf16[384,512]{1,0:T(8,128)(2,1)S(1)} %copy-done.31), channel_id=1, source_target_pairs={{0,2},{1,3},{2,0},{3,1},{4,6},{5,7},{6,4},{7,5},{8,10},{9,11},{10,... | collective-permute-start | bytes 1179656 | tf_op jit(solution)/shard_map/ppermute | solution.py:1141
  58.9 41.5 %collective-permute-start.12 = (bf16[1024,512]{1,0:T(8,128)(2,1)}, bf16[1024,512]{1,0:T(8,128)(2,1)S(1)}, u32[]{:S(2)}, u32[]{:S(2)}) collective-permute-start(bf16[1024,512]{1,0:T(8,128)(2,1)} %pack_late.1.refs_11_), channel_id=1, source_target_pairs={{0,2},{1,3},{2,0},{3,1},{4,6},{5,7},{6,4},{7,5},{8,10},{9,11},{10,... | collective-permute-start | bytes 3145736 | tf_op jit(solution)/shard_map/ppermute | solution.py:1141
  59.6 2.4 collective-permute-start.10
  97.0 21.2 %collective-permute-start.13 = (bf16[1024,512]{1,0:T(8,128)(2,1)}, bf16[1024,512]{1,0:T(8,128)(2,1)S(1)}, u32[]{:S(2)}, u32[]{:S(2)}) collective-permute-start(bf16[1024,512]{1,0:T(8,128)(2,1)} %pack_late.1.refs_11_), channel_id=1, source_target_pairs={{0,1},{1,0},{2,3},{3,2},{4,5},{5,4},{6,7},{7,6},{8,9},{9,8},{10,11... | collective-permute-start | bytes 3145736 | tf_op jit(solution)/shard_map/ppermute | solution.py:1141
  100.4 17.8 %collective-permute-start.14 = (bf16[1024,512]{1,0:T(8,128)(2,1)S(1)}, bf16[1024,512]{1,0:T(8,128)(2,1)S(1)}, u32[]{:S(2)}, u32[]{:S(2)}) collective-permute-start(bf16[1024,512]{1,0:T(8,128)(2,1)S(1)} %collective-permute-done.12.refs_12_), channel_id=1, source_target_pairs={{0,1},{1,0},{2,3},{3,2},{4,5},{5,4},{6,7},{7,6},{8,9},{9,8},{10,11... | collective-permute-start | bytes 3145736 | tf_op jit(solution)/shard_map/ppermute | solution.py:1141
  143.6 13.5 %all-to-all-start.1 = ((f32[32,2,512]{2,1,0:T(2,128)}), f32[32,2,512]{2,1,0:T(2,128)S(1)}, u32[]{:S(2)}, u32[]{:S(2)}) async-start(f32[32,2,512]{2,1,0:T(2,128)} %broadcast_in_dim.17), calls=%async_computation.1 | async-start | bytes 262144 | tf_op jit(solution)/shard_map/all_to_all | solution.py:1245
  157.1 18.0 %collective-permute-start.15 = (bf16[2,1024,512]{2,1,0:T(8,128)(2,1)}, bf16[2,1024,512]{2,1,0:T(8,128)(2,1)}, u32[]{:S(2)}, u32[]{:S(2)}) collective-permute-start(bf16[2,1024,512]{2,1,0:T(8,128)(2,1)} %get-tuple-element.175), channel_id=1, source_target_pairs={{0,1},{1,0},{2,3},{3,2},{4,5},{5,4},{6,7},{7,6},{8,9},{9,8},{10,11... | collective-permute-start | bytes 6291464 | tf_op jit(solution)/shard_map/ppermute | solution.py:1141
  176.6 31.8 %collective-permute-start.16 = (bf16[1,1024,512]{2,1,0:T(8,128)(2,1)S(1)}, bf16[1,1024,512]{2,1,0:T(8,128)(2,1)}, u32[]{:S(2)}, u32[]{:S(2)}) collective-permute-start(bf16[1,1024,512]{2,1,0:T(8,128)(2,1)S(1)} %add_convert_fusion), channel_id=1, source_target_pairs={{0,2},{1,3},{2,0},{3,1},{4,6},{5,7},{6,4},{7,5},{8,10},{9,11},{10,... | collective-permute-start | bytes 3145736 | tf_op jit(solution)/shard_map/ppermute | solution.py:1141
  195.7 12.7 %collective-permute-start.18 = (bf16[2,384,512]{2,1,0:T(8,128)(2,1)}, bf16[2,384,512]{2,1,0:T(8,128)(2,1)}, u32[]{:S(2)}, u32[]{:S(2)}) collective-permute-start(bf16[2,384,512]{2,1,0:T(8,128)(2,1)} %get-tuple-element.185), channel_id=1, source_target_pairs={{0,1},{1,0},{2,3},{3,2},{4,5},{5,4},{6,7},{7,6},{8,9},{9,8},{10,11... | collective-permute-start | bytes 2359304 | tf_op jit(solution)/shard_map/ppermute | solution.py:1141
  209.9 21.4 %collective-permute-start.17 = (bf16[1,512,512]{2,1,0:T(8,128)(2,1)S(1)}, bf16[1,512,512]{2,1,0:T(8,128)(2,1)S(1)}, u32[]{:S(2)}, u32[]{:S(2)}) collective-permute-start(bf16[1,512,512]{2,1,0:T(8,128)(2,1)S(1)} %add_convert_fusion.4), channel_id=1, source_target_pairs={{0,4},{4,0},{8,12},{12,8},{16,20},{20,16},{24,28},{28,24},{1,5},{5... | collective-permute-start | bytes 1572872 | tf_op jit(solution)/shard_map/ppermute | solution.py:1141
  213.3 16.1 %collective-permute-start.19 = (bf16[1,384,512]{2,1,0:T(8,128)(2,1)}, bf16[1,384,512]{2,1,0:T(8,128)(2,1)}, u32[]{:S(2)}, u32[]{:S(2)}) collective-permute-start(bf16[1,384,512]{2,1,0:T(8,128)(2,1)} %add_convert_fusion.5), channel_id=1, source_target_pairs={{0,2},{1,3},{2,0},{3,1},{4,6},{5,7},{6,4},{7,5},{8,10},{9,11},{10,... | collective-permute-start | bytes 1179656 | tf_op jit(solution)/shard_map/ppermute | solution.py:1141
  239.7 15.5 %collective-permute-start.22 = (bf16[2,512,512]{2,1,0:T(8,128)(2,1)}, bf16[2,512,512]{2,1,0:T(8,128)(2,1)}, u32[]{:S(2)}, u32[]{:S(2)}) collective-permute-start(bf16[2,512,512]{2,1,0:T(8,128)(2,1)} %get-tuple-element.198), channel_id=1, source_target_pairs={{0,1},{1,0},{2,3},{3,2},{4,5},{5,4},{6,7},{7,6},{8,9},{9,8},{10,11... | collective-permute-start | bytes 3145736 | tf_op jit(solution)/shard_map/ppermute | solution.py:1141
  241.7 11.1 %collective-permute-start.21 = (bf16[1,192,512]{2,1,0:T(8,128)(2,1)}, bf16[1,192,512]{2,1,0:T(8,128)(2,1)S(1)}, u32[]{:S(2)}, u32[]{:S(2)}) collective-permute-start(bf16[1,192,512]{2,1,0:T(8,128)(2,1)} %add_convert_fusion.12), channel_id=1, source_target_pairs={{0,4},{4,0},{8,12},{12,8},{16,20},{20,16},{24,28},{28,24},{1,5},{5... | collective-permute-start | bytes 589832 | tf_op jit(solution)/shard_map/ppermute | solution.py:1141
  242.0 11.9 %collective-permute-start.20 = (bf16[1,256,512]{2,1,0:T(8,128)(2,1)S(1)}, bf16[1,256,512]{2,1,0:T(8,128)(2,1)S(1)}, u32[]{:S(2)}, u32[]{:S(2)}) collective-permute-start(bf16[1,256,512]{2,1,0:T(8,128)(2,1)S(1)} %add_convert_fusion.11), channel_id=1, source_target_pairs={{0,8},{4,12},{8,0},{12,4},{16,24},{20,28},{24,16},{28,20},{1,9},{5... | collective-permute-start | bytes 786440 | tf_op jit(solution)/shard_map/ppermute | solution.py:1141
  263.2 2.9 collective-permute-start.23
  263.2 27.1 %collective-permute-start.24 = (bf16[1,512,512]{2,1,0:T(8,128)(2,1)S(1)}, bf16[1,512,512]{2,1,0:T(8,128)(2,1)}, u32[]{:S(2)}, u32[]{:S(2)}) collective-permute-start(bf16[1,512,512]{2,1,0:T(8,128)(2,1)S(1)} %add_convert_fusion.3), channel_id=1, source_target_pairs={{0,2},{1,3},{2,0},{3,1},{4,6},{5,7},{6,4},{7,5},{8,10},{9,11},{10,... | collective-permute-start | bytes 1572872 | tf_op jit(solution)/shard_map/ppermute | solution.py:1141
  267.6 25.0 %collective-permute-start.25 = (bf16[1,512,512]{2,1,0:T(8,128)(2,1)S(1)}, bf16[1,512,512]{2,1,0:T(8,128)(2,1)S(1)}, u32[]{:S(2)}, u32[]{:S(2)}) collective-permute-start(bf16[1,512,512]{2,1,0:T(8,128)(2,1)S(1)} %add_convert_fusion.2), channel_id=1, source_target_pairs={{0,2},{1,3},{2,0},{3,1},{4,6},{5,7},{6,4},{7,5},{8,10},{9,11},{10,... | collective-permute-start | bytes 1572872 | tf_op jit(solution)/shard_map/ppermute | solution.py:1141
  269.1 7.2 %collective-permute-start.27 = (bf16[1,96,512]{2,1,0:T(8,128)(2,1)S(1)}, bf16[1,96,512]{2,1,0:T(8,128)(2,1)S(1)}, u32[]{:S(2)}, u32[]{:S(2)}) collective-permute-start(bf16[1,96,512]{2,1,0:T(8,128)(2,1)S(1)} %add_convert_fusion.24), channel_id=1, source_target_pairs={{0,8},{4,12},{8,0},{12,4},{16,24},{20,28},{24,16},{28,20},{1,9},{5... | collective-permute-start | bytes 294920 | tf_op jit(solution)/shard_map/ppermute | solution.py:1141
  269.4 20.9 %collective-permute-start.26 = (bf16[1,256,512]{2,1,0:T(8,128)(2,1)S(1)}, bf16[1,256,512]{2,1,0:T(8,128)(2,1)S(1)}, u32[]{:S(2)}, u32[]{:S(2)}) collective-permute-start(bf16[1,256,512]{2,1,0:T(8,128)(2,1)S(1)} %add_convert_fusion.10), channel_id=1, source_target_pairs={{0,16},{4,20},{8,24},{12,28},{16,0},{20,4},{24,8},{28,12},{1,17},{... | collective-permute-start | bytes 786440 | tf_op jit(solution)/shard_map/ppermute | solution.py:1141
  299.6 3.0 collective-permute-start.28
  303.8 25.8 %collective-permute-start.29 = (bf16[1,528,512]{2,1,0:T(8,128)(2,1)S(1)}, bf16[1,528,512]{2,1,0:T(8,128)(2,1)S(1)}, u32[]{:S(2)}, u32[]{:S(2)}) collective-permute-start(bf16[1,528,512]{2,1,0:T(8,128)(2,1)S(1)} %add_convert_fusion.1), channel_id=1, source_target_pairs={{0,2},{1,3},{2,0},{3,1},{4,6},{5,7},{6,4},{7,5},{8,10},{9,11},{10,... | collective-permute-start | bytes 1622024 | tf_op jit(solution)/shard_map/ppermute | solution.py:1141
  306.0 6.5 %collective-permute-start.47 = (bf16[1,96,512]{2,1,0:T(8,128)(2,1)S(1)}, bf16[1,96,512]{2,1,0:T(8,128)(2,1)S(1)}, u32[]{:S(2)}, u32[]{:S(2)}) collective-permute-start(bf16[1,96,512]{2,1,0:T(8,128)(2,1)S(1)} %add_convert_fusion.23), channel_id=1, source_target_pairs={{0,16},{4,20},{8,24},{12,28},{16,0},{20,4},{24,8},{28,12},{1,17},{... | collective-permute-start | bytes 294920 | tf_op jit(solution)/shard_map/ppermute | solution.py:1141
  308.4 11.5 %collective-permute-start.42 = (bf16[1,256,512]{2,1,0:T(8,128)(2,1)S(1)}, bf16[1,256,512]{2,1,0:T(8,128)(2,1)S(1)}, u32[]{:S(2)}, u32[]{:S(2)}) collective-permute-start(bf16[1,256,512]{2,1,0:T(8,128)(2,1)S(1)} %add_convert_fusion.7), channel_id=1, source_target_pairs={{0,4},{4,0},{8,12},{12,8},{16,20},{20,16},{24,28},{28,24},{1,5},{5... | collective-permute-start | bytes 786440 | tf_op jit(solution)/shard_map/ppermute | solution.py:1141
  310.5 12.8 %collective-permute-start.37 = (bf16[1,256,512]{2,1,0:T(8,128)(2,1)S(1)}, bf16[1,256,512]{2,1,0:T(8,128)(2,1)S(1)}, u32[]{:S(2)}, u32[]{:S(2)}) collective-permute-start(bf16[1,256,512]{2,1,0:T(8,128)(2,1)S(1)} %add_convert_fusion.8), channel_id=1, source_target_pairs={{0,4},{4,0},{8,12},{12,8},{16,20},{20,16},{24,28},{28,24},{1,5},{5... | collective-permute-start | bytes 786440 | tf_op jit(solution)/shard_map/ppermute | solution.py:1141
  312.6 5.7 %collective-permute-start.48 = (bf16[96,512]{1,0:T(8,128)(2,1)S(1)}, bf16[96,512]{1,0:T(8,128)(2,1)S(1)}, u32[]{:S(2)}, u32[]{:S(2)}) collective-permute-start(bf16[96,512]{1,0:T(8,128)(2,1)S(1)} %fusion.5), channel_id=1, source_target_pairs={{0,8},{4,12},{8,0},{12,4},{16,24},{20,28},{24,16},{28,20},{1,9},{5... | collective-permute-start | bytes 294920 | tf_op jit(solution)/shard_map/ppermute | solution.py:1141
  312.7 11.2 %collective-permute-start.35 = (bf16[256,512]{1,0:T(8,128)(2,1)S(1)}, bf16[256,512]{1,0:T(8,128)(2,1)S(1)}, u32[]{:S(2)}, u32[]{:S(2)}) collective-permute-start(bf16[256,512]{1,0:T(8,128)(2,1)S(1)} %fusion), channel_id=1, source_target_pairs={{0,8},{4,12},{8,0},{12,4},{16,24},{20,28},{24,16},{28,20},{1,9},{5... | collective-permute-start | bytes 786440 | tf_op jit(solution)/shard_map/ppermute | solution.py:1141
  318.3 8.9 %collective-permute-start.49 = (bf16[192,512]{1,0:T(8,128)(2,1)S(1)}, bf16[192,512]{1,0:T(8,128)(2,1)S(1)}, u32[]{:S(2)}, u32[]{:S(2)}) collective-permute-start(bf16[192,512]{1,0:T(8,128)(2,1)S(1)} %maximum_select_fusion.9), channel_id=1, source_target_pairs={{0,4},{4,0},{8,12},{12,8},{16,20},{20,16},{24,28},{28,24},{1,5},{5... | collective-permute-start | bytes 589832 | tf_op jit(solution)/shard_map/ppermute | solution.py:1141
  321.1 9.6 %collective-permute-start.43 = (bf16[1,128,512]{2,1,0:T(8,128)(2,1)S(1)}, bf16[1,128,512]{2,1,0:T(8,128)(2,1)S(1)}, u32[]{:S(2)}, u32[]{:S(2)}) collective-permute-start(bf16[1,128,512]{2,1,0:T(8,128)(2,1)S(1)} %add_convert_fusion.18), channel_id=1, source_target_pairs={{0,8},{4,12},{8,0},{12,4},{16,24},{20,28},{24,16},{28,20},{1,9},{5... | collective-permute-start | bytes 393224 | tf_op jit(solution)/shard_map/ppermute | solution.py:1141
  323.4 11.0 %collective-permute-start.38 = (bf16[1,128,512]{2,1,0:T(8,128)(2,1)S(1)}, bf16[1,128,512]{2,1,0:T(8,128)(2,1)S(1)}, u32[]{:S(2)}, u32[]{:S(2)}) collective-permute-start(bf16[1,128,512]{2,1,0:T(8,128)(2,1)S(1)} %add_convert_fusion.21), channel_id=1, source_target_pairs={{0,8},{4,12},{8,0},{12,4},{16,24},{20,28},{24,16},{28,20},{1,9},{5... | collective-permute-start | bytes 393224 | tf_op jit(solution)/shard_map/ppermute | solution.py:1141
  324.1 38.7 %collective-permute-start.36 = (bf16[512,512]{1,0:T(8,128)(2,1)S(1)}, bf16[512,512]{1,0:T(8,128)(2,1)S(1)}, u32[]{:S(2)}, u32[]{:S(2)}) collective-permute-start(bf16[512,512]{1,0:T(8,128)(2,1)S(1)} %maximum_select_fusion.2), channel_id=1, source_target_pairs={{0,4},{4,0},{8,12},{12,8},{16,20},{20,16},{24,28},{28,24},{1,5},{5... | collective-permute-start | bytes 1572872 | tf_op jit(solution)/shard_map/ppermute | solution.py:1141
  329.7 13.4 %collective-permute-start.30 = (bf16[1,264,512]{2,1,0:T(8,128)(2,1)S(1)}, bf16[1,264,512]{2,1,0:T(8,128)(2,1)S(1)}, u32[]{:S(2)}, u32[]{:S(2)}) collective-permute-start(bf16[1,264,512]{2,1,0:T(8,128)(2,1)S(1)} %add_convert_fusion.6), channel_id=1, source_target_pairs={{0,4},{4,0},{8,12},{12,8},{16,20},{20,16},{24,28},{28,24},{1,5},{5... | collective-permute-start | bytes 811016 | tf_op jit(solution)/shard_map/ppermute | solution.py:1141
  331.8 11.5 %collective-permute-start.44 = (bf16[1,128,512]{2,1,0:T(8,128)(2,1)S(1)}, bf16[1,128,512]{2,1,0:T(8,128)(2,1)S(1)}, u32[]{:S(2)}, u32[]{:S(2)}) collective-permute-start(bf16[1,128,512]{2,1,0:T(8,128)(2,1)S(1)} %add_convert_fusion.17), channel_id=1, source_target_pairs={{0,16},{4,20},{8,24},{12,28},{16,0},{20,4},{24,8},{28,12},{1,17},{... | collective-permute-start | bytes 393224 | tf_op jit(solution)/shard_map/ppermute | solution.py:1141
  334.6 17.3 %collective-permute-start.39 = (bf16[1,128,512]{2,1,0:T(8,128)(2,1)S(1)}, bf16[1,128,512]{2,1,0:T(8,128)(2,1)S(1)}, u32[]{:S(2)}, u32[]{:S(2)}) collective-permute-start(bf16[1,128,512]{2,1,0:T(8,128)(2,1)S(1)} %add_convert_fusion.20), channel_id=1, source_target_pairs={{0,16},{4,20},{8,24},{12,28},{16,0},{20,4},{24,8},{28,12},{1,17},{... | collective-permute-start | bytes 393224 | tf_op jit(solution)/shard_map/ppermute | solution.py:1141
  343.3 5.4 %collective-permute-start.31 = (bf16[1,132,512]{2,1,0:T(8,128)(2,1)S(1)}, bf16[1,132,512]{2,1,0:T(8,128)(2,1)S(1)}, u32[]{:S(2)}, u32[]{:S(2)}) collective-permute-start(bf16[1,132,512]{2,1,0:T(8,128)(2,1)S(1)} %add_convert_fusion.15), channel_id=1, source_target_pairs={{0,8},{4,12},{8,0},{12,4},{16,24},{20,28},{24,16},{28,20},{1,9},{5... | collective-permute-start | bytes 405512 | tf_op jit(solution)/shard_map/ppermute | solution.py:1141
  343.4 14.0 %collective-permute-start.45 = (bf16[128,512]{1,0:T(8,128)(2,1)S(1)}, bf16[128,512]{1,0:T(8,128)(2,1)S(1)}, u32[]{:S(2)}, u32[]{:S(2)}) collective-permute-start(bf16[128,512]{1,0:T(8,128)(2,1)S(1)} %fusion.4), channel_id=1, source_target_pairs={{0,8},{4,12},{8,0},{12,4},{16,24},{20,28},{24,16},{28,20},{1,9},{5... | collective-permute-start | bytes 393224 | tf_op jit(solution)/shard_map/ppermute | solution.py:1141
  348.9 7.1 %collective-permute-start.32 = (bf16[1,132,512]{2,1,0:T(8,128)(2,1)S(1)}, bf16[1,132,512]{2,1,0:T(8,128)(2,1)S(1)}, u32[]{:S(2)}, u32[]{:S(2)}) collective-permute-start(bf16[1,132,512]{2,1,0:T(8,128)(2,1)S(1)} %add_convert_fusion.14), channel_id=1, source_target_pairs={{0,16},{4,20},{8,24},{12,28},{16,0},{20,4},{24,8},{28,12},{1,17},{... | collective-permute-start | bytes 405512 | tf_op jit(solution)/shard_map/ppermute | solution.py:1141
  351.9 7.2 %collective-permute-start.40 = (bf16[128,512]{1,0:T(8,128)(2,1)S(1)}, bf16[128,512]{1,0:T(8,128)(2,1)S(1)}, u32[]{:S(2)}, u32[]{:S(2)}) collective-permute-start(bf16[128,512]{1,0:T(8,128)(2,1)S(1)} %fusion.3), channel_id=1, source_target_pairs={{0,8},{4,12},{8,0},{12,4},{16,24},{20,28},{24,16},{28,20},{1,9},{5... | collective-permute-start | bytes 393224 | tf_op jit(solution)/shard_map/ppermute | solution.py:1141
  356.1 5.1 %collective-permute-start.33 = (bf16[132,512]{1,0:T(8,128)(2,1)S(1)}, bf16[132,512]{1,0:T(8,128)(2,1)S(1)}, u32[]{:S(2)}, u32[]{:S(2)}) collective-permute-start(bf16[132,512]{1,0:T(8,128)(2,1)S(1)} %fusion.2), channel_id=1, source_target_pairs={{0,8},{4,12},{8,0},{12,4},{16,24},{20,28},{24,16},{28,20},{1,9},{5... | collective-permute-start | bytes 405512 | tf_op jit(solution)/shard_map/ppermute | solution.py:1141
  357.5 9.7 %collective-permute-start.46 = (bf16[256,512]{1,0:T(8,128)(2,1)S(1)}, bf16[256,512]{1,0:T(8,128)(2,1)S(1)}, u32[]{:S(2)}, u32[]{:S(2)}) collective-permute-start(bf16[256,512]{1,0:T(8,128)(2,1)S(1)} %maximum_select_fusion.8), channel_id=1, source_target_pairs={{0,4},{4,0},{8,12},{12,8},{16,20},{20,16},{24,28},{28,24},{1,5},{5... | collective-permute-start | bytes 786440 | tf_op jit(solution)/shard_map/ppermute | solution.py:1141
  359.1 11.2 %collective-permute-start.41 = (bf16[256,512]{1,0:T(8,128)(2,1)S(1)}, bf16[256,512]{1,0:T(8,128)(2,1)S(1)}, u32[]{:S(2)}, u32[]{:S(2)}) collective-permute-start(bf16[256,512]{1,0:T(8,128)(2,1)S(1)} %maximum_select_fusion.7), channel_id=1, source_target_pairs={{0,4},{4,0},{8,12},{12,8},{16,20},{20,16},{24,28},{28,24},{1,5},{5... | collective-permute-start | bytes 786440 | tf_op jit(solution)/shard_map/ppermute | solution.py:1141
  361.3 11.7 %collective-permute-start.34 = (bf16[264,512]{1,0:T(8,128)(2,1)S(1)}, bf16[264,512]{1,0:T(8,128)(2,1)S(1)}, u32[]{:S(2)}, u32[]{:S(2)}) collective-permute-start(bf16[264,512]{1,0:T(8,128)(2,1)S(1)} %maximum_select_fusion.6), channel_id=1, source_target_pairs={{0,4},{4,0},{8,12},{12,8},{16,20},{20,16},{24,28},{28,24},{1,5},{5... | collective-permute-start | bytes 811016 | tf_op jit(solution)/shard_map/ppermute | solution.py:1141
  (64 other events, 590.4 us)

commit v5 on v4

--- a/solution.py
+++ b/solution.py
@@ -193,7 +193,7 @@
     lead = len(scalars)
     cost = pl.CostEstimate(flops=int(flops), bytes_accessed=int(size), transcendentals=int(count))
     params = pltpu.CompilerParams(vmem_limit_bytes=LIMIT)
-    if piped or grid[0] > 1:
+    if piped or (grid[0] > 1 and not name.startswith("weight_grad")):
         inputs = [pltpu.with_memory_space_constraint(v, pltpu.HBM) for v in inputs]
         outs = [pltpu.HBM(v.shape, v.dtype) for v in outs]
         return pl.pallas_call(

time: 388 us -> 385 us (level)
  starting transfers between devices: 54.2 us -> 45.5 us
  Pallas kernels: 215 us -> 219 us
  other arithmetic: 29.3 us -> 33.2 us
    pallas_call x1 -> x5, Pallas kernels: 15.7 us -> 37.1 us  [run(): pl.pallas_call(kernel, in_specs=[pl.BlockSpec(memory_space=pltpu.SMEM)] *...]
    pallas_call x19 -> x15, Pallas kernels: 183 us -> 167 us  [run(): pl.pallas_call(lambda *refs: body(pl.program_id(0), *refs), grid_spec=plt...]
    ppermute x50, starting transfers between devices: 51.6 us -> 42.9 us  [swap(): return lax.ppermute(value, axis, [(k, k ^ mask) for k in range(size)])]
    convert_element_type x20, other arithmetic: 20.3 us -> 24.2 us  [sum_of(): return total.astype(bf16)]
    unnamed x125 -> x131, local copies, waits for them, and re-layouts: 9.19 us -> 10.8 us
  transfers between devices with their start and end apart: 51 -> 51, of which waited for: 17 -> 17; matrix products, arithmetic and copies ran while one was open for 7% -> 7% of each run, Pallas kernels for 43% -> 45%
where the time goes in v5:
time: 385 us; the launch traced here: 381 us
  Pallas kernels  219 us (57%)
  waiting for transfers between devices  48.7 us (13%)
  starting transfers between devices  45.5 us (12%)
  other arithmetic  33.2 us (9%)
  blocking collectives  16.8 us (4%)
  local copies, waits for them, and re-layouts  14.8 us (4%)
    pallas_call x15, Pallas kernels, run(): pl.pallas_call(lambda *refs: body(pl.program_id(0), *refs), grid_spec=plt...  167 us
    ppermute x50, waiting for transfers between devices, swap(): return lax.ppermute(value, axis, [(k, k ^ mask) for k in range(size)])  48.7 us
    ppermute x50, starting transfers between devices, swap(): return lax.ppermute(value, axis, [(k, k ^ mask) for k in range(size)])  42.9 us
    pallas_call x5, Pallas kernels, run(): pl.pallas_call(kernel, in_specs=[pl.BlockSpec(memory_space=pltpu.SMEM)] *...  37.1 us
    convert_element_type x20, other arithmetic, sum_of(): return total.astype(bf16)  24.2 us
    all_to_all x1, blocking collectives, from_everyone(): return lax.all_to_all(spread, axes, 0, 0, tiled=True)  16.8 us
    unnamed x131, local copies, waits for them, and re-layouts  10.8 us
    pallas_call x3, Pallas kernels, adam_pair(): pl.pallas_call(adam_body, grid=(n,), in_specs=specs, out_specs=[spec_a] *...  8.73 us
  transfers between devices with their start and end apart: 51, of which 17 were waited for; matrix products, arithmetic and copies ran while one was open for 7% of the time, Pallas kernels for 45%

profile of v5, /device:TPU:0, one launch (start us, length us, event | category | flops | bytes accessed | tf_op | source)
XLA Modules:
  0.0 380.8 jit_solution(6414065999062403368)
XLA Ops:
  0.7 2.7 pack_early.1.refs_3_.refs_10_
  3.4 3.0 collective-permute-start
  7.4 1.9 fusion.1
  9.3 1.8 pad_maximum_fusion
  11.2 1.9 pack_conv.1.refs_6_.refs_7_.refs_9_
  13.1 2.0 pack_attn.1.refs_5_.refs_6_.refs_13_
  15.1 2.7 pack_late.1.refs_11_
  20.3 11.9 %collective-permute-done.3.refs_4_.refs_11_ = bf16[1024,512]{1,0:T(8,128)(2,1)S(1)} collective-permute-done((bf16[1024,512]{1,0:T(8,128)(2,1)}, bf16[1024,512]{1,0:T(8,128)(2,1)S(1)}, u32[]{:S(2)}, u32[]{:S(2)}) %collective-permute-start.3) | collective-permute-done | bytes 1048608 | tf_op jit(solution)/shard_map/ppermute | solution.py:1141
  32.7 2.2 collective-permute-done.5.refs_6_.refs_13_
  35.8 11.0 %ff_forward.1 = (f32[1024,512]{1,0:T(8,128)}, bf16[1024,512]{1,0:T(8,128)(2,1)}, bf16[1024,2048]{1,0:T(8,128)(2,1)}, bf16[1024,2048]{1,0:T(8,128)(2,1)}) custom-call(s32[1]{0:T(128)} %bitcast.2.refs_0_.refs_1_, bf16[1024,512]{1,0:T(8,128)(2,1)} %refs_3_.6, f32[12,512]{1,0:T(8,128)} %bitcast.41, bf16[1024,512]{1,0:T(8,128)(2,1)} %pack_early.1.refs_3_.refs_10_, ...), custom_call_target="tpu_custom_call" | custom-call | flops 4294967296 | bytes 16801792 | tf_op jit(solution)/shard_map/ff_forward/pallas_call | solution.py:199
  50.4 8.4 %query_key_value.1 = (bf16[1024,512]{1,0:T(8,128)(2,1)}, bf16[1024,512]{1,0:T(8,128)(2,1)}, bf16[1024,512]{1,0:T(8,128)(2,1)}, bf16[1024,512]{1,0:T(8,128)(2,1)}, bf16[512,1024]{1,0:T(8,128)(2,1)}) custom-call(s32[1]{0:T(128)} %bitcast.2.refs_0_.refs_1_, f32[1024,512]{1,0:T(8,128)} %get-tuple-element.144.refs_1_.refs_5_.refs_3_, f32[12,512]{1,0:T(8,128)} %bitcast.42, ...), custom_call_target="tpu_custom_call" | custom-call | flops 1610612736 | bytes 10510336 | tf_op jit(solution)/shard_map/query_key_value/pallas_call | solution.py:199
  62.0 21.6 %attention_forward.1 = (f32[1024,512]{1,0:T(8,128)}, bf16[1024,512]{1,0:T(8,128)(2,1)}, f32[8,1024]{1,0:T(8,128)}) custom-call(s32[4]{0:T(128)S(1)} %bitcast.52, s32[1]{0:T(128)} %bitcast.2.refs_0_.refs_1_, bf16[1024,512]{1,0:T(8,128)(2,1)} %get-tuple-element.152.refs_2_.refs_1_, bf16[1024,512]{1,0:T(8,128)(2,1)} %get-tuple-element.153.refs_3_.refs_2_, ...), custom_call_target="tpu_custom_call" | custom-call | flops 2147483648 | bytes 10518528 | tf_op jit(solution)/shard_map/attention_forward/pallas_call | solution.py:199
  83.7 17.8 %gated_convolution.1 = (bf16[1024,512]{1,0:T(8,128)(2,1)}, bf16[1024,1024]{1,0:T(8,128)(2,1)}, f32[1024,512]{1,0:T(8,128)}, f32[4,1120,128]{2,1,0:T(8,128)}, f32[3,512]{1,0:T(4,128)}) custom-call(s32[4]{0:T(128)S(1)} %bitcast.53, s32[1]{0:T(128)} %bitcast.2.refs_0_.refs_1_, s32[3,128]{1,0:T(4,128)S(1)} %add_add_fusion.refs_2_.refs_1_, ...), custom_call_target="tpu_custom_call" | custom-call | flops 2147483648 | bytes 11302912 | tf_op jit(solution)/shard_map/gated_convolution/pallas_call | solution.py:199
  102.8 16.8 %all_to_all.10.refs_3_ = f32[32,3,512]{2,1,0:T(4,128)} all-to-all(f32[32,3,512]{2,1,0:T(4,128)S(1)} %broadcast_in_dim.16), channel_id=1, replica_groups=mesh['dp'=8,'fsdp'=4] {'dp','fsdp'}, dimensions={0} | all-to-all | bytes 393216 | tf_op jit(solution)/shard_map/all_to_all | solution.py:1245
  121.0 22.6 %norm_feed_forward_and_back.1 = (bf16[1024,512]{1,0:T(8,128)(2,1)}, f32[1024,512]{1,0:T(8,128)}, f32[1024,512]{1,0:T(8,128)}, bf16[1024,512]{1,0:T(8,128)(2,1)},...) custom-call(s32[4]{0:T(128)S(1)} %bitcast.54, ...), custom_call_target="tpu_custom_call" | custom-call | flops 9663676416 | bytes 29075456 | tf_op jit(solution)/shard_map/norm_feed_forward_and_back/pallas_call | solution.py:199
  145.0 2.6 all-to-all-start.1
  147.6 10.7 %weight_grad_late.1 = (bf16[2,1024,512]{2,1,0:T(8,128)(2,1)}, bf16[2,1024,512]{2,1,0:T(8,128)(2,1)}) custom-call(s32[1]{0:T(128)} %bitcast.2.refs_0_.refs_1_, bf16[1024,512]{1,0:T(8,128)(2,1)} %get-tuple-element.164.refs_1_, bf16[1024,2048]{1,0:T(8,128)(2,1)} %get-tuple-element.165.refs_2_, bf16[1024,2048]{1,0:T(8,128)(2,1)} %get-tuple-element.166.refs_3_, ...), custom_call_target="tpu_custom_call" | custom-call | flops 4294967296 | bytes 14680064 | tf_op jit(solution)/shard_map/weight_grad_late/pallas_call | solution.py:199
  161.7 15.7 %convolution_backward.1 = (f32[4,1120,128]{2,1,0:T(8,128)}, f32[4,32,128]{2,1,0:T(8,128)S(1)}) custom-call(s32[4]{0:T(128)S(1)} %bitcast.55, s32[3,128]{1,0:T(4,128)S(1)} %add_add_fusion.refs_2_.refs_1_, f32[1024,512]{1,0:T(8,128)S(1)} %copy-done.32, f32[1024,512]{1,0:T(8,128)S(1)} %copy-done.30, f32[3,512]{1,0:T(4,128)S(1)} %copy-done.33, ...), custom_call_target="tpu_custom_call" | custom-call | flops 8053063680 | bytes 9074688 | tf_op jit(solution)/shard_map/convolution_backward/pallas_call | solution.py:231
  178.9 1.8 collective-permute-start.16
  180.7 11.8 %gates_backward.1 = (bf16[1024,1024]{1,0:T(8,128)(2,1)}, f32[1024,512]{1,0:T(8,128)}, bf16[1024,512]{1,0:T(8,128)(2,1)}, bf16[1024,512]{1,0:T(8,128)(2,1)}, f32[8,1024]{1,0:T(8,128)}, /*index=5*/f32[2,512]{1,0:T(2,128)}) custom-call(s32[4]{0:T(128)S(1)} %bitcast.56, s32[1]{0:T(128)} %bitcast.2.refs_0_.refs_1_, s32[3,128]{1,0:T(4,128)S(1)} %add_add_fusion.refs_2_.refs_1_, ...), custom_call_target="tpu_custom_call" | custom-call | flops 1610612736 | bytes 19656704 | tf_op jit(solution)/shard_map/gates_backward/pallas_call | solution.py:199
  192.6 4.1 %weight_grad_conv.1 = (bf16[2,384,512]{2,1,0:T(8,128)(2,1)S(1)}, bf16[2,384,512]{2,1,0:T(8,128)(2,1)S(1)}) custom-call(s32[1]{0:T(128)} %bitcast.2.refs_0_.refs_1_, bf16[1024,512]{1,0:T(8,128)(2,1)S(1)} %copy-done.26, bf16[1024,1024]{1,0:T(8,128)(2,1)} %get-tuple-element.182.refs_2_, bf16[1024,512]{1,0:T(8,128)(2,1)S(1)} %copy-done.27, ...), custom_call_target="tpu_custom_call" | custom-call | flops 1610612736 | bytes 6815744 | tf_op jit(solution)/shard_map/weight_grad_conv/pallas_call | solution.py:231
  196.8 15.4 %attention_backward.2.refs_2_.refs_1_ = bf16[1024,768]{1,0:T(8,128)(2,1)} custom-call(s32[4]{0:T(128)S(1)} %bitcast.57, bf16[1024,512]{1,0:T(8,128)(2,1)} %get-tuple-element.152.refs_2_.refs_1_, bf16[1024,512]{1,0:T(8,128)(2,1)} %get-tuple-element.153.refs_3_.refs_2_, bf16[512,1024]{1,0:T(8,128)(2,1)} %get-tuple-element.162.refs_3_, ...), custom_call_target="tpu_custom_call" | custom-call | flops 2684354560 | bytes 7929856 | tf_op jit(solution)/shard_map/attention_backward/pallas_call | solution.py:199
  217.0 15.6 %attention_backward.3.refs_3_.refs_2_ = bf16[1024,768]{1,0:T(8,128)(2,1)} custom-call(s32[4]{0:T(128)S(1)} %bitcast.58, bf16[1024,512]{1,0:T(8,128)(2,1)} %get-tuple-element.152.refs_2_.refs_1_, bf16[1024,512]{1,0:T(8,128)(2,1)} %get-tuple-element.153.refs_3_.refs_2_, bf16[512,1024]{1,0:T(8,128)(2,1)} %get-tuple-element.162.refs_3_, ...), custom_call_target="tpu_custom_call" | custom-call | flops 2684354560 | bytes 7929856 | tf_op jit(solution)/shard_map/attention_backward/pallas_call | solution.py:199
  232.6 1.9 add_convert_fusion.12
  236.0 5.2 %weight_grad_attn.1 = (bf16[2,512,512]{2,1,0:T(8,128)(2,1)S(1)}, bf16[2,512,512]{2,1,0:T(8,128)(2,1)S(1)}) custom-call(s32[1]{0:T(128)} %bitcast.2.refs_0_.refs_1_, bf16[1024,512]{1,0:T(8,128)(2,1)S(1)} %copy-done.25, bf16[1024,768]{1,0:T(8,128)(2,1)} %attention_backward.2.refs_2_.refs_1_, bf16[1024,768]{1,0:T(8,128)(2,1)} %attention_backward.3.refs_3_.refs_2_, ...), custom_call_target="tpu_custom_call" | custom-call | flops 2147483648 | bytes 8388608 | tf_op jit(solution)/shard_map/weight_grad_attn/pallas_call | solution.py:231
  241.4 4.3 %collective-permute-start.20 = (bf16[1,256,512]{2,1,0:T(8,128)(2,1)S(1)}, bf16[1,256,512]{2,1,0:T(8,128)(2,1)S(1)}, u32[]{:S(2)}, u32[]{:S(2)}) collective-permute-start(bf16[1,256,512]{2,1,0:T(8,128)(2,1)S(1)} %add_convert_fusion.11), channel_id=1, source_target_pairs={{0,8},{4,12},{8,0},{12,4},{16,24},{20,28},{24,16},{28,20},{1,9},{5... | collective-permute-start | bytes 786440 | tf_op jit(solution)/shard_map/ppermute | solution.py:1141
  245.7 8.8 %query_key_value_backward.1 = (f32[1024,512]{1,0:T(8,128)}, bf16[1024,512]{1,0:T(8,128)(2,1)}, f32[2,512]{1,0:T(2,128)}) custom-call(s32[1]{0:T(128)} %bitcast.2.refs_0_.refs_1_, bf16[1024,768]{1,0:T(8,128)(2,1)} %attention_backward.2.refs_2_.refs_1_, bf16[1024,768]{1,0:T(8,128)(2,1)} %attention_backward.3.refs_3_.refs_2_, ...), custom_call_target="tpu_custom_call" | custom-call | flops 1610612736 | bytes 12611584 | tf_op jit(solution)/shard_map/query_key_value_backward/pallas_call | solution.py:199
  258.1 5.6 %weight_grad_shrink.1 = (bf16[2,512,512]{2,1,0:T(8,128)(2,1)S(1)}, bf16[2,512,512]{2,1,0:T(8,128)(2,1)S(1)}) custom-call(s32[1]{0:T(128)} %bitcast.2.refs_0_.refs_1_, bf16[1024,2048]{1,0:T(8,128)(2,1)} %get-tuple-element.203.refs_1_, bf16[1024,512]{1,0:T(8,128)(2,1)S(1)} %copy-done.24), custom_call_target="tpu_custom_call" | custom-call | flops 2147483648 | bytes 7340032 | tf_op jit(solution)/shard_map/weight_grad_shrink/pallas_call | solution.py:231
  264.1 2.4 collective-permute-done.23
  267.8 2.1 collective-permute-start.26
  269.9 4.2 %collective-permute-done.27 = bf16[1,96,512]{2,1,0:T(8,128)(2,1)S(1)} collective-permute-done((bf16[1,96,512]{2,1,0:T(8,128)(2,1)S(1)}, bf16[1,96,512]{2,1,0:T(8,128)(2,1)S(1)}, u32[]{:S(2)}, u32[]{:S(2)}) %collective-permute-start.27) | collective-permute-done | bytes 98336 | tf_op jit(solution)/shard_map/ppermute | solution.py:1141
  274.1 14.1 %feed_forward_backward.1 = (f32[1024,512]{1,0:T(8,128)}, bf16[1024,2048]{1,0:T(8,128)(2,1)}, f32[44,512]{1,0:T(8,128)}) custom-call(s32[1]{0:T(128)} %bitcast.2.refs_0_.refs_1_, f32[1024,512]{1,0:T(8,128)} %get-tuple-element.201.refs_1_, bf16[1024,512]{1,0:T(8,128)(2,1)} %get-tuple-element.211.refs_2_, bf16[1024,512]{1,0:T(8,128)(2,1)} %refs_3_.6, ...), custom_call_target="tpu_custom_call" | custom-call | flops 4294967296 | bytes 19075072 | tf_op jit(solution)/shard_map/feed_forward_backward/pallas_call | solution.py:199
  291.1 6.5 %weight_grad_expand.1 = (bf16[2,528,512]{2,1,0:T(8,128)(2,1)S(1)}, bf16[2,528,512]{2,1,0:T(8,128)(2,1)}) custom-call(s32[1]{0:T(128)} %bitcast.2.refs_0_.refs_1_, bf16[1024,512]{1,0:T(8,128)(2,1)S(1)} %copy-done.29, bf16[1024,2048]{1,0:T(8,128)(2,1)} %get-tuple-element.224.refs_2_, bf16[4,16,512]{2,1,0:T(8,128)(2,1)S(1)} %bitcast.49), custom_call_target="tpu_custom_call" | custom-call | flops 2147483648 | bytes 7471104 | tf_op jit(solution)/shard_map/weight_grad_expand/pallas_call | solution.py:231
  297.6 3.0 collective-permute-done.28
  308.8 2.5 collective-permute-done.47
  311.6 2.1 collective-permute-start.35
  313.6 3.5 collective-permute-done.48
  324.6 2.1 adam_conv.1
  329.8 3.8 %collective-permute-start.44 = (bf16[1,128,512]{2,1,0:T(8,128)(2,1)S(1)}, bf16[1,128,512]{2,1,0:T(8,128)(2,1)S(1)}, u32[]{:S(2)}, u32[]{:S(2)}) collective-permute-start(bf16[1,128,512]{2,1,0:T(8,128)(2,1)S(1)} %add_convert_fusion.17), channel_id=1, source_target_pairs={{0,16},{4,20},{8,24},{12,28},{16,0},{20,4},{24,8},{28,12},{1,17},{... | collective-permute-start | bytes 393224 | tf_op jit(solution)/shard_map/ppermute | solution.py:1141
  334.8 6.1 %collective-permute-done.30 = bf16[1,264,512]{2,1,0:T(8,128)(2,1)S(1)} collective-permute-done((bf16[1,264,512]{2,1,0:T(8,128)(2,1)S(1)}, bf16[1,264,512]{2,1,0:T(8,128)(2,1)S(1)}, u32[]{:S(2)}, u32[]{:S(2)}) %collective-permute-start.30) | collective-permute-done | bytes 270368 | tf_op jit(solution)/shard_map/ppermute | solution.py:1141
  344.3 2.9 collective-permute-done.31
  348.3 3.3 collective-permute-start.32
  351.7 4.3 %collective-permute-done.32 = bf16[1,132,512]{2,1,0:T(8,128)(2,1)S(1)} collective-permute-done((bf16[1,132,512]{2,1,0:T(8,128)(2,1)S(1)}, bf16[1,132,512]{2,1,0:T(8,128)(2,1)S(1)}, u32[]{:S(2)}, u32[]{:S(2)}) %collective-permute-start.32) | collective-permute-done | bytes 135200 | tf_op jit(solution)/shard_map/ppermute | solution.py:1141
  359.4 1.8 collective-permute-done.33
  363.4 3.8 adam_late.1
  367.5 2.8 adam_attn.1
  370.5 2.5 adam_shrink.1
  374.9 4.2 %adam_expand.1 = (f32[2,128,2048]{2,1,0:T(8,128)}, f32[2,128,2048]{2,1,0:T(8,128)}, f32[2,128,2048]{2,1,0:T(8,128)}) custom-call(bf16[528,512]{1,0:T(8,128)(2,1)S(1)} %maximum_select_fusion.1.refs_0_, f32[2,128,2048]{2,1,0:T(8,128)S(1)} %copy-done.1, f32[2,128,2048]{2,1,0:T(8,128)S(1)} %copy-done.5, ...), custom_call_target="tpu_custom_call", output_to_operand_aliasing={{0}: (4, {}), {1}: (5, {}), {2}: (6, {})} | custom-call | flops 5242880 | bytes 6815744 | tf_op jit(solution)/shard_map/adam_expand/pallas_call | solution.py:1305
  (287 shorter events, 68.6 us)
Async XLA Ops:
  3.4 14.4 %collective-permute-start = (bf16[44,128]{1,0:T(8,128)(2,1)S(1)}, bf16[44,128]{1,0:T(8,128)(2,1)S(1)}, u32[]{:S(2)}, u32[]{:S(2)}) collective-permute-start(bf16[44,128]{1,0:T(8,128)(2,1)S(1)} %pad_maximum_fusion.2), channel_id=1, source_target_pairs={{0,2},{1,3},{2,0},{3,1},{4,6},{5,7},{6,4},{7,5},{8,10},{9,11},{10,... | collective-permute-start | bytes 33800 | tf_op jit(solution)/shard_map/ppermute | solution.py:1141
  6.4 11.6 %collective-permute-start.1 = (bf16[44,128]{1,0:T(8,128)(2,1)S(1)}, bf16[44,128]{1,0:T(8,128)(2,1)S(1)}, u32[]{:S(2)}, u32[]{:S(2)}) collective-permute-start(bf16[44,128]{1,0:T(8,128)(2,1)S(1)} %pad_maximum_fusion.2), channel_id=1, source_target_pairs={{0,1},{1,0},{2,3},{3,2},{4,5},{5,4},{6,7},{7,6},{8,9},{9,8},{10,11... | collective-permute-start | bytes 33800 | tf_op jit(solution)/shard_map/ppermute | solution.py:1141
  6.4 25.8 %collective-permute-start.3 = (bf16[1024,512]{1,0:T(8,128)(2,1)}, bf16[1024,512]{1,0:T(8,128)(2,1)S(1)}, u32[]{:S(2)}, u32[]{:S(2)}) collective-permute-start(bf16[1024,512]{1,0:T(8,128)(2,1)} %pack_early.1.refs_3_.refs_10_), channel_id=1, source_target_pairs={{0,2},{1,3},{2,0},{3,1},{4,6},{5,7},{6,4},{7,5},{8,10},{9,11},{10,... | collective-permute-start | bytes 3145736 | tf_op jit(solution)/shard_map/ppermute | solution.py:1141
  6.6 26.1 %collective-permute-start.4 = (bf16[1024,512]{1,0:T(8,128)(2,1)}, bf16[1024,512]{1,0:T(8,128)(2,1)S(1)}, u32[]{:S(2)}, u32[]{:S(2)}) collective-permute-start(bf16[1024,512]{1,0:T(8,128)(2,1)} %pack_early.1.refs_3_.refs_10_), channel_id=1, source_target_pairs={{0,1},{1,0},{2,3},{3,2},{4,5},{5,4},{6,7},{7,6},{8,9},{9,8},{10,11... | collective-permute-start | bytes 3145736 | tf_op jit(solution)/shard_map/ppermute | solution.py:1141
  32.2 2.7 collective-permute-start.5
  32.2 14.6 %collective-permute-start.6 = (bf16[512,512]{1,0:T(8,128)(2,1)S(1)}, bf16[512,512]{1,0:T(8,128)(2,1)S(1)}, u32[]{:S(2)}, u32[]{:S(2)}) collective-permute-start(bf16[512,512]{1,0:T(8,128)(2,1)S(1)} %copy-done.34), channel_id=1, source_target_pairs={{0,2},{1,3},{2,0},{3,1},{4,6},{5,7},{6,4},{7,5},{8,10},{9,11},{10,... | collective-permute-start | bytes 1572872 | tf_op jit(solution)/shard_map/ppermute | solution.py:1141
  47.1 2.5 collective-permute-start.7
  47.4 11.4 %collective-permute-start.9 = (bf16[384,512]{1,0:T(8,128)(2,1)S(1)}, bf16[384,512]{1,0:T(8,128)(2,1)}, u32[]{:S(2)}, u32[]{:S(2)}) collective-permute-start(bf16[384,512]{1,0:T(8,128)(2,1)S(1)} %copy-done.39), channel_id=1, source_target_pairs={{0,2},{1,3},{2,0},{3,1},{4,6},{5,7},{6,4},{7,5},{8,10},{9,11},{10,... | collective-permute-start | bytes 1179656 | tf_op jit(solution)/shard_map/ppermute | solution.py:1141
  58.9 42.7 %collective-permute-start.12 = (bf16[1024,512]{1,0:T(8,128)(2,1)}, bf16[1024,512]{1,0:T(8,128)(2,1)S(1)}, u32[]{:S(2)}, u32[]{:S(2)}) collective-permute-start(bf16[1024,512]{1,0:T(8,128)(2,1)} %pack_late.1.refs_11_), channel_id=1, source_target_pairs={{0,2},{1,3},{2,0},{3,1},{4,6},{5,7},{6,4},{7,5},{8,10},{9,11},{10,... | collective-permute-start | bytes 3145736 | tf_op jit(solution)/shard_map/ppermute | solution.py:1141
  59.6 2.5 collective-permute-start.10
  101.5 18.1 %collective-permute-start.13 = (bf16[1024,512]{1,0:T(8,128)(2,1)}, bf16[1024,512]{1,0:T(8,128)(2,1)S(1)}, u32[]{:S(2)}, u32[]{:S(2)}) collective-permute-start(bf16[1024,512]{1,0:T(8,128)(2,1)} %pack_late.1.refs_11_), channel_id=1, source_target_pairs={{0,1},{1,0},{2,3},{3,2},{4,5},{5,4},{6,7},{7,6},{8,9},{9,8},{10,11... | collective-permute-start | bytes 3145736 | tf_op jit(solution)/shard_map/ppermute | solution.py:1141
  101.6 18.0 %collective-permute-start.14 = (bf16[1024,512]{1,0:T(8,128)(2,1)S(1)}, bf16[1024,512]{1,0:T(8,128)(2,1)S(1)}, u32[]{:S(2)}, u32[]{:S(2)}) collective-permute-start(bf16[1024,512]{1,0:T(8,128)(2,1)S(1)} %collective-permute-done.12.refs_12_), channel_id=1, source_target_pairs={{0,1},{1,0},{2,3},{3,2},{4,5},{5,4},{6,7},{7,6},{8,9},{9,8},{10,11... | collective-permute-start | bytes 3145736 | tf_op jit(solution)/shard_map/ppermute | solution.py:1141
  145.0 13.3 %all-to-all-start.1 = ((f32[32,2,512]{2,1,0:T(2,128)}), f32[32,2,512]{2,1,0:T(2,128)S(1)}, u32[]{:S(2)}, u32[]{:S(2)}) async-start(f32[32,2,512]{2,1,0:T(2,128)} %broadcast_in_dim.17), calls=%async_computation.1 | async-start | bytes 262144 | tf_op jit(solution)/shard_map/all_to_all | solution.py:1245
  158.4 19.0 %collective-permute-start.15 = (bf16[2,1024,512]{2,1,0:T(8,128)(2,1)}, bf16[2,1024,512]{2,1,0:T(8,128)(2,1)}, u32[]{:S(2)}, u32[]{:S(2)}) collective-permute-start(bf16[2,1024,512]{2,1,0:T(8,128)(2,1)} %get-tuple-element.175), channel_id=1, source_target_pairs={{0,1},{1,0},{2,3},{3,2},{4,5},{5,4},{6,7},{7,6},{8,9},{9,8},{10,11... | collective-permute-start | bytes 6291464 | tf_op jit(solution)/shard_map/ppermute | solution.py:1141
  178.9 33.3 %collective-permute-start.16 = (bf16[1,1024,512]{2,1,0:T(8,128)(2,1)S(1)}, bf16[1,1024,512]{2,1,0:T(8,128)(2,1)}, u32[]{:S(2)}, u32[]{:S(2)}) collective-permute-start(bf16[1,1024,512]{2,1,0:T(8,128)(2,1)S(1)} %add_convert_fusion), channel_id=1, source_target_pairs={{0,2},{1,3},{2,0},{3,1},{4,6},{5,7},{6,4},{7,5},{8,10},{9,11},{10,... | collective-permute-start | bytes 3145736 | tf_op jit(solution)/shard_map/ppermute | solution.py:1141
  196.6 15.6 %collective-permute-start.18 = (bf16[2,384,512]{2,1,0:T(8,128)(2,1)S(1)}, bf16[2,384,512]{2,1,0:T(8,128)(2,1)}, u32[]{:S(2)}, u32[]{:S(2)}) collective-permute-start(bf16[2,384,512]{2,1,0:T(8,128)(2,1)S(1)} %get-tuple-element.185), channel_id=1, source_target_pairs={{0,1},{1,0},{2,3},{3,2},{4,5},{5,4},{6,7},{7,6},{8,9},{9,8},{10,11... | collective-permute-start | bytes 2359304 | tf_op jit(solution)/shard_map/ppermute | solution.py:1141
  213.8 20.7 %collective-permute-start.17 = (bf16[1,512,512]{2,1,0:T(8,128)(2,1)S(1)}, bf16[1,512,512]{2,1,0:T(8,128)(2,1)S(1)}, u32[]{:S(2)}, u32[]{:S(2)}) collective-permute-start(bf16[1,512,512]{2,1,0:T(8,128)(2,1)S(1)} %add_convert_fusion.4), channel_id=1, source_target_pairs={{0,4},{4,0},{8,12},{12,8},{16,20},{20,16},{24,28},{28,24},{1,5},{5... | collective-permute-start | bytes 1572872 | tf_op jit(solution)/shard_map/ppermute | solution.py:1141
  215.7 16.9 %collective-permute-start.19 = (bf16[1,384,512]{2,1,0:T(8,128)(2,1)S(1)}, bf16[1,384,512]{2,1,0:T(8,128)(2,1)S(1)}, u32[]{:S(2)}, u32[]{:S(2)}) collective-permute-start(bf16[1,384,512]{2,1,0:T(8,128)(2,1)S(1)} %add_convert_fusion.5), channel_id=1, source_target_pairs={{0,2},{1,3},{2,0},{3,1},{4,6},{5,7},{6,4},{7,5},{8,10},{9,11},{10,... | collective-permute-start | bytes 1179656 | tf_op jit(solution)/shard_map/ppermute | solution.py:1141
  241.2 15.8 %collective-permute-start.22 = (bf16[2,512,512]{2,1,0:T(8,128)(2,1)S(1)}, bf16[2,512,512]{2,1,0:T(8,128)(2,1)}, u32[]{:S(2)}, u32[]{:S(2)}) collective-permute-start(bf16[2,512,512]{2,1,0:T(8,128)(2,1)S(1)} %get-tuple-element.198), channel_id=1, source_target_pairs={{0,1},{1,0},{2,3},{3,2},{4,5},{5,4},{6,7},{7,6},{8,9},{9,8},{10,11... | collective-permute-start | bytes 3145736 | tf_op jit(solution)/shard_map/ppermute | solution.py:1141
  241.3 13.2 %collective-permute-start.21 = (bf16[1,192,512]{2,1,0:T(8,128)(2,1)}, bf16[1,192,512]{2,1,0:T(8,128)(2,1)S(1)}, u32[]{:S(2)}, u32[]{:S(2)}) collective-permute-start(bf16[1,192,512]{2,1,0:T(8,128)(2,1)} %add_convert_fusion.12), channel_id=1, source_target_pairs={{0,4},{4,0},{8,12},{12,8},{16,20},{20,16},{24,28},{28,24},{1,5},{5... | collective-permute-start | bytes 589832 | tf_op jit(solution)/shard_map/ppermute | solution.py:1141
  241.4 14.3 %collective-permute-start.20 = (bf16[1,256,512]{2,1,0:T(8,128)(2,1)S(1)}, bf16[1,256,512]{2,1,0:T(8,128)(2,1)S(1)}, u32[]{:S(2)}, u32[]{:S(2)}) collective-permute-start(bf16[1,256,512]{2,1,0:T(8,128)(2,1)S(1)} %add_convert_fusion.11), channel_id=1, source_target_pairs={{0,8},{4,12},{8,0},{12,4},{16,24},{20,28},{24,16},{28,20},{1,9},{5... | collective-permute-start | bytes 786440 | tf_op jit(solution)/shard_map/ppermute | solution.py:1141
  263.8 2.7 collective-permute-start.23
  263.9 24.3 %collective-permute-start.24 = (bf16[1,512,512]{2,1,0:T(8,128)(2,1)S(1)}, bf16[1,512,512]{2,1,0:T(8,128)(2,1)}, u32[]{:S(2)}, u32[]{:S(2)}) collective-permute-start(bf16[1,512,512]{2,1,0:T(8,128)(2,1)S(1)} %add_convert_fusion.3), channel_id=1, source_target_pairs={{0,2},{1,3},{2,0},{3,1},{4,6},{5,7},{6,4},{7,5},{8,10},{9,11},{10,... | collective-permute-start | bytes 1572872 | tf_op jit(solution)/shard_map/ppermute | solution.py:1141
  267.6 22.3 %collective-permute-start.25 = (bf16[1,512,512]{2,1,0:T(8,128)(2,1)}, bf16[1,512,512]{2,1,0:T(8,128)(2,1)}, u32[]{:S(2)}, u32[]{:S(2)}) collective-permute-start(bf16[1,512,512]{2,1,0:T(8,128)(2,1)} %add_convert_fusion.2), channel_id=1, source_target_pairs={{0,2},{1,3},{2,0},{3,1},{4,6},{5,7},{6,4},{7,5},{8,10},{9,11},{10,... | collective-permute-start | bytes 1572872 | tf_op jit(solution)/shard_map/ppermute | solution.py:1141
  267.8 6.3 %collective-permute-start.27 = (bf16[1,96,512]{2,1,0:T(8,128)(2,1)S(1)}, bf16[1,96,512]{2,1,0:T(8,128)(2,1)S(1)}, u32[]{:S(2)}, u32[]{:S(2)}) collective-permute-start(bf16[1,96,512]{2,1,0:T(8,128)(2,1)S(1)} %add_convert_fusion.24), channel_id=1, source_target_pairs={{0,8},{4,12},{8,0},{12,4},{16,24},{20,28},{24,16},{28,20},{1,9},{5... | collective-permute-start | bytes 294920 | tf_op jit(solution)/shard_map/ppermute | solution.py:1141
  267.8 20.4 %collective-permute-start.26 = (bf16[1,256,512]{2,1,0:T(8,128)(2,1)S(1)}, bf16[1,256,512]{2,1,0:T(8,128)(2,1)S(1)}, u32[]{:S(2)}, u32[]{:S(2)}) collective-permute-start(bf16[1,256,512]{2,1,0:T(8,128)(2,1)S(1)} %add_convert_fusion.10), channel_id=1, source_target_pairs={{0,16},{4,20},{8,24},{12,28},{16,0},{20,4},{24,8},{28,12},{1,17},{... | collective-permute-start | bytes 786440 | tf_op jit(solution)/shard_map/ppermute | solution.py:1141
  297.6 3.0 collective-permute-start.28
  301.9 24.9 %collective-permute-start.29 = (bf16[1,528,512]{2,1,0:T(8,128)(2,1)S(1)}, bf16[1,528,512]{2,1,0:T(8,128)(2,1)S(1)}, u32[]{:S(2)}, u32[]{:S(2)}) collective-permute-start(bf16[1,528,512]{2,1,0:T(8,128)(2,1)S(1)} %add_convert_fusion.1), channel_id=1, source_target_pairs={{0,2},{1,3},{2,0},{3,1},{4,6},{5,7},{6,4},{7,5},{8,10},{9,11},{10,... | collective-permute-start | bytes 1622024 | tf_op jit(solution)/shard_map/ppermute | solution.py:1141
  304.4 6.9 %collective-permute-start.47 = (bf16[1,96,512]{2,1,0:T(8,128)(2,1)S(1)}, bf16[1,96,512]{2,1,0:T(8,128)(2,1)S(1)}, u32[]{:S(2)}, u32[]{:S(2)}) collective-permute-start(bf16[1,96,512]{2,1,0:T(8,128)(2,1)S(1)} %add_convert_fusion.23), channel_id=1, source_target_pairs={{0,16},{4,20},{8,24},{12,28},{16,0},{20,4},{24,8},{28,12},{1,17},{... | collective-permute-start | bytes 294920 | tf_op jit(solution)/shard_map/ppermute | solution.py:1141
  305.6 13.0 %collective-permute-start.42 = (bf16[1,256,512]{2,1,0:T(8,128)(2,1)S(1)}, bf16[1,256,512]{2,1,0:T(8,128)(2,1)S(1)}, u32[]{:S(2)}, u32[]{:S(2)}) collective-permute-start(bf16[1,256,512]{2,1,0:T(8,128)(2,1)S(1)} %add_convert_fusion.7), channel_id=1, source_target_pairs={{0,4},{4,0},{8,12},{12,8},{16,20},{20,16},{24,28},{28,24},{1,5},{5... | collective-permute-start | bytes 786440 | tf_op jit(solution)/shard_map/ppermute | solution.py:1141
  308.3 12.2 %collective-permute-start.37 = (bf16[1,256,512]{2,1,0:T(8,128)(2,1)S(1)}, bf16[1,256,512]{2,1,0:T(8,128)(2,1)S(1)}, u32[]{:S(2)}, u32[]{:S(2)}) collective-permute-start(bf16[1,256,512]{2,1,0:T(8,128)(2,1)S(1)} %add_convert_fusion.8), channel_id=1, source_target_pairs={{0,4},{4,0},{8,12},{12,8},{16,20},{20,16},{24,28},{28,24},{1,5},{5... | collective-permute-start | bytes 786440 | tf_op jit(solution)/shard_map/ppermute | solution.py:1141
  311.4 5.7 %collective-permute-start.48 = (bf16[96,512]{1,0:T(8,128)(2,1)S(1)}, bf16[96,512]{1,0:T(8,128)(2,1)S(1)}, u32[]{:S(2)}, u32[]{:S(2)}) collective-permute-start(bf16[96,512]{1,0:T(8,128)(2,1)S(1)} %fusion.5), channel_id=1, source_target_pairs={{0,8},{4,12},{8,0},{12,4},{16,24},{20,28},{24,16},{28,20},{1,9},{5... | collective-permute-start | bytes 294920 | tf_op jit(solution)/shard_map/ppermute | solution.py:1141
  311.6 11.4 %collective-permute-start.35 = (bf16[256,512]{1,0:T(8,128)(2,1)S(1)}, bf16[256,512]{1,0:T(8,128)(2,1)S(1)}, u32[]{:S(2)}, u32[]{:S(2)}) collective-permute-start(bf16[256,512]{1,0:T(8,128)(2,1)S(1)} %fusion), channel_id=1, source_target_pairs={{0,8},{4,12},{8,0},{12,4},{16,24},{20,28},{24,16},{28,20},{1,9},{5... | collective-permute-start | bytes 786440 | tf_op jit(solution)/shard_map/ppermute | solution.py:1141
  317.2 7.2 %collective-permute-start.49 = (bf16[192,512]{1,0:T(8,128)(2,1)S(1)}, bf16[192,512]{1,0:T(8,128)(2,1)S(1)}, u32[]{:S(2)}, u32[]{:S(2)}) collective-permute-start(bf16[192,512]{1,0:T(8,128)(2,1)S(1)} %maximum_select_fusion.9), channel_id=1, source_target_pairs={{0,4},{4,0},{8,12},{12,8},{16,20},{20,16},{24,28},{28,24},{1,5},{5... | collective-permute-start | bytes 589832 | tf_op jit(solution)/shard_map/ppermute | solution.py:1141
  319.8 9.0 %collective-permute-start.43 = (bf16[1,128,512]{2,1,0:T(8,128)(2,1)S(1)}, bf16[1,128,512]{2,1,0:T(8,128)(2,1)S(1)}, u32[]{:S(2)}, u32[]{:S(2)}) collective-permute-start(bf16[1,128,512]{2,1,0:T(8,128)(2,1)S(1)} %add_convert_fusion.18), channel_id=1, source_target_pairs={{0,8},{4,12},{8,0},{12,4},{16,24},{20,28},{24,16},{28,20},{1,9},{5... | collective-permute-start | bytes 393224 | tf_op jit(solution)/shard_map/ppermute | solution.py:1141
  321.4 12.2 %collective-permute-start.38 = (bf16[1,128,512]{2,1,0:T(8,128)(2,1)S(1)}, bf16[1,128,512]{2,1,0:T(8,128)(2,1)S(1)}, u32[]{:S(2)}, u32[]{:S(2)}) collective-permute-start(bf16[1,128,512]{2,1,0:T(8,128)(2,1)S(1)} %add_convert_fusion.21), channel_id=1, source_target_pairs={{0,8},{4,12},{8,0},{12,4},{16,24},{20,28},{24,16},{28,20},{1,9},{5... | collective-permute-start | bytes 393224 | tf_op jit(solution)/shard_map/ppermute | solution.py:1141
  323.1 39.7 %collective-permute-start.36 = (bf16[512,512]{1,0:T(8,128)(2,1)S(1)}, bf16[512,512]{1,0:T(8,128)(2,1)S(1)}, u32[]{:S(2)}, u32[]{:S(2)}) collective-permute-start(bf16[512,512]{1,0:T(8,128)(2,1)S(1)} %maximum_select_fusion.2), channel_id=1, source_target_pairs={{0,4},{4,0},{8,12},{12,8},{16,20},{20,16},{24,28},{28,24},{1,5},{5... | collective-permute-start | bytes 1572872 | tf_op jit(solution)/shard_map/ppermute | solution.py:1141
  327.9 13.0 %collective-permute-start.30 = (bf16[1,264,512]{2,1,0:T(8,128)(2,1)S(1)}, bf16[1,264,512]{2,1,0:T(8,128)(2,1)S(1)}, u32[]{:S(2)}, u32[]{:S(2)}) collective-permute-start(bf16[1,264,512]{2,1,0:T(8,128)(2,1)S(1)} %add_convert_fusion.6), channel_id=1, source_target_pairs={{0,4},{4,0},{8,12},{12,8},{16,20},{20,16},{24,28},{28,24},{1,5},{5... | collective-permute-start | bytes 811016 | tf_op jit(solution)/shard_map/ppermute | solution.py:1141
  329.8 12.8 %collective-permute-start.44 = (bf16[1,128,512]{2,1,0:T(8,128)(2,1)S(1)}, bf16[1,128,512]{2,1,0:T(8,128)(2,1)S(1)}, u32[]{:S(2)}, u32[]{:S(2)}) collective-permute-start(bf16[1,128,512]{2,1,0:T(8,128)(2,1)S(1)} %add_convert_fusion.17), channel_id=1, source_target_pairs={{0,16},{4,20},{8,24},{12,28},{16,0},{20,4},{24,8},{28,12},{1,17},{... | collective-permute-start | bytes 393224 | tf_op jit(solution)/shard_map/ppermute | solution.py:1141
  334.7 16.9 %collective-permute-start.39 = (bf16[1,128,512]{2,1,0:T(8,128)(2,1)S(1)}, bf16[1,128,512]{2,1,0:T(8,128)(2,1)S(1)}, u32[]{:S(2)}, u32[]{:S(2)}) collective-permute-start(bf16[1,128,512]{2,1,0:T(8,128)(2,1)S(1)} %add_convert_fusion.20), channel_id=1, source_target_pairs={{0,16},{4,20},{8,24},{12,28},{16,0},{20,4},{24,8},{28,12},{1,17},{... | collective-permute-start | bytes 393224 | tf_op jit(solution)/shard_map/ppermute | solution.py:1141
  342.1 5.1 %collective-permute-start.31 = (bf16[1,132,512]{2,1,0:T(8,128)(2,1)S(1)}, bf16[1,132,512]{2,1,0:T(8,128)(2,1)S(1)}, u32[]{:S(2)}, u32[]{:S(2)}) collective-permute-start(bf16[1,132,512]{2,1,0:T(8,128)(2,1)S(1)} %add_convert_fusion.15), channel_id=1, source_target_pairs={{0,8},{4,12},{8,0},{12,4},{16,24},{20,28},{24,16},{28,20},{1,9},{5... | collective-permute-start | bytes 405512 | tf_op jit(solution)/shard_map/ppermute | solution.py:1141
  342.7 13.5 %collective-permute-start.45 = (bf16[128,512]{1,0:T(8,128)(2,1)S(1)}, bf16[128,512]{1,0:T(8,128)(2,1)S(1)}, u32[]{:S(2)}, u32[]{:S(2)}) collective-permute-start(bf16[128,512]{1,0:T(8,128)(2,1)S(1)} %fusion.4), channel_id=1, source_target_pairs={{0,8},{4,12},{8,0},{12,4},{16,24},{20,28},{24,16},{28,20},{1,9},{5... | collective-permute-start | bytes 393224 | tf_op jit(solution)/shard_map/ppermute | solution.py:1141
  348.3 7.8 %collective-permute-start.32 = (bf16[1,132,512]{2,1,0:T(8,128)(2,1)S(1)}, bf16[1,132,512]{2,1,0:T(8,128)(2,1)S(1)}, u32[]{:S(2)}, u32[]{:S(2)}) collective-permute-start(bf16[1,132,512]{2,1,0:T(8,128)(2,1)S(1)} %add_convert_fusion.14), channel_id=1, source_target_pairs={{0,16},{4,20},{8,24},{12,28},{16,0},{20,4},{24,8},{28,12},{1,17},{... | collective-permute-start | bytes 405512 | tf_op jit(solution)/shard_map/ppermute | solution.py:1141
  351.6 6.3 %collective-permute-start.40 = (bf16[128,512]{1,0:T(8,128)(2,1)S(1)}, bf16[128,512]{1,0:T(8,128)(2,1)S(1)}, u32[]{:S(2)}, u32[]{:S(2)}) collective-permute-start(bf16[128,512]{1,0:T(8,128)(2,1)S(1)} %fusion.3), channel_id=1, source_target_pairs={{0,8},{4,12},{8,0},{12,4},{16,24},{20,28},{24,16},{28,20},{1,9},{5... | collective-permute-start | bytes 393224 | tf_op jit(solution)/shard_map/ppermute | solution.py:1141
  356.1 5.1 %collective-permute-start.33 = (bf16[132,512]{1,0:T(8,128)(2,1)S(1)}, bf16[132,512]{1,0:T(8,128)(2,1)S(1)}, u32[]{:S(2)}, u32[]{:S(2)}) collective-permute-start(bf16[132,512]{1,0:T(8,128)(2,1)S(1)} %fusion.2), channel_id=1, source_target_pairs={{0,8},{4,12},{8,0},{12,4},{16,24},{20,28},{24,16},{28,20},{1,9},{5... | collective-permute-start | bytes 405512 | tf_op jit(solution)/shard_map/ppermute | solution.py:1141
  356.2 10.9 %collective-permute-start.46 = (bf16[256,512]{1,0:T(8,128)(2,1)S(1)}, bf16[256,512]{1,0:T(8,128)(2,1)S(1)}, u32[]{:S(2)}, u32[]{:S(2)}) collective-permute-start(bf16[256,512]{1,0:T(8,128)(2,1)S(1)} %maximum_select_fusion.8), channel_id=1, source_target_pairs={{0,4},{4,0},{8,12},{12,8},{16,20},{20,16},{24,28},{28,24},{1,5},{5... | collective-permute-start | bytes 786440 | tf_op jit(solution)/shard_map/ppermute | solution.py:1141
  358.0 12.3 %collective-permute-start.41 = (bf16[256,512]{1,0:T(8,128)(2,1)S(1)}, bf16[256,512]{1,0:T(8,128)(2,1)S(1)}, u32[]{:S(2)}, u32[]{:S(2)}) collective-permute-start(bf16[256,512]{1,0:T(8,128)(2,1)S(1)} %maximum_select_fusion.7), channel_id=1, source_target_pairs={{0,4},{4,0},{8,12},{12,8},{16,20},{20,16},{24,28},{28,24},{1,5},{5... | collective-permute-start | bytes 786440 | tf_op jit(solution)/shard_map/ppermute | solution.py:1141
  361.3 11.7 %collective-permute-start.34 = (bf16[264,512]{1,0:T(8,128)(2,1)S(1)}, bf16[264,512]{1,0:T(8,128)(2,1)S(1)}, u32[]{:S(2)}, u32[]{:S(2)}) collective-permute-start(bf16[264,512]{1,0:T(8,128)(2,1)S(1)} %maximum_select_fusion.6), channel_id=1, source_target_pairs={{0,4},{4,0},{8,12},{12,8},{16,20},{20,16},{24,28},{28,24},{1,5},{5... | collective-permute-start | bytes 811016 | tf_op jit(solution)/shard_map/ppermute | solution.py:1141
  (67 other events, 666.7 us)
